TPU v7x, 32 devices: a whole 2x2x4 slice. The times are simulated.
32 devices in a mesh: seq: 4 (over y, x), dp: 8 (over z, core).
Axes of the slice: x: 2, y: 2, z: 4, core: 2. Of those that a mesh axis runs over, the one named last changes fastest.
Arguments:
- tokens: bfloat16 [16, 1024, 768], P('dp', 'seq'), may hold values from -6 to 6
- lengths: int32 [16], P('dp'), may hold values from 512 to 1024, as said below
- random_features: float32 [64, 256], replicated, may hold values from -6 to 6
- w_query: bfloat16 [768, 768], P(None, 'dp'), may hold values from -0.21875 to 0.21875
- w_key: bfloat16 [768, 768], P(None, 'dp'), may hold values from -0.21875 to 0.21875
- w_value: bfloat16 [768, 768], P(None, 'dp'), may hold values from -0.21875 to 0.21875
- w_output: bfloat16 [768, 768], P(None, 'dp'), may hold values from -3.5 to 3.5
- w_in: bfloat16 [768, 3072], P(None, 'dp'), may hold values from -0.21875 to 0.21875
- w_out: bfloat16 [3072, 768], P(None, 'dp'), may hold values from -0.109375 to 0.109375
- ln1_gain: bfloat16 [768], P('dp'), may hold values from 0.099609375 to 1.8984375
- ln1_bias: bfloat16 [768], P('dp'), may hold values from -3 to 3
- ln2_gain: bfloat16 [768], P('dp'), may hold values from 0.099609375 to 1.8984375
- ln2_bias: bfloat16 [768], P('dp'), may hold values from -3 to 3
- cotangent: bfloat16 [16, 1024, 768], P('dp', 'seq'), may hold values from -6 to 6
Outputs:
- layer_out: bfloat16 [16, 1024, 768], P('dp', 'seq')
- tokens_grad: float32 [16, 1024, 768], P('dp', 'seq')
- w_query_grad: float32 [768, 768], P(None, 'dp')
- w_key_grad: float32 [768, 768], P(None, 'dp')
- w_value_grad: float32 [768, 768], P(None, 'dp')
- w_output_grad: float32 [768, 768], P(None, 'dp')
- w_in_grad: float32 [768, 3072], P(None, 'dp')
- w_out_grad: float32 [3072, 768], P(None, 'dp')
- ln1_gain_grad: float32 [768], P('dp')
- ln1_bias_grad: float32 [768], P('dp')
- ln2_gain_grad: float32 [768], P('dp')
- ln2_bias_grad: float32 [768], P('dp')
Inputs may be any that keep to these rules, and one draw needn't show every extreme that they name: `lengths`: every sequence holds between 512 and 1024 valid tokens at its start; both ends occur.
All inputs are finite; a program needn't handle non-finite values.
Results may differ from a plain program's by a relative error of at most 0.015.
The roundings to bfloat16 on the way count: a program that leaves them out, or rounds other values in their place, can miss the bound.
Values may be sent and summed in bfloat16 or wider, within the bound.
A program may use at most 192 MiB of HBM per device.

v0:
```python
from functools import partial

import jax
import jax.numpy as jnp
from jax import lax
from jax.sharding import PartitionSpec as P

HEAD = 64


highest = lax.Precision.HIGHEST
norm_epsilon = 1e-12


def layer_norm(row_block, gain_vec, bias_vec):
    mean_val = jnp.mean(row_block, -1, keepdims=True)
    centered = row_block - mean_val
    inv_std = lax.rsqrt(jnp.mean(centered * centered, -1, keepdims=True) + norm_epsilon)
    normed = centered * inv_std
    return (normed * gain_vec + bias_vec, normed, inv_std)


def norm_back(grad_out, normed, inv_std, gain_vec):
    grad_normed = grad_out * gain_vec
    inner_term = (
        grad_normed
        - jnp.mean(grad_normed, -1, keepdims=True)
        - normed * jnp.mean(grad_normed * normed, -1, keepdims=True)
    )
    return (inv_std * inner_term, jnp.sum(grad_out * normed, 0), jnp.sum(grad_out, 0))


def row_product(left, right):
    return lax.dot_general(
        left, right, (((0,), (0,)), ((), ())), preferred_element_type=jnp.float32
    )


def feature_map(projected, random_features):
    scaled = projected.astype(jnp.float32) * HEAD ** (-0.25)
    projection = jnp.einsum("snhe,em->snhm", scaled, random_features, precision=highest)
    return (jnp.exp(projection - 0.5 * jnp.sum(scaled * scaled, -1, keepdims=True)), scaled)


def feature_back(grad_features, features, scaled, random_features):
    grad_proj = grad_features * features
    grad_scaled = jnp.einsum("snhm,em->snhe", grad_proj, random_features, precision=highest)
    grad_scaled = grad_scaled - scaled * jnp.sum(grad_proj, -1, keepdims=True)
    return grad_scaled * HEAD ** (-0.25)


def keep_local(key_state, key_total):
    return (key_state, key_total)


def mixer_forward(queries, key_proj, value_proj, key_mask, random_features, reducer):
    q_feat, q_scaled = feature_map(queries, random_features)
    k_feat, k_scaled = feature_map(key_proj, random_features)
    k_feat = k_feat * key_mask[:, :, None, None]
    key_state = jnp.einsum(
        "snhm,snhe->shme", k_feat, value_proj.astype(jnp.float32), precision=highest
    )
    key_total = jnp.sum(k_feat, 1)
    key_state, key_total = reducer(key_state, key_total)
    numerator = jnp.einsum("snhm,shme->snhe", q_feat, key_state, precision=highest)
    denominator = jnp.einsum("snhm,shm->snh", q_feat, key_total, precision=highest)
    context = numerator / denominator[..., None]
    return (
        context,
        (q_feat, q_scaled, k_feat, k_scaled, key_state, key_total, denominator, context),
    )


def mixer_backward(grad_context, value_proj, kept_mixer, random_features, reducer):
    q_feat, q_scaled, k_feat, k_scaled, key_state, key_total, denominator, context = kept_mixer
    grad_ctx = grad_context.astype(jnp.float32)
    grad_num = grad_ctx / denominator[..., None]
    grad_den = -jnp.sum(grad_ctx * context, -1) / denominator
    grad_qfeat = (
        jnp.einsum("snhe,shme->snhm", grad_num, key_state, precision=highest)
        + grad_den[..., None] * key_total[:, None]
    )
    grad_state = jnp.einsum("snhm,snhe->shme", q_feat, grad_num, precision=highest)
    grad_total = jnp.einsum("snhm,snh->shm", q_feat, grad_den, precision=highest)
    grad_state, grad_total = reducer(grad_state, grad_total)
    values_f32 = value_proj.astype(jnp.float32)
    grad_kfeat = (
        jnp.einsum("snhe,shme->snhm", values_f32, grad_state, precision=highest)
        + grad_total[:, None]
    )
    grad_values = jnp.einsum("snhm,shme->snhe", k_feat, grad_state, precision=highest)
    grad_queries = feature_back(grad_qfeat, q_feat, q_scaled, random_features)
    grad_keys = feature_back(grad_kfeat, k_feat, k_scaled, random_features)
    return (grad_queries, grad_keys, grad_values)


def shards(
    tokens,
    lengths,
    random_features,
    w_query,
    w_key,
    w_value,
    w_output,
    w_in,
    w_out,
    ln1_gain,
    ln1_bias,
    ln2_gain,
    ln2_bias,
    cotangent,
):
    seq_count, local_len, model_width = tokens.shape
    row_count = seq_count * local_len
    seq_parts = lax.axis_size("seq")
    heads_all = model_width // HEAD
    wq_full, wk_full, wv_full, wo_full, win_full, wout_full, gain1, bias1, gain2, bias2 = (
        lax.all_gather(w_query, "dp", axis=1, tiled=True),
        lax.all_gather(w_key, "dp", axis=1, tiled=True),
        lax.all_gather(w_value, "dp", axis=1, tiled=True),
        lax.all_gather(w_output, "dp", axis=1, tiled=True),
        lax.all_gather(w_in, "dp", axis=1, tiled=True),
        lax.all_gather(w_out, "dp", axis=1, tiled=True),
        lax.all_gather(ln1_gain, "dp", axis=0, tiled=True),
        lax.all_gather(ln1_bias, "dp", axis=0, tiled=True),
        lax.all_gather(ln2_gain, "dp", axis=0, tiled=True),
        lax.all_gather(ln2_bias, "dp", axis=0, tiled=True),
    )
    tok_rows = tokens.reshape(row_count, model_width)
    query_proj = jnp.dot(tok_rows, wq_full, preferred_element_type=jnp.float32).astype(jnp.bfloat16)
    key_proj = jnp.dot(tok_rows, wk_full, preferred_element_type=jnp.float32).astype(jnp.bfloat16)
    value_proj = jnp.dot(tok_rows, wv_full, preferred_element_type=jnp.float32).astype(jnp.bfloat16)
    local_pos = lax.axis_index("seq") * local_len + jnp.arange(local_len, dtype=jnp.int32)
    row_valid = (local_pos[None, :] < lengths[:, None]).astype(jnp.float32)
    full_len = local_len * seq_parts
    head_group = heads_all // seq_parts
    q_heads, k_heads, v_heads = (
        lax.all_to_all(
            query_proj.reshape(seq_count, local_len, model_width),
            "seq",
            split_axis=2,
            concat_axis=1,
            tiled=True,
        ),
        lax.all_to_all(
            key_proj.reshape(seq_count, local_len, model_width),
            "seq",
            split_axis=2,
            concat_axis=1,
            tiled=True,
        ),
        lax.all_to_all(
            value_proj.reshape(seq_count, local_len, model_width),
            "seq",
            split_axis=2,
            concat_axis=1,
            tiled=True,
        ),
    )
    q_heads = q_heads.reshape(seq_count, full_len, head_group, HEAD)
    k_heads = k_heads.reshape(seq_count, full_len, head_group, HEAD)
    v_heads = v_heads.reshape(seq_count, full_len, head_group, HEAD)
    full_pos = jnp.arange(full_len, dtype=jnp.int32)
    key_mask = (full_pos[None, :] < lengths[:, None]).astype(jnp.float32)
    context, kept_mixer = mixer_forward(
        q_heads, k_heads, v_heads, key_mask, random_features, keep_local
    )
    ctx_low = context.astype(jnp.bfloat16).reshape(seq_count, full_len, head_group * HEAD)
    ctx_tokens = lax.all_to_all(ctx_low, "seq", split_axis=1, concat_axis=2, tiled=True)
    ctx_rows = ctx_tokens.reshape(row_count, model_width)
    attn_out = jnp.dot(ctx_rows, wo_full, preferred_element_type=jnp.float32)
    resid1 = tok_rows.astype(jnp.float32) + attn_out
    hidden, normed1, inv1 = layer_norm(resid1, gain1.astype(jnp.float32), bias1.astype(jnp.float32))
    hidden_low = hidden.astype(jnp.bfloat16)
    pre_act = jnp.dot(hidden_low, win_full, preferred_element_type=jnp.float32)
    activated, gelu_pull = jax.vjp(partial(jax.nn.gelu, approximate=False), pre_act)
    act_low = activated.astype(jnp.bfloat16)
    ffn_out = jnp.dot(act_low, wout_full, preferred_element_type=jnp.float32)
    normed_out, normed2, inv2 = layer_norm(
        hidden + ffn_out, gain2.astype(jnp.float32), bias2.astype(jnp.float32)
    )
    valid_rows = row_valid.reshape(row_count, 1)
    layer_out = (
        (normed_out * valid_rows).astype(jnp.bfloat16).reshape(seq_count, local_len, model_width)
    )
    wq_back, wk_back, wv_back, wo_back, win_back, wout_back, gain1_back, gain2_back = (
        lax.all_gather(w_query, "dp", axis=1, tiled=True),
        lax.all_gather(w_key, "dp", axis=1, tiled=True),
        lax.all_gather(w_value, "dp", axis=1, tiled=True),
        lax.all_gather(w_output, "dp", axis=1, tiled=True),
        lax.all_gather(w_in, "dp", axis=1, tiled=True),
        lax.all_gather(w_out, "dp", axis=1, tiled=True),
        lax.all_gather(ln1_gain, "dp", axis=0, tiled=True),
        lax.all_gather(ln2_gain, "dp", axis=0, tiled=True),
    )
    grad_y = cotangent.reshape(row_count, model_width).astype(jnp.float32) * valid_rows
    grad_r2, grad_gain2, grad_bias2 = norm_back(
        grad_y, normed2, inv2, gain2_back.astype(jnp.float32)
    )
    grad_ffn = grad_r2.astype(jnp.bfloat16)
    grad_wout = row_product(act_low, grad_ffn)
    grad_act = lax.dot_general(
        grad_ffn, wout_back, (((1,), (1,)), ((), ())), preferred_element_type=jnp.float32
    )
    grad_pre = gelu_pull(grad_act)[0].astype(jnp.bfloat16)
    grad_win = row_product(hidden_low, grad_pre)
    grad_hidden = grad_r2 + lax.dot_general(
        grad_pre, win_back, (((1,), (1,)), ((), ())), preferred_element_type=jnp.float32
    )
    grad_r1, grad_gain1, grad_bias1 = norm_back(
        grad_hidden, normed1, inv1, gain1_back.astype(jnp.float32)
    )
    grad_attn = grad_r1.astype(jnp.bfloat16)
    grad_wo = row_product(ctx_rows, grad_attn)
    grad_ctx = lax.dot_general(
        grad_attn, wo_back, (((1,), (1,)), ((), ())), preferred_element_type=jnp.float32
    ).astype(jnp.bfloat16)
    grad_heads = lax.all_to_all(
        grad_ctx.reshape(seq_count, local_len, model_width),
        "seq",
        split_axis=2,
        concat_axis=1,
        tiled=True,
    )
    grad_heads = grad_heads.reshape(seq_count, full_len, head_group, HEAD)
    grad_q, grad_k, grad_v = mixer_backward(
        grad_heads, v_heads, kept_mixer, random_features, keep_local
    )
    grad_q_tok, grad_k_tok, grad_v_tok = (
        lax.all_to_all(
            grad_q.astype(jnp.bfloat16).reshape(seq_count, full_len, head_group * HEAD),
            "seq",
            split_axis=1,
            concat_axis=2,
            tiled=True,
        ),
        lax.all_to_all(
            grad_k.astype(jnp.bfloat16).reshape(seq_count, full_len, head_group * HEAD),
            "seq",
            split_axis=1,
            concat_axis=2,
            tiled=True,
        ),
        lax.all_to_all(
            grad_v.astype(jnp.bfloat16).reshape(seq_count, full_len, head_group * HEAD),
            "seq",
            split_axis=1,
            concat_axis=2,
            tiled=True,
        ),
    )
    grad_q_rows = grad_q_tok.reshape(row_count, model_width)
    grad_k_rows = grad_k_tok.reshape(row_count, model_width)
    grad_v_rows = grad_v_tok.reshape(row_count, model_width)
    grad_wq = row_product(tok_rows, grad_q_rows)
    grad_wk = row_product(tok_rows, grad_k_rows)
    grad_wv = row_product(tok_rows, grad_v_rows)
    contract_out = (((1,), (1,)), ((), ()))
    grad_tokens = grad_r1 + lax.dot_general(
        grad_q_rows, wq_back, contract_out, preferred_element_type=jnp.float32
    )
    grad_tokens = grad_tokens + lax.dot_general(
        grad_k_rows, wk_back, contract_out, preferred_element_type=jnp.float32
    )
    grad_tokens = grad_tokens + lax.dot_general(
        grad_v_rows, wv_back, contract_out, preferred_element_type=jnp.float32
    )
    (
        share_wq,
        share_wk,
        share_wv,
        share_wo,
        share_win,
        share_wout,
        share_g1,
        share_b1,
        share_g2,
        share_b2,
    ) = (
        lax.psum_scatter(grad_wq, "dp", scatter_dimension=1, tiled=True),
        lax.psum_scatter(grad_wk, "dp", scatter_dimension=1, tiled=True),
        lax.psum_scatter(grad_wv, "dp", scatter_dimension=1, tiled=True),
        lax.psum_scatter(grad_wo, "dp", scatter_dimension=1, tiled=True),
        lax.psum_scatter(grad_win, "dp", scatter_dimension=1, tiled=True),
        lax.psum_scatter(grad_wout, "dp", scatter_dimension=1, tiled=True),
        lax.psum_scatter(grad_gain1, "dp", scatter_dimension=0, tiled=True),
        lax.psum_scatter(grad_bias1, "dp", scatter_dimension=0, tiled=True),
        lax.psum_scatter(grad_gain2, "dp", scatter_dimension=0, tiled=True),
        lax.psum_scatter(grad_bias2, "dp", scatter_dimension=0, tiled=True),
    )
    (
        final_wq,
        final_wk,
        final_wv,
        final_wo,
        final_win,
        final_wout,
        final_g1,
        final_b1,
        final_g2,
        final_b2,
    ) = (
        lax.psum(share_wq.astype(jnp.bfloat16), "seq").astype(jnp.float32),
        lax.psum(share_wk.astype(jnp.bfloat16), "seq").astype(jnp.float32),
        lax.psum(share_wv.astype(jnp.bfloat16), "seq").astype(jnp.float32),
        lax.psum(share_wo.astype(jnp.bfloat16), "seq").astype(jnp.float32),
        lax.psum(share_win.astype(jnp.bfloat16), "seq").astype(jnp.float32),
        lax.psum(share_wout.astype(jnp.bfloat16), "seq").astype(jnp.float32),
        lax.psum(share_g1.astype(jnp.bfloat16), "seq").astype(jnp.float32),
        lax.psum(share_b1.astype(jnp.bfloat16), "seq").astype(jnp.float32),
        lax.psum(share_g2.astype(jnp.bfloat16), "seq").astype(jnp.float32),
        lax.psum(share_b2.astype(jnp.bfloat16), "seq").astype(jnp.float32),
    )
    return (
        layer_out,
        grad_tokens.reshape(seq_count, local_len, model_width),
        final_wq,
        final_wk,
        final_wv,
        final_wo,
        final_win,
        final_wout,
        final_g1,
        final_b1,
        final_g2,
        final_b2,
    )


def solution(mesh):
    in_specs = (
        P("dp", "seq", None),
        P("dp"),
        P(),
        P(None, "dp"),
        P(None, "dp"),
        P(None, "dp"),
        P(None, "dp"),
        P(None, "dp"),
        P(None, "dp"),
        P("dp"),
        P("dp"),
        P("dp"),
        P("dp"),
        P("dp", "seq", None),
    )
    out_specs = (
        P("dp", "seq", None),
        P("dp", "seq", None),
        P(None, "dp"),
        P(None, "dp"),
        P(None, "dp"),
        P(None, "dp"),
        P(None, "dp"),
        P(None, "dp"),
        P("dp"),
        P("dp"),
        P("dp"),
        P("dp"),
    )
    return jax.shard_map(shards, mesh=mesh, in_specs=in_specs, out_specs=out_specs, check_vma=False)
```

profile of v0, /device:TPU:0, one launch (start us, length us, event | category | flops | bytes accessed | tf_op | source)
XLA Modules:
  0.0 704.7 jit_solution(9426483692324572481)
XLA Ops:
  10.6 24.6 %all-gather.7.cloned.1.call-done = bf16[768,768]{0,1:T(8,128)(2,1)} async-done(((bf16[768,96]{0,1:T(8,128)(2,1)}), bf16[768,768]{0,1:T(8,128)(2,1)}) %all-gather.7.cloned.1.call-update) | async-done | bytes 1179664 | tf_op jit(solution)/shard_map/all_gather | solution.py:119
  43.5 15.9 %all-gather.11.cloned.1.call-done = bf16[768,768]{0,1:T(8,128)(2,1)} async-done(((bf16[768,96]{0,1:T(8,128)(2,1)}), bf16[768,768]{0,1:T(8,128)(2,1)}) %all-gather.11.cloned.1.call-update) | async-done | bytes 1179664 | tf_op jit(solution)/shard_map/all_gather | solution.py:118
  69.8 16.1 %all-reduce.9 = (bf16[768]{0:T(1024)(128)(2,1)S(1)}, bf16[768]{0:T(1024)(128)(2,1)S(1)}, bf16[768]{0:T(1024)(128)(2,1)S(1)}, bf16[768]{0:T(1024)(128)(2,1)S(1)}) all-reduce(bf16[768]{0:T(1024)(128)(2,1)S(1)} %dynamic-update-slice.1, bf16[768]{0:T(1024)(128)(2,1)S(1)} %dynamic-update-slice, ...), channel_id=1, replica_groups=mesh['seq'=4,'dp'=8] {'dp'}, use_global_device_ids=true, to_apply=%add.1 | all-reduce | flops 3072 | bytes 12288
  111.4 7.3 %fusion.20 = f32[2,1024,3,256]{1,3,2,0:T(8,128)S(1)} fusion(f32[2,1024,3,64]{1,3,2,0:T(8,128)S(1)} %reshape.237, f32[64,256]{1,0:T(8,128)S(1)} %copy-done), kind=kOutput, calls=%fused_computation.64 | convolution fusion | flops 1208352768 | bytes 7929856 | tf_op jit(solution)/shard_map/snhe,em->snhm/dot_general | solution.py:41
  118.7 7.2 %fusion.16 = (f32[2,3,256]{2,1,0:T(4,128)S(1)}, f32[2,1024,3,256]{3,1,2,0:T(8,128)S(1)}) fusion(f32[2,1024]{1,0:T(2,128)S(1)} %compare_convert_fusion, f32[2,1024,3]{1,2,0:T(4,128)S(1)} %broadcast_multiply_fusion.3, f32[64,256]{1,0:T(8,128)S(1)} %copy-done, f32[2,1024,3,64]{1,3,2,0:T(8,128)S(1)} %reshape.236), kind=kOutput, calls=%fused_computation.31 | convolution fusion | flops 1213069824 | bytes 7968768 | tf_op jit(solution)/shard_map/snhe,em->snhm/dot_general | solution.py:41
  144.9 12.6 %all-to-all-done.3 = bf16[2,1024,192]{2,0,1:T(2,128)(2,1)S(1)} async-done(((bf16[2,1024,192]{2,0,1:T(2,128)(2,1)}), bf16[2,1024,192]{2,0,1:T(2,128)(2,1)S(1)}, u32[]{:S(2)}, u32[]{:S(2)}) %all-to-all-start.3) | async-done | bytes 786464 | tf_op jit(solution)/shard_map/all_to_all | solution.py:169
  169.4 20.8 %multiply_convert_fusion = (bf16[512,3072]{1,0:T(8,128)(2,1)}, f32[512,3072]{1,0:T(8,128)}, f32[512,3072]{1,0:T(8,128)}) fusion(bf16[768,3072]{1,0:T(8,128)(2,1)} %all-gather.15.cloned.1.call-done, f32[512,768]{1,0:T(8,128)} %copy-done.21, f32[768]{0:T(1024)S(1)} %convert_element_type.205, f32[768]{0:T(1024)S(1)} %convert_element_type.204, ...), kind=kOutput, calls=%fused_computation.6 | convolution fusion | flops 2520121344 | bytes 22030336 | tf_op jit(solution)/shard_map/dot_general | solution.py:175
  190.2 21.2 %all-gather.17.cloned.1.call-done = bf16[3072,768]{0,1:T(8,128)(2,1)} async-done(((bf16[3072,96]{0,1:T(8,128)(2,1)}), bf16[3072,768]{0,1:T(8,128)(2,1)}) %all-gather.17.cloned.1.call-update) | async-done | bytes 4718608 | tf_op jit(solution)/shard_map/all_gather | solution.py:123
  220.7 7.8 %add_convert_fusion = bf16[512,3072]{1,0:T(8,128)(2,1)S(1)} fusion(f32[512,3072]{1,0:T(8,128)S(1)} %copy-done.41, f32[512,3072]{1,0:T(8,128)} %get-tuple-element.52, bf16[3072,768]{0,1:T(8,128)(2,1)S(1)} %copy-done.33, f32[512,768]{1,0:T(8,128)S(1)} %get-tuple-element.40), kind=kOutput, calls=%fused_computation.5 | convolution fusion | flops 2438332416 | bytes 22020096 | tf_op jit(solution)/shard_map/dot_general | solution.py:202
  240.4 15.3 %all_to_all.102 = bf16[2,256,768]{1,0,2:T(2,128)(2,1)S(1)} all-to-all(bf16[2,256,768]{1,0,2:T(2,128)(2,1)S(1)} %copy.73), channel_id=1, replica_groups=mesh['seq'=4,'dp'=8] {'seq'}, dimensions={2} | all-to-all | bytes 1572864 | tf_op jit(solution)/shard_map/all_to_all | solution.py:218
  261.2 10.2 %fusion.8 = f32[2,3,256,64]{2,3,1,0:T(8,128)S(1)} fusion(f32[2,1024,3,256]{1,3,2,0:T(8,128)} %copy-done.1, f32[2,1024,3]{1,2,0:T(4,128)S(1)} %broadcast_multiply_fusion.2, f32[2,1024,3,64]{1,3,2,0:T(8,128)} %reshape.240, f32[2,1024,3]{1,2,0:T(4,128)S(1)} %bitcast.205), kind=kOutput, calls=%fused_computation.23 | convolution fusion | flops 1209925632 | bytes 8306688 | tf_op jit(solution)/shard_map/snhm,snhe->shme/dot_general | solution.py:83
  271.4 7.8 %fusion.24 = bf16[2,3,64,1024]{3,2,1,0:T(8,128)(2,1)} fusion(f32[2,3,256,64]{2,3,1,0:T(8,128)S(1)} %fusion.8, f32[2,1024,3,256]{3,1,2,0:T(8,128)S(1)} %bitcast.160, f32[2,1024]{1,0:T(2,128)S(1)} %compare_convert_fusion, f32[2,1024,3]{1,2,0:T(4,128)S(1)} %broadcast_multiply_fusion.3), kind=kOutput, calls=%fused_computation.74 | convolution fusion | flops 1211498496 | bytes 7503872 | tf_op jit(solution)/shard_map/snhm,shme->snhe/dot_general | solution.py:91
  281.7 15.8 %all_to_all.103 = bf16[2,1024,192]{2,0,1:T(2,128)(2,1)S(1)} all-to-all(bf16[2,1024,192]{2,0,1:T(2,128)(2,1)S(1)} %copy.85), channel_id=1, replica_groups=mesh['seq'=4,'dp'=8] {'seq'}, dimensions={1} | all-to-all | bytes 1572864 | tf_op jit(solution)/shard_map/all_to_all | solution.py:244
  306.1 8.3 %fusion.7 = f32[2,3,1,256]{3,2,1,0:T(1,128)S(1)} fusion(f32[2,1024,3,256]{1,3,2,0:T(8,128)} %copy-done.1, f32[2,1024,3]{1,2,0:T(4,128)S(1)} %broadcast_multiply_fusion.2, f32[2,1024,3,1]{1,2,0,3:T(4,128)S(1)} %bitcast.207), kind=kOutput, calls=%fused_computation.22 | convolution fusion | flops 20447232 | bytes 6346752 | tf_op jit(solution)/shard_map/snhm,snh->shm/dot_general | solution.py:84
  326.4 14.9 %all_to_all.104 = bf16[2,1024,192]{2,0,1:T(2,128)(2,1)S(1)} all-to-all(bf16[2,1024,192]{2,0,1:T(2,128)(2,1)S(1)} %copy.82), channel_id=1, replica_groups=mesh['seq'=4,'dp'=8] {'seq'}, dimensions={1} | all-to-all | bytes 1572864 | tf_op jit(solution)/shard_map/all_to_all | solution.py:237
  347.5 11.6 %fusion.56 = (f32[2,1024,3]{1,2,0:T(4,128)S(1)}, f32[2,1024,3,256]{1,3,2,0:T(8,128)S(1)}) fusion(f32[2,1024,3,256]{1,3,2,0:T(8,128)} %copy-done.1, f32[2,1024,3]{1,2,0:T(4,128)S(1)} %broadcast_multiply_fusion.2, f32[2,3,256]{2,1,0:T(4,128)S(1)} %get-tuple-element.46, f32[2,1024,3]{1,2,0:T(4,128)S(1)} %negate_divide_fusion, ...), kind=kOutput, calls=%fused_computation.125 | convolution fusion | flops 1216210944 | bytes 14653440 | tf_op jit(solution)/shard_map/snhe,shme->snhm/dot_general | solution.py:80
  364.4 13.3 %all_to_all.105 = bf16[2,1024,192]{2,0,1:T(2,128)(2,1)S(1)} all-to-all(bf16[2,1024,192]{2,0,1:T(2,128)(2,1)S(1)} %copy.77), channel_id=1, replica_groups=mesh['seq'=4,'dp'=8] {'seq'}, dimensions={1} | all-to-all | bytes 1572864 | tf_op jit(solution)/shard_map/all_to_all | solution.py:230
  382.9 7.2 %fusion.46 = f32[768,3072]{1,0:T(8,128)} fusion(bf16[512,3072]{1,0:T(8,128)(2,1)} %copy-done.40, f32[512,768]{1,0:T(8,128)S(1)} %copy-done.23, f32[768]{0:T(1024)S(1)} %convert_element_type.205, f32[768]{0:T(1024)S(1)} %convert_element_type.204, f32[512]{0:T(512)S(1)} %add_rsqrt_fusion.1, f32[512]{0:T(512)S(1)} %broadcast_multiply_fusion.8), kind=kOutput, calls=%fused_computation.118 | convolution fusion | flops 2417885184 | bytes 14166016 | tf_op jit(solution)/shard_map/dot_general | solution.py:34
  403.6 16.2 %reduce-scatter.7.cloned.1.call-done = f32[768,96]{0,1:T(8,128)} async-done(((f32[768,768]{0,1:T(8,128)}), f32[768,96]{0,1:T(8,128)}) %reduce-scatter.7.cloned.1.call-update) | async-done | bytes 294928 | tf_op jit(solution)/shard_map/reduce_scatter | solution.py:280
  421.5 99.0 %reduce-scatter.15.cloned.1.call-done = f32[768,384]{1,0:T(8,128)} async-done(((f32[768,3072]{1,0:T(8,128)}), f32[768,384]{1,0:T(8,128)}) %reduce-scatter.15.cloned.1.call-update) | async-done | bytes 1179664 | tf_op jit(solution)/shard_map/reduce_scatter | solution.py:284
  522.6 97.9 %reduce-scatter.17.cloned.1.call-done = f32[3072,96]{0,1:T(8,128)} async-done(((f32[3072,768]{0,1:T(8,128)}), f32[3072,96]{0,1:T(8,128)}) %reduce-scatter.17.cloned.1.call-update) | async-done | bytes 1179664 | tf_op jit(solution)/shard_map/reduce_scatter | solution.py:285
  623.4 25.9 %all-reduce.8 = (bf16[768]{0:T(1024)(128)(2,1)S(1)}, bf16[768]{0:T(1024)(128)(2,1)S(1)}, bf16[768]{0:T(1024)(128)(2,1)S(1)}, bf16[768]{0:T(1024)(128)(2,1)S(1)}) all-reduce(f32[768]{0:T(1024)S(1)} %get-tuple-element.12, f32[768]{0:T(1024)S(1)} %get-tuple-element.17, ...), channel_id=8, replica_groups=mesh['seq'=4,'dp'=8] {'dp'}, use_global_device_ids=true, to_apply=%region_27.0.clone | all-reduce | flops 3072 | bytes 18432
  649.6 9.9 %all-reduce.10 = (bf16[96]{0:T(256)(128)(2,1)S(1)}, bf16[96]{0:T(256)(128)(2,1)S(1)}, bf16[96]{0:T(256)(128)(2,1)S(1)}, bf16[96]{0:T(256)(128)(2,1)S(1)}) all-reduce(bf16[96]{0:T(256)(128)(2,1)S(1)} %dynamic-slice.19, bf16[96]{0:T(256)(128)(2,1)S(1)} %dynamic-slice.18, ...), channel_id=1, replica_groups=mesh['seq'=4,'dp'=8] {'seq'}, use_global_device_ids=true, to_apply=%region_28.0 | all-reduce | flops 384 | bytes 1536 | tf_op jit(solution)/shard_map/psum | solution.py:309
  667.2 20.8 %all-reduce.14.cloned.1.call-done = (bf16[768,96]{0,1:T(8,128)(2,1)}, bf16[768,96]{0,1:T(8,128)(2,1)}, bf16[768,96]{0,1:T(8,128)(2,1)}, bf16[768,96]{0,1:T(8,128...) async-done(((bf16[768,96]{0,1:T(8,128)(2,1)}, bf16[768,96]{0,1:T(8,128)(2,1)}, bf16[768,96]{0,1:T(8,128)(2,1)}, bf16[768,96]{0,1:T(8,128)(2,1)}, ...) | async-done | bytes 1769488 | tf_op jit(solution)/shard_map/psum | solution.py:303
  (255 shorter events, 180.5 us)
Async XLA Ops:
  7.2 104.2 %copy-start = (f32[64,256]{1,0:T(8,128)S(1)}, f32[64,256]{1,0:T(8,128)}, u32[]{:S(2)}) copy-start(f32[64,256]{1,0:T(8,128)} %param.16) | copy-start | bytes 196612
  7.2 28.0 %all-gather.7.cloned.1.call-start = ((), (), s32[]{:S(2)}) async-start(), calls=%async_computation.14 | async-start | bytes 1327104 | tf_op jit(solution)/shard_map/all_gather | solution.py:119
  7.9 51.4 %all-gather.11.cloned.1.call-start = ((), (), s32[]{:S(2)}) async-start(), calls=%async_computation.16 | async-start | bytes 1327104 | tf_op jit(solution)/shard_map/all_gather | solution.py:118
  8.7 77.2 %all-gather.9.cloned.1.call-start = ((), (), s32[]{:S(2)}) async-start(), calls=%async_computation.15 | async-start | bytes 1327104 | tf_op jit(solution)/shard_map/all_gather | solution.py:120
  9.4 156.0 %all-gather.13.cloned.1.call-start = ((), (), s32[]{:S(2)}) async-start(), calls=%async_computation.17 | async-start | bytes 1327104 | tf_op jit(solution)/shard_map/all_gather | solution.py:121
  10.0 159.4 %all-gather.15.cloned.1.call-start = ((), (), s32[]{:S(2)}) async-start(), calls=%async_computation.18 | async-start | bytes 5308416 | tf_op jit(solution)/shard_map/all_gather | solution.py:122
  37.5 21.9 %copy-start.12 = (bf16[2,256,768]{2,1,0:T(8,128)(2,1)S(1)}, bf16[2,256,768]{2,1,0:T(8,128)(2,1)}, u32[]{:S(2)}) copy-start(bf16[2,256,768]{2,1,0:T(8,128)(2,1)} %param.14) | copy-start | bytes 2359300
  39.3 24.0 %all-to-all-start = ((bf16[2,256,768]{1,0,2:T(2,128)(2,1)}), bf16[2,256,768]{1,0,2:T(2,128)(2,1)S(1)}, u32[]{:S(2)}, u32[]{:S(2)}) async-start(bf16[2,256,768]{1,0,2:T(2,128)(2,1)} %copy.60), calls=%async_computation | async-start | bytes 1572864 | tf_op jit(solution)/shard_map/all_to_all | solution.py:145
  42.8 168.6 %all-gather.17.cloned.1.call-start = ((), (), s32[]{:S(2)}) async-start(), calls=%async_computation.19 | async-start | bytes 5308416 | tf_op jit(solution)/shard_map/all_gather | solution.py:123
  63.3 28.6 %all-to-all-start.2 = ((bf16[2,256,768]{1,0,2:T(2,128)(2,1)}), bf16[2,256,768]{1,0,2:T(2,128)(2,1)}, u32[]{:S(2)}, u32[]{:S(2)}) async-start(bf16[2,256,768]{1,0,2:T(2,128)(2,1)} %copy.66), calls=%async_computation.2 | async-start | bytes 1572864 | tf_op jit(solution)/shard_map/all_to_all | solution.py:138
  91.9 26.8 %copy-start.3 = (f32[2,1024,3,64]{1,3,2,0:T(8,128)}, f32[2,1024,3,64]{1,3,2,0:T(8,128)S(1)}, u32[]{:S(2)}) copy-start(f32[2,1024,3,64]{1,3,2,0:T(8,128)S(1)} %reshape.236) | copy-start | bytes 4718596
  91.9 14.2 %all-to-all-start.1 = ((bf16[2,256,768]{1,0,2:T(2,128)(2,1)}), bf16[2,256,768]{1,0,2:T(2,128)(2,1)}, u32[]{:S(2)}, u32[]{:S(2)}) async-start(bf16[2,256,768]{1,0,2:T(2,128)(2,1)} %copy.63), calls=%async_computation.1 | async-start | bytes 1572864 | tf_op jit(solution)/shard_map/all_to_all | solution.py:152
  118.7 14.4 %copy-start.1 = (f32[2,1024,3,256]{1,3,2,0:T(8,128)}, f32[2,1024,3,256]{1,3,2,0:T(8,128)S(1)}, u32[]{:S(2)}) copy-start(f32[2,1024,3,256]{1,3,2,0:T(8,128)S(1)} %fusion.20) | copy-start | bytes 18874372
  140.8 16.7 %all-to-all-start.3 = ((bf16[2,1024,192]{2,0,1:T(2,128)(2,1)}), bf16[2,1024,192]{2,0,1:T(2,128)(2,1)S(1)}, u32[]{:S(2)}, u32[]{:S(2)}) async-start(bf16[2,1024,192]{2,0,1:T(2,128)(2,1)} %copy.70), calls=%async_computation.3 | async-start | bytes 2097152 | tf_op jit(solution)/shard_map/all_to_all | solution.py:169
  144.3 254.4 %reduce-scatter.13.cloned.1.call-start = ((), (), s32[]{:S(2)}) async-start(), calls=%async_computation.23 | async-start | bytes 2654208 | tf_op jit(solution)/shard_map/reduce_scatter | solution.py:283
  235.0 165.3 %reduce-scatter.11.cloned.1.call-start = ((), (), s32[]{:S(2)}) async-start(), calls=%async_computation.22 | async-start | bytes 2654208 | tf_op jit(solution)/shard_map/reduce_scatter | solution.py:282
  258.1 13.3 %slice-start = ((s8[6291456]{0:T(1024)(128)(4,1)}), s8[2097152]{0:T(1024)(128)(4,1)S(1)}, s32[]{:S(2)}) async-start(s8[6291456]{0:T(1024)(128)(4,1)} %bitcast.159), calls=%async_computation.27 | async-start | bytes 4194304
  301.4 13.0 %slice-start.2 = ((s8[6291456]{0:T(1024)(128)(4,1)}), s8[2097152]{0:T(1024)(128)(4,1)S(1)}, s32[]{:S(2)}) async-start(s8[6291456]{0:T(1024)(128)(4,1)} %bitcast.161), calls=%async_computation.29 | async-start | bytes 4194304
  303.6 98.3 %reduce-scatter.9.cloned.1.call-start = ((), (), s32[]{:S(2)}) async-start(), calls=%async_computation.21 | async-start | bytes 2654208 | tf_op jit(solution)/shard_map/reduce_scatter | solution.py:281
  347.5 72.3 %reduce-scatter.7.cloned.1.call-start = ((), (), s32[]{:S(2)}) async-start(), calls=%async_computation.20 | async-start | bytes 2654208 | tf_op jit(solution)/shard_map/reduce_scatter | solution.py:280
  382.9 137.6 %reduce-scatter.15.cloned.1.call-start = ((), (), s32[]{:S(2)}) async-start(), calls=%async_computation.24 | async-start | bytes 10616832 | tf_op jit(solution)/shard_map/reduce_scatter | solution.py:284
  390.2 230.3 %reduce-scatter.17.cloned.1.call-start = ((), (), s32[]{:S(2)}) async-start(), calls=%async_computation.25 | async-start | bytes 10616832 | tf_op jit(solution)/shard_map/reduce_scatter | solution.py:285
  398.6 289.4 %all-reduce.14.cloned.1.call-start = ((), (), s32[]{:S(2)}) async-start(), calls=%async_computation.26 | async-start | bytes 3538944 | tf_op jit(solution)/shard_map/psum | solution.py:303
  421.5 240.1 %copy-start.35 = (bf16[768,768]{0,1:T(8,128)(2,1)S(1)}, bf16[768,768]{0,1:T(8,128)(2,1)}, u32[]{:S(2)}) copy-start(bf16[768,768]{0,1:T(8,128)(2,1)} %all-gather.11.cloned.1.call-done) | copy-start | bytes 3538948
  (41 other events, 201.2 us)
Sparse Core Ops, SparseCore 0:
  9.6 25.4 all-gather.6
  36.8 22.5 all-gather.10
  61.0 22.6 all-gather.8
  85.2 22.2 all-gather.12
  108.9 51.0 all-gather.14
  161.5 49.8 all-gather.16
  235.2 35.8 reduce-scatter.12
  303.8 34.1 reduce-scatter.10
  347.6 34.1 reduce-scatter.8
  383.9 35.8 reduce-scatter.6
  422.1 98.2 reduce-scatter.14
  522.6 97.8 reduce-scatter.16
  624.9 63.0 all-reduce.13
where the time goes:
time: 711 us; the launch traced here: 705 us
  waiting for transfers between devices  315 us (44%)
  matrix products  157 us (22%)
  blocking collectives  111 us (16%)
  local copies, waits for them, and re-layouts  57.5 us (8%)
  other arithmetic  30.1 us (4%)
  starting transfers between devices  16.5 us (2%)
  between operations  16.4 us (2%)
    reduce_scatter x1, waiting for transfers between devices, shards(): lax.psum_scatter(grad_win, 'dp', scatter_dimension=1, tiled=True)  99 us
    reduce_scatter x1, waiting for transfers between devices, shards(): lax.psum_scatter(grad_wout, 'dp', scatter_dimension=1, tiled=True)  97.9 us
    unnamed x2, blocking collectives  42 us
    all_gather x1, waiting for transfers between devices, shards(): lax.all_gather(w_key, 'dp', axis=1, tiled=True)  24.6 us
    dot_general x6, matrix products, row_product(): lax.dot_general(left, right, (((0,), (0,)), ((), ())), preferred_element_...  23.1 us
    all_gather x1, waiting for transfers between devices, shards(): lax.all_gather(w_out, 'dp', axis=1, tiled=True)  21.2 us
    psum x1, waiting for transfers between devices, shards(): lax.psum(share_wq.astype(jnp.bfloat16), 'seq').astype(jnp.float32)  20.8 us
    dot_general x1, matrix products, shards(): pre_act = jnp.dot(hidden_low, win_full, preferred_element_type=jnp.float32)  20.8 us
  transfers between devices with their start and end apart: 17, of which 9 were waited for; matrix products, arithmetic and copies ran while one was open for 29% of the time, Pallas kernels for 0%

commit v1 on v0

--- a/solution.py
+++ b/solution.py
@@ -1,9 +1,133 @@
+import functools
 from functools import partial
 
 import jax
 import jax.numpy as jnp
 from jax import lax
+from jax.experimental import pallas as pl
+from jax.experimental.pallas import tpu as pltpu
 from jax.sharding import PartitionSpec as P
+
+MESH = pl.DeviceIdType.MESH
+bf = jnp.bfloat16
+
+
+def coords():
+    s, d = lax.axis_index("seq"), lax.axis_index("dp")
+    return s // 2, s % 2, d // 2, d % 2
+
+def dev(y, x, z, c):
+    return (y * 2 + x, z * 2 + c)
+
+def entry_barrier(peers):
+    sem = pltpu.get_barrier_semaphore()
+    for p in peers:
+        pl.semaphore_signal(sem, inc=1, device_id=p, device_id_type=MESH)
+    pl.semaphore_wait(sem, len(peers))
+
+def piece(g, ref, d, y, x):
+    if g < 2:  return ref.at[y, d, x]
+    if g == 2: return ref.at[d, y, x]
+    return ref.at[y, x, d]
+def lpiece(g, ref, y, x):
+    return ref.at[y, x]
+def shard(g, ref, d):
+    if g < 2:  return ref.at[:, d]
+    if g == 2: return ref.at[d]
+    return ref.at[:, :, d]
+
+def ag_kernel(nz, *refs):
+    loc, out, sems = refs[:4], refs[4:8], refs[8:]
+    zs, zr, xs, xr, ys, yr, ds_, dr, ss, sr, ls = sems
+    y, x, z, c = coords()
+    ynb, xnb, sib = dev(1 - y, x, z, c), dev(y, 1 - x, z, c), dev(y, x, z, 1 - c)
+    zpeer = [dev(y, x, (z + k) % nz, c) for k in range(1, nz)]
+    entry_barrier([ynb, xnb, sib] + zpeer)
+    half = loc[0].shape[-1] // 2
+    H = (pl.ds(0, half), pl.ds(half, half))
+    me = z * 2 + c
+    started = []
+    def rc(src, dst, ssem, rsem, to):
+        cp = pltpu.make_async_remote_copy(src_ref=src, dst_ref=dst, send_sem=ssem, recv_sem=rsem, device_id=to, device_id_type=MESH)
+        return cp
+    def go(cp):
+        cp.start(); started.append(cp)
+    def recv(dst, ssem, rsem, to):
+        rc(dst, dst, ssem, rsem, to).wait_recv()
+    G = range(4)
+    for g in G:
+        for k in range(1, nz):
+            go(rc(lpiece(g, loc[g], y, x), piece(g, out[g], me, y, x), zs.at[g, k-1], zr.at[g, k-1], zpeer[k-1]))
+        go(rc(loc[g], shard(g, out[g], me), ss.at[g, 0], sr.at[g, 0], sib))
+    lc = []
+    for g in G:
+        cp = pltpu.make_async_copy(loc[g], shard(g, out[g], me), ls.at[g]); cp.start(); lc.append(cp)
+    def st1(g):
+        for k in range(1, nz):
+            d = ((z + nz - k) % nz) * 2 + c
+            p = piece(g, out[g], d, y, x)
+            recv(p, zs.at[g, k-1], zr.at[g, k-1], zpeer[k-1])
+            go(rc(p, p, xs.at[g, k-1], xr.at[g, k-1], xnb))
+            go(rc(p, p, ys.at[g, k-1], yr.at[g, k-1], ynb))
+    def st2(g):
+        for k in range(1, nz):
+            d = ((z + nz - k) % nz) * 2 + c
+            p = piece(g, out[g], d, y, 1 - x)
+            recv(p, xs.at[g, k-1], xr.at[g, k-1], xnb)
+            pa = p.at[:, H[0]]
+            go(rc(pa, pa, ds_.at[g, k-1, 0], dr.at[g, k-1, 0], ynb))
+            p = piece(g, out[g], d, 1 - y, x)
+            recv(p, ys.at[g, k-1], yr.at[g, k-1], ynb)
+            pb = p.at[:, H[1]]
+            go(rc(pb, pb, ds_.at[g, k-1, 1], dr.at[g, k-1, 1], xnb))
+    def st3(g):
+        for k in range(1, nz):
+            d = ((z + nz - k) % nz) * 2 + c
+            p = piece(g, out[g], d, 1 - y, 1 - x)
+            pa, pb = p.at[:, H[0]], p.at[:, H[1]]
+            recv(pa, ds_.at[g, k-1, 0], dr.at[g, k-1, 0], ynb)
+            recv(pb, ds_.at[g, k-1, 1], dr.at[g, k-1, 1], xnb)
+            sh = shard(g, out[g], d)
+            go(rc(sh, sh, ss.at[g, k], sr.at[g, k], sib))
+    for t in range(6):
+        if t < 4: st1(t)
+        if 0 <= t - 1 < 4: st2(t - 1)
+        if 0 <= t - 2 < 4: st3(t - 2)
+    for g in G:
+        for k in range(nz):
+            d = ((z + nz - k) % nz) * 2 + (1 - c)
+            sh = shard(g, out[g], d)
+            recv(sh, ss.at[g, k], sr.at[g, k], sib)
+    for cp in lc: cp.wait()
+    for cp in started: cp.wait_send()
+
+def gather_weights(kv, qo, win, wout, dp):
+    nz = dp // 2
+    D = kv.shape[-1]
+    a, b, c_ = kv.shape[2], win.shape[2], wout.shape[2]
+    shp = [(2, dp, 2, a, D), (2, dp, 2, a, D), (dp, 2, 2, b, D), (2, 2, dp, c_, D)]
+    S = pltpu.SemaphoreType.DMA
+    n = nz - 1
+    hb = pl.BlockSpec(memory_space=pl.ANY)
+    return pl.pallas_call(
+        functools.partial(ag_kernel, nz),
+        out_shape=[jax.ShapeDtypeStruct(s, bf) for s in shp],
+        in_specs=[hb] * 4, out_specs=[hb] * 4,
+        scratch_shapes=[S((4, n)), S((4, n)), S((4, n)), S((4, n)), S((4, n)), S((4, n)), S((4, n, 2)), S((4, n, 2)), S((4, nz)), S((4, nz)), S((4,))],
+        compiler_params=pltpu.CompilerParams(collective_id=1, has_side_effects=True),
+    )(kv, qo, win, wout)
+
+def pack(wq, wk, wv, wo, win, wout):
+    D = wq.shape[0]
+    sh = wq.shape[1]
+    t = jnp.transpose
+    kv = jnp.stack([t(wk), t(wv)]).reshape(2, 2, sh // 2, D)
+    qo = jnp.stack([t(wq), t(wo)]).reshape(2, 2, sh // 2, D)
+    wi = t(win).reshape(2, 2, win.shape[1] // 4, D)
+    ff = wout.shape[0]
+    wu = t(wout.reshape(ff // D, D, sh), (0, 2, 1)).reshape(2, 2, sh, D)
+    return kv, qo, wi, wu
+
 
 HEAD = 64
 
@@ -49,8 +173,9 @@
     return grad_scaled * HEAD ** (-0.25)
 
 
-def keep_local(key_state, key_total):
-    return (key_state, key_total)
+def seq_sum(key_state, key_total):
+    joined = lax.psum(jnp.concatenate([key_state, key_total[..., None]], -1), "seq")
+    return (joined[..., :-1], joined[..., -1])
 
 
 def mixer_forward(queries, key_proj, value_proj, key_mask, random_features, reducer):
@@ -114,68 +239,42 @@
     row_count = seq_count * local_len
     seq_parts = lax.axis_size("seq")
     heads_all = model_width // HEAD
-    wq_full, wk_full, wv_full, wo_full, win_full, wout_full, gain1, bias1, gain2, bias2 = (
-        lax.all_gather(w_query, "dp", axis=1, tiled=True),
-        lax.all_gather(w_key, "dp", axis=1, tiled=True),
-        lax.all_gather(w_value, "dp", axis=1, tiled=True),
-        lax.all_gather(w_output, "dp", axis=1, tiled=True),
-        lax.all_gather(w_in, "dp", axis=1, tiled=True),
-        lax.all_gather(w_out, "dp", axis=1, tiled=True),
-        lax.all_gather(ln1_gain, "dp", axis=0, tiled=True),
-        lax.all_gather(ln1_bias, "dp", axis=0, tiled=True),
-        lax.all_gather(ln2_gain, "dp", axis=0, tiled=True),
-        lax.all_gather(ln2_bias, "dp", axis=0, tiled=True),
+    dp_size = lax.axis_size("dp")
+    ff_width = w_in.shape[1] * dp_size
+    if seq_parts == 4 and dp_size == 8 and w_query.shape[1] % 32 == 0:
+        kv, qo, wi, wu = gather_weights(*pack(w_query, w_key, w_value, w_output, w_in, w_out), dp_size)
+        square = (model_width, model_width)
+        wk_full, wv_full = kv[0].reshape(square), kv[1].reshape(square)
+        wq_full, wo_full = qo[0].reshape(square), qo[1].reshape(square)
+        win_full = wi.reshape(ff_width, model_width)
+        wout_full = jnp.transpose(wu.reshape(ff_width // model_width, *square), (1, 0, 2)).reshape(model_width, ff_width)
+    else:
+        wq_full, wk_full, wv_full, wo_full, win_full, wout_full = (
+            lax.all_gather(w, "dp", axis=1, tiled=True).T
+            for w in (w_query, w_key, w_value, w_output, w_in, w_out)
+        )
+    gain1, bias1, gain2, bias2 = lax.all_gather(
+        jnp.stack([ln1_gain, ln1_bias, ln2_gain, ln2_bias]), "dp", axis=1, tiled=True
     )
     tok_rows = tokens.reshape(row_count, model_width)
-    query_proj = jnp.dot(tok_rows, wq_full, preferred_element_type=jnp.float32).astype(jnp.bfloat16)
-    key_proj = jnp.dot(tok_rows, wk_full, preferred_element_type=jnp.float32).astype(jnp.bfloat16)
-    value_proj = jnp.dot(tok_rows, wv_full, preferred_element_type=jnp.float32).astype(jnp.bfloat16)
+    query_proj = lax.dot_general(tok_rows, wq_full, (((1,), (1,)), ((), ())), preferred_element_type=jnp.float32).astype(jnp.bfloat16)
+    key_proj = lax.dot_general(tok_rows, wk_full, (((1,), (1,)), ((), ())), preferred_element_type=jnp.float32).astype(jnp.bfloat16)
+    value_proj = lax.dot_general(tok_rows, wv_full, (((1,), (1,)), ((), ())), preferred_element_type=jnp.float32).astype(jnp.bfloat16)
     local_pos = lax.axis_index("seq") * local_len + jnp.arange(local_len, dtype=jnp.int32)
     row_valid = (local_pos[None, :] < lengths[:, None]).astype(jnp.float32)
-    full_len = local_len * seq_parts
-    head_group = heads_all // seq_parts
-    q_heads, k_heads, v_heads = (
-        lax.all_to_all(
-            query_proj.reshape(seq_count, local_len, model_width),
-            "seq",
-            split_axis=2,
-            concat_axis=1,
-            tiled=True,
-        ),
-        lax.all_to_all(
-            key_proj.reshape(seq_count, local_len, model_width),
-            "seq",
-            split_axis=2,
-            concat_axis=1,
-            tiled=True,
-        ),
-        lax.all_to_all(
-            value_proj.reshape(seq_count, local_len, model_width),
-            "seq",
-            split_axis=2,
-            concat_axis=1,
-            tiled=True,
-        ),
-    )
-    q_heads = q_heads.reshape(seq_count, full_len, head_group, HEAD)
-    k_heads = k_heads.reshape(seq_count, full_len, head_group, HEAD)
-    v_heads = v_heads.reshape(seq_count, full_len, head_group, HEAD)
-    full_pos = jnp.arange(full_len, dtype=jnp.int32)
-    key_mask = (full_pos[None, :] < lengths[:, None]).astype(jnp.float32)
-    context, kept_mixer = mixer_forward(
-        q_heads, k_heads, v_heads, key_mask, random_features, keep_local
-    )
-    ctx_low = context.astype(jnp.bfloat16).reshape(seq_count, full_len, head_group * HEAD)
-    ctx_tokens = lax.all_to_all(ctx_low, "seq", split_axis=1, concat_axis=2, tiled=True)
-    ctx_rows = ctx_tokens.reshape(row_count, model_width)
-    attn_out = jnp.dot(ctx_rows, wo_full, preferred_element_type=jnp.float32)
+    q_heads = query_proj.reshape(seq_count, local_len, heads_all, HEAD)
+    k_heads = key_proj.reshape(seq_count, local_len, heads_all, HEAD)
+    v_heads = value_proj.reshape(seq_count, local_len, heads_all, HEAD)
+    context, kept_mixer = mixer_forward(q_heads, k_heads, v_heads, row_valid, random_features, seq_sum)
+    ctx_rows = context.astype(jnp.bfloat16).reshape(row_count, model_width)
+    attn_out = lax.dot_general(ctx_rows, wo_full, (((1,), (1,)), ((), ())), preferred_element_type=jnp.float32)
     resid1 = tok_rows.astype(jnp.float32) + attn_out
     hidden, normed1, inv1 = layer_norm(resid1, gain1.astype(jnp.float32), bias1.astype(jnp.float32))
     hidden_low = hidden.astype(jnp.bfloat16)
-    pre_act = jnp.dot(hidden_low, win_full, preferred_element_type=jnp.float32)
+    pre_act = lax.dot_general(hidden_low, win_full, (((1,), (1,)), ((), ())), preferred_element_type=jnp.float32)
     activated, gelu_pull = jax.vjp(partial(jax.nn.gelu, approximate=False), pre_act)
     act_low = activated.astype(jnp.bfloat16)
-    ffn_out = jnp.dot(act_low, wout_full, preferred_element_type=jnp.float32)
+    ffn_out = lax.dot_general(act_low, wout_full, (((1,), (1,)), ((), ())), preferred_element_type=jnp.float32)
     normed_out, normed2, inv2 = layer_norm(
         hidden + ffn_out, gain2.astype(jnp.float32), bias2.astype(jnp.float32)
     )
@@ -184,15 +283,7 @@
         (normed_out * valid_rows).astype(jnp.bfloat16).reshape(seq_count, local_len, model_width)
     )
     wq_back, wk_back, wv_back, wo_back, win_back, wout_back, gain1_back, gain2_back = (
-        lax.all_gather(w_query, "dp", axis=1, tiled=True),
-        lax.all_gather(w_key, "dp", axis=1, tiled=True),
-        lax.all_gather(w_value, "dp", axis=1, tiled=True),
-        lax.all_gather(w_output, "dp", axis=1, tiled=True),
-        lax.all_gather(w_in, "dp", axis=1, tiled=True),
-        lax.all_gather(w_out, "dp", axis=1, tiled=True),
-        lax.all_gather(ln1_gain, "dp", axis=0, tiled=True),
-        lax.all_gather(ln2_gain, "dp", axis=0, tiled=True),
-    )
+        wq_full, wk_full, wv_full, wo_full, win_full, wout_full, gain1, gain2)
     grad_y = cotangent.reshape(row_count, model_width).astype(jnp.float32) * valid_rows
     grad_r2, grad_gain2, grad_bias2 = norm_back(
         grad_y, normed2, inv2, gain2_back.astype(jnp.float32)
@@ -200,12 +291,12 @@
     grad_ffn = grad_r2.astype(jnp.bfloat16)
     grad_wout = row_product(act_low, grad_ffn)
     grad_act = lax.dot_general(
-        grad_ffn, wout_back, (((1,), (1,)), ((), ())), preferred_element_type=jnp.float32
+        grad_ffn, wout_back, (((1,), (0,)), ((), ())), preferred_element_type=jnp.float32
     )
     grad_pre = gelu_pull(grad_act)[0].astype(jnp.bfloat16)
     grad_win = row_product(hidden_low, grad_pre)
     grad_hidden = grad_r2 + lax.dot_general(
-        grad_pre, win_back, (((1,), (1,)), ((), ())), preferred_element_type=jnp.float32
+        grad_pre, win_back, (((1,), (0,)), ((), ())), preferred_element_type=jnp.float32
     )
     grad_r1, grad_gain1, grad_bias1 = norm_back(
         grad_hidden, normed1, inv1, gain1_back.astype(jnp.float32)
@@ -213,49 +304,17 @@
     grad_attn = grad_r1.astype(jnp.bfloat16)
     grad_wo = row_product(ctx_rows, grad_attn)
     grad_ctx = lax.dot_general(
-        grad_attn, wo_back, (((1,), (1,)), ((), ())), preferred_element_type=jnp.float32
+        grad_attn, wo_back, (((1,), (0,)), ((), ())), preferred_element_type=jnp.float32
     ).astype(jnp.bfloat16)
-    grad_heads = lax.all_to_all(
-        grad_ctx.reshape(seq_count, local_len, model_width),
-        "seq",
-        split_axis=2,
-        concat_axis=1,
-        tiled=True,
-    )
-    grad_heads = grad_heads.reshape(seq_count, full_len, head_group, HEAD)
-    grad_q, grad_k, grad_v = mixer_backward(
-        grad_heads, v_heads, kept_mixer, random_features, keep_local
-    )
-    grad_q_tok, grad_k_tok, grad_v_tok = (
-        lax.all_to_all(
-            grad_q.astype(jnp.bfloat16).reshape(seq_count, full_len, head_group * HEAD),
-            "seq",
-            split_axis=1,
-            concat_axis=2,
-            tiled=True,
-        ),
-        lax.all_to_all(
-            grad_k.astype(jnp.bfloat16).reshape(seq_count, full_len, head_group * HEAD),
-            "seq",
-            split_axis=1,
-            concat_axis=2,
-            tiled=True,
-        ),
-        lax.all_to_all(
-            grad_v.astype(jnp.bfloat16).reshape(seq_count, full_len, head_group * HEAD),
-            "seq",
-            split_axis=1,
-            concat_axis=2,
-            tiled=True,
-        ),
-    )
-    grad_q_rows = grad_q_tok.reshape(row_count, model_width)
-    grad_k_rows = grad_k_tok.reshape(row_count, model_width)
-    grad_v_rows = grad_v_tok.reshape(row_count, model_width)
+    grad_heads = grad_ctx.reshape(seq_count, local_len, heads_all, HEAD)
+    grad_q, grad_k, grad_v = mixer_backward(grad_heads, v_heads, kept_mixer, random_features, seq_sum)
+    grad_q_rows, grad_k_rows, grad_v_rows = (
+        g.astype(jnp.bfloat16).reshape(row_count, model_width) for g in (grad_q, grad_k, grad_v)
+    )
     grad_wq = row_product(tok_rows, grad_q_rows)
     grad_wk = row_product(tok_rows, grad_k_rows)
     grad_wv = row_product(tok_rows, grad_v_rows)
-    contract_out = (((1,), (1,)), ((), ()))
+    contract_out = (((1,), (0,)), ((), ()))
     grad_tokens = grad_r1 + lax.dot_general(
         grad_q_rows, wq_back, contract_out, preferred_element_type=jnp.float32
     )
@@ -277,12 +336,12 @@
         share_g2,
         share_b2,
     ) = (
-        lax.psum_scatter(grad_wq, "dp", scatter_dimension=1, tiled=True),
-        lax.psum_scatter(grad_wk, "dp", scatter_dimension=1, tiled=True),
-        lax.psum_scatter(grad_wv, "dp", scatter_dimension=1, tiled=True),
-        lax.psum_scatter(grad_wo, "dp", scatter_dimension=1, tiled=True),
-        lax.psum_scatter(grad_win, "dp", scatter_dimension=1, tiled=True),
-        lax.psum_scatter(grad_wout, "dp", scatter_dimension=1, tiled=True),
+        lax.psum_scatter(grad_wq.astype(jnp.bfloat16), "dp", scatter_dimension=1, tiled=True),
+        lax.psum_scatter(grad_wk.astype(jnp.bfloat16), "dp", scatter_dimension=1, tiled=True),
+        lax.psum_scatter(grad_wv.astype(jnp.bfloat16), "dp", scatter_dimension=1, tiled=True),
+        lax.psum_scatter(grad_wo.astype(jnp.bfloat16), "dp", scatter_dimension=1, tiled=True),
+        lax.psum_scatter(grad_win.astype(jnp.bfloat16), "dp", scatter_dimension=1, tiled=True),
+        lax.psum_scatter(grad_wout.astype(jnp.bfloat16), "dp", scatter_dimension=1, tiled=True),
         lax.psum_scatter(grad_gain1, "dp", scatter_dimension=0, tiled=True),
         lax.psum_scatter(grad_bias1, "dp", scatter_dimension=0, tiled=True),
         lax.psum_scatter(grad_gain2, "dp", scatter_dimension=0, tiled=True),

time: 711 us -> 669 us (0.941)
  Pallas kernels: 0 us -> 67.9 us
  blocking collectives: 111 us -> 49.9 us
  waiting for transfers between devices: 315 us -> 288 us
  starting transfers between devices: 16.5 us -> 0.37 us
  matrix products: 157 us -> 168 us
  other arithmetic: 30.1 us -> 21 us
  local copies, waits for them, and re-layouts: 57.5 us -> 49.1 us
    pallas_call x0 -> x1, Pallas kernels: none -> 67.9 us  [gather_weights(): pl.pallas_call(functools.partial(ag_kernel, nz), out_shape=[jax.ShapeDtyp...]
    all_gather x6 -> x0, waiting for transfers between devices: 61.8 us -> none  [the longest x1 24.6 us: shards(): lax.all_gather(w_key, 'dp', axis=1, tiled=True)]
    all_to_all x4 -> x0, blocking collectives: 59.4 us -> none  [the longest x1 15.8 us: shards(): lax.all_to_all(grad_v.astype(jnp.bfloat16).reshape(seq_count, full_len, h...]
    psum x0 -> x2, waiting for transfers between devices: none -> 58.2 us  [seq_sum(): lax.psum(jnp.concatenate([key_state, key_total[..., None]], -1), 'seq')]
    reduce_scatter x6 -> x5, waiting for transfers between devices: 213 us -> 188 us  [the longest x1 55.4 us: shards(): lax.psum_scatter(grad_wout.astype(jnp.bfloat16), 'dp', scatter_dimension=...]
    all_to_all x13 -> x0, local copies, waits for them, and re-layouts: 18.4 us -> none  [the longest x2 5.96 us: shards(): lax.all_to_all(ctx_low, 'seq', split_axis=1, concat_axis=2, tiled=True)]
    unnamed x2 -> x1, blocking collectives: 42 us -> 25.9 us
    unnamed x13 -> x10, waiting for transfers between devices: 3.75 us -> 19.8 us
  transfers between devices with their start and end apart: 17 -> 9, of which waited for: 9 -> 9; matrix products, arithmetic and copies ran while one was open for 29% -> 15% of each run, Pallas kernels for 0% -> 0%
where the time goes in v1:
time: 669 us; the launch traced here: 660 us
  waiting for transfers between devices  288 us (43%)
  matrix products  168 us (25%)
  Pallas kernels  67.9 us (10%)
  blocking collectives  49.9 us (7%)
  local copies, waits for them, and re-layouts  49.1 us (7%)
  other arithmetic  21 us (3%)
  between operations  15.8 us (2%)
    pallas_call x1, Pallas kernels, gather_weights(): pl.pallas_call(functools.partial(ag_kernel, nz), out_shape=[jax.ShapeDtyp...  67.9 us
    psum x2, waiting for transfers between devices, seq_sum(): lax.psum(jnp.concatenate([key_state, key_total[..., None]], -1), 'seq')  58.2 us
    reduce_scatter x1, waiting for transfers between devices, shards(): lax.psum_scatter(grad_wout.astype(jnp.bfloat16), 'dp', scatter_dimension=...  55.4 us
    reduce_scatter x1, waiting for transfers between devices, shards(): lax.psum_scatter(grad_wk.astype(jnp.bfloat16), 'dp', scatter_dimension=1,...  34.1 us
    reduce_scatter x1, waiting for transfers between devices, shards(): lax.psum_scatter(grad_wo.astype(jnp.bfloat16), 'dp', scatter_dimension=1,...  33.5 us
    reduce_scatter x1, waiting for transfers between devices, shards(): lax.psum_scatter(grad_wv.astype(jnp.bfloat16), 'dp', scatter_dimension=1,...  33.4 us
    reduce_scatter x1, waiting for transfers between devices, shards(): lax.psum_scatter(grad_wq.astype(jnp.bfloat16), 'dp', scatter_dimension=1,...  32 us
    dot_general x1, matrix products, shards(): lax.dot_general(hidden_low, win_full, (((1,), (1,)), ((), ())), preferred...  29.8 us
  transfers between devices with their start and end apart: 9, of which 9 were waited for; matrix products, arithmetic and copies ran while one was open for 15% of the time, Pallas kernels for 0%

profile of v1, /device:TPU:0, one launch (start us, length us, event | category | flops | bytes accessed | tf_op | source)
XLA Modules:
  0.0 659.8 jit_solution(10281514531315076193)
XLA Ops:
  11.9 67.9 %shard_map.229 = (bf16[2,8,2,48,768]{4,3,2,1,0:T(8,128)(2,1)}, bf16[2,8,2,48,768]{4,3,2,1,0:T(8,128)(2,1)}, bf16[8,2,2,96,768]{4,3,2,1,0:T(8,128)(2,1)}, bf16[2,2,8,96,768]{4,3,2,1,0:T(8,128)(2,1)}) custom-call(bf16[2,2,48,768]{3,2,1,0:T(8,128)(2,1)} %pad_maximum_fusion.2.refs_0_, bf16[2,2,48,768]{3,2,1,0:T(8,128)(2,1)} %pad_maximum_fusion.3.refs_1_, ...), custom_call_target="tpu_custom_call" | custom-call | tf_op jit(solution)/shard_map/pallas_call | solution.py:112
  89.9 8.5 %fusion.16 = (f32[2,12,256]{2,1,0:T(8,128)S(1)}, f32[2,256,12,256]{3,1,2,0:T(8,128)}) fusion(f32[2,256]{1,0:T(2,128)S(1)} %get-tuple-element.55, f32[2,256,12]{1,2,0:T(8,128)S(1)} %broadcast_multiply_fusion.3, f32[64,256]{1,0:T(8,128)S(1)} %copy-done, f32[2,256,12,64]{1,0,3,2:T(2,128)S(1)} %reshape.228), kind=kOutput, calls=%fused_computation.33 | convolution fusion | flops 1213065216 | bytes 7981056 | tf_op jit(solution)/shard_map/snhe,em->snhm/dot_general | solution.py:165
  111.9 14.0 %all-gather = bf16[8,96,4]{1,2,0:T(4,128)(2,1)S(1)} all-gather(bf16[1,96,4]{1,2,0:T(4,128)(2,1)S(1)} %maximum_bitcast_fusion), channel_id=1, replica_groups=mesh['seq'=4,'dp'=8] {'dp'}, dimensions={0}, use_global_device_ids=true | all-gather | bytes 6912 | tf_op jit(solution)/shard_map/all_gather | solution.py:256
  134.5 7.1 %fusion.32 = f32[2,256,12,256]{1,3,2,0:T(8,128)} fusion(f32[2,256,12,64]{1,0,3,2:T(2,128)S(1)} %reshape.229, f32[64,256]{1,0:T(8,128)S(1)} %copy-done), kind=kOutput, calls=%fused_computation.87 | convolution fusion | flops 1208352768 | bytes 7929856 | tf_op jit(solution)/shard_map/snhe,em->snhm/dot_general | solution.py:165
  141.6 31.1 %all-reduce.11.cloned.1.call-done = f32[2,12,256,65]{2,3,1,0:T(8,128)} async-done(((f32[2,12,256,65]{2,3,1,0:T(8,128)}), f32[2,12,256,65]{2,3,1,0:T(8,128)}) %all-reduce.11.cloned.1.call-update) | async-done | bytes 1597456 | tf_op jit(solution)/shard_map/psum | solution.py:177
  179.4 7.2 %fusion.68 = (bf16[2,256,12,64]{1,3,2,0:T(8,128)(2,1)S(1)}, f32[2,256,12,64]{1,3,2,0:T(8,128)}) fusion(f32[2,256,12]{1,2,0:T(8,128)S(1)} %bitcast.212, f32[2,256,12,256]{1,3,2,0:T(8,128)S(1)} %copy-done.1, f32[2,256,12]{1,2,0:T(8,128)S(1)} %broadcast_multiply_fusion.2, f32[2,12,256,65]{2,3,1,0:T(8,128)} %all-reduce.11.cloned.1.call-done), kind=kOutput, calls=%fused_computation.148 | convolution fusion | flops 1210318848 | bytes 10272768 | tf_op jit(solution)/shard_map/snhm,shme->snhe/dot_general | solution.py:190
  189.3 29.8 %multiply_convert_fusion = (bf16[512,3072]{1,0:T(8,128)(2,1)S(1)}, f32[512,3072]{1,0:T(8,128)}, f32[512,3072]{1,0:T(8,128)}) fusion(bf16[3072,768]{1,0:T(8,128)(2,1)S(1)} %bitcast.234, f32[512,768]{1,0:T(8,128)S(1)} %get-tuple-element.61, f32[768]{0:T(1024)S(1)} %get-tuple-element.30, f32[768]{0:T(1024)S(1)} %get-tuple-element.31, ...), kind=kOutput, calls=%fused_computation.6 | convolution fusion | flops 2520121344 | bytes 22030336 | tf_op jit(solution)/shard_map/dot_general | solution.py:274
  225.4 9.0 %add_convert_fusion = bf16[512,3072]{1,0:T(8,128)(2,1)} fusion(f32[512,3072]{1,0:T(8,128)} %get-tuple-element.47, f32[512,3072]{1,0:T(8,128)} %get-tuple-element.62, bf16[768,3072]{0,1:T(8,128)(2,1)S(1)} %bitcast.187, f32[512,768]{1,0:T(8,128)S(1)} %get-tuple-element.52), kind=kOutput, calls=%fused_computation.5 | convolution fusion | flops 2438332416 | bytes 22020096 | tf_op jit(solution)/shard_map/dot_general | solution.py:293
  247.1 10.2 %fusion.8 = f32[2,12,256,64]{2,3,1,0:T(8,128)S(1)} fusion(f32[2,256,12,256]{1,3,2,0:T(8,128)} %fusion.32, f32[2,256,12]{1,2,0:T(8,128)S(1)} %broadcast_multiply_fusion.2, f32[2,256,12,64]{1,0,3,2:T(2,128)} %reshape.236, f32[2,256,12]{1,2,0:T(8,128)S(1)} %bitcast.213), kind=kOutput, calls=%fused_computation.25 | convolution fusion | flops 1209925632 | bytes 9486336 | tf_op jit(solution)/shard_map/snhm,snhe->shme/dot_general | solution.py:208
  273.1 6.7 %copy.104 = bf16[768,3072]{0,1:T(8,128)(2,1)} copy(bf16[768,3072]{1,0:T(8,128)(2,1)} %convolution_convert_fusion.1) | data formatting | bytes 9437184
  281.2 9.5 %fusion.72 = (f32[2,256,12]{1,2,0:T(8,128)S(1)}, f32[2,256,12,256]{1,3,2,0:T(8,128)S(1)}) fusion(f32[2,256,12,256]{1,3,2,0:T(8,128)} %fusion.32, f32[2,256,12]{1,2,0:T(8,128)S(1)} %broadcast_multiply_fusion.2, f32[2,12,256]{2,1,0:T(8,128)S(1)} %copy.80, f32[2,256,12]{1,2,0:T(8,128)S(1)} %negate_divide_fusion, f32[2,256,12,64]{1,0,3,2:T(2,128)S(1)} %copy-done.9, ...), kind=kOutput, calls=%fused_computation.152 | convolution fusion | flops 1216210944 | bytes 15851520 | tf_op jit(solution)/shard_map/snhe,shme->snhm/dot_general | solution.py:205
  302.1 27.2 %all-reduce.13.cloned.1.call-done = f32[2,12,256,65]{2,3,1,0:T(8,128)} async-done(((f32[2,12,256,65]{2,3,1,0:T(8,128)}), f32[2,12,256,65]{2,3,1,0:T(8,128)}) %all-reduce.13.cloned.1.call-update) | async-done | bytes 1597456 | tf_op jit(solution)/shard_map/psum | solution.py:177
  330.2 7.1 %fusion.71 = (f32[2,256,12]{1,2,0:T(8,128)S(1)}, f32[2,256,12,256]{3,1,2,0:T(8,128)S(1)}) fusion(f32[2,256]{1,0:T(2,128)S(1)} %get-tuple-element.55, f32[2,256,12,256]{3,1,2,0:T(8,128)} %get-tuple-element.57, f32[2,256,12]{1,2,0:T(8,128)S(1)} %broadcast_multiply_fusion.3, f32[2,12,256]{2,1,0:T(8,128)S(1)} %copy.88, ...), kind=kOutput, calls=%fused_computation.151 | convolution fusion | flops 1215817728 | bytes 15017984 | tf_op jit(solution)/shard_map/snhe,shme->snhm/dot_general | solution.py:213
  347.4 9.0 %fusion.34 = bf16[2,256,12,64]{1,3,2,0:T(8,128)(2,1)S(1)} fusion(f32[2,256,12,256]{3,1,2,0:T(8,128)} %get-tuple-element.57, f32[2,256]{1,0:T(2,128)S(1)} %get-tuple-element.55, f32[2,256,12]{1,2,0:T(8,128)S(1)} %broadcast_multiply_fusion.3, f32[2,12,256,65]{2,3,1,0:T(8,128)S(1)} %copy-done.14), kind=kOutput, calls=%fused_computation.90 | convolution fusion | flops 1211498496 | bytes 8685568 | tf_op jit(solution)/shard_map/snhm,shme->snhe/dot_general | solution.py:216
  359.4 7.3 %convolution_convert_fusion = bf16[3072,768]{0,1:T(8,128)(2,1)} fusion(bf16[512,3072]{1,0:T(8,128)(2,1)} %copy-done.47, f32[512,768]{1,0:T(8,128)} %copy-done.19), kind=kOutput, calls=%fused_computation.22 | convolution fusion | flops 2418671616 | bytes 9437184 | tf_op jit(solution)/shard_map/dot_general | solution.py:158
  366.8 19.6 %reduce-scatter.19.cloned.1.call-done = bf16[384,768]{1,0:T(8,128)(2,1)} async-done(((bf16[3072,768]{1,0:T(8,128)(2,1)}), bf16[384,768]{1,0:T(8,128)(2,1)}) %reduce-scatter.19.cloned.1.call-update) | async-done | bytes 589840
  388.6 32.0 %reduce-scatter.9.cloned.1.call-done = bf16[768,96]{0,1:T(8,128)(2,1)} async-done(((bf16[768,768]{0,1:T(8,128)(2,1)}), bf16[768,96]{0,1:T(8,128)(2,1)}) %reduce-scatter.9.cloned.1.call-update) | async-done | bytes 147472 | tf_op jit(solution)/shard_map/reduce_scatter | solution.py:339
  420.6 33.5 %reduce-scatter.15.cloned.1.call-done = bf16[768,96]{0,1:T(8,128)(2,1)} async-done(((bf16[768,768]{0,1:T(8,128)(2,1)}), bf16[768,96]{0,1:T(8,128)(2,1)}) %reduce-scatter.15.cloned.1.call-update) | async-done | bytes 147472 | tf_op jit(solution)/shard_map/reduce_scatter | solution.py:342
  454.2 34.1 %reduce-scatter.11.cloned.1.call-done = bf16[768,96]{0,1:T(8,128)(2,1)} async-done(((bf16[768,768]{0,1:T(8,128)(2,1)}), bf16[768,96]{0,1:T(8,128)(2,1)}) %reduce-scatter.11.cloned.1.call-update) | async-done | bytes 147472 | tf_op jit(solution)/shard_map/reduce_scatter | solution.py:340
  488.2 33.4 %reduce-scatter.13.cloned.1.call-done = bf16[768,96]{0,1:T(8,128)(2,1)} async-done(((bf16[768,768]{0,1:T(8,128)(2,1)}), bf16[768,96]{0,1:T(8,128)(2,1)}) %reduce-scatter.13.cloned.1.call-update) | async-done | bytes 147472 | tf_op jit(solution)/shard_map/reduce_scatter | solution.py:341
  521.6 55.4 %reduce-scatter.17.cloned.1.call-done = bf16[3072,96]{0,1:T(8,128)(2,1)} async-done(((bf16[3072,768]{0,1:T(8,128)(2,1)}), bf16[3072,96]{0,1:T(8,128)(2,1)}) %reduce-scatter.17.cloned.1.call-update) | async-done | bytes 589840 | tf_op jit(solution)/shard_map/reduce_scatter | solution.py:344
  578.3 25.9 %all-reduce.4 = (bf16[768]{0:T(1024)(128)(2,1)S(1)}, bf16[768]{0:T(1024)(128)(2,1)S(1)}, bf16[768]{0:T(1024)(128)(2,1)S(1)}, bf16[768]{0:T(1024)(128)(2,1)S(1)}) all-reduce(f32[768]{0:T(1024)S(1)} %get-tuple-element.20, f32[768]{0:T(1024)S(1)} %get-tuple-element.25, ...), channel_id=8, replica_groups=mesh['seq'=4,'dp'=8] {'dp'}, use_global_device_ids=true, to_apply=%region_29.0.clone | all-reduce | flops 3072 | bytes 18432
  604.6 9.9 %all-reduce.5 = (bf16[96]{0:T(256)(128)(2,1)S(1)}, bf16[96]{0:T(256)(128)(2,1)S(1)}, bf16[96]{0:T(256)(128)(2,1)S(1)}, bf16[96]{0:T(256)(128)(2,1)S(1)}) all-reduce(bf16[96]{0:T(256)(128)(2,1)S(1)} %dynamic-slice.15, bf16[96]{0:T(256)(128)(2,1)S(1)} %dynamic-slice.14, ...), channel_id=1, replica_groups=mesh['seq'=4,'dp'=8] {'seq'}, use_global_device_ids=true, to_apply=%region_30.0 | all-reduce | flops 384 | bytes 1536 | tf_op jit(solution)/shard_map/psum | solution.py:368
  622.2 21.7 %all-reduce.15.cloned.1.call-done = (bf16[768,96]{0,1:T(8,128)(2,1)}, bf16[768,96]{0,1:T(8,128)(2,1)}, bf16[768,96]{0,1:T(8,128)(2,1)}, bf16[768,96]{0,1:T(8,128...) async-done(((bf16[768,96]{0,1:T(8,128)(2,1)}, bf16[768,96]{0,1:T(8,128)(2,1)}, bf16[768,96]{0,1:T(8,128)(2,1)}, bf16[768,96]{0,1:T(8,128)(2,1)}, ...) | async-done | bytes 1769488 | tf_op jit(solution)/shard_map/psum | solution.py:362
  (226 shorter events, 126.9 us)
Async XLA Ops:
  7.2 82.7 %copy-start = (f32[64,256]{1,0:T(8,128)S(1)}, f32[64,256]{1,0:T(8,128)}, u32[]{:S(2)}) copy-start(f32[64,256]{1,0:T(8,128)} %param.16) | copy-start | bytes 196612
  7.2 165.4 %all-reduce.11.cloned.1.call-start = ((), (), s32[]{:S(2)}) async-start(), calls=%async_computation.6 | async-start | bytes 3538944 | tf_op jit(solution)/shard_map/psum | solution.py:177
  83.9 14.5 %copy-start.15 = (bf16[1,8,2,48,768]{4,3,2,1,0:T(8,128)(2,1)}, bf16[1,8,2,48,768]{4,3,2,1,0:T(8,128)(2,1)S(1)}, u32[]{:S(2)}) copy-start(bf16[1,8,2,48,768]{4,3,2,1,0:T(8,128)(2,1)S(1)} %get-tuple-element.71) | copy-start | bytes 3538948
  106.3 222.9 %all-reduce.13.cloned.1.call-start = ((), (), s32[]{:S(2)}) async-start(), calls=%async_computation.7 | async-start | bytes 3538944 | tf_op jit(solution)/shard_map/psum | solution.py:177
  111.8 22.7 %copy-start.6 = (f32[2,256,12,64]{1,0,3,2:T(2,128)}, f32[2,256,12,64]{1,0,3,2:T(2,128)S(1)}, u32[]{:S(2)}) copy-start(f32[2,256,12,64]{1,0,3,2:T(2,128)S(1)} %reshape.229) | copy-start | bytes 4718596
  172.7 16.6 %slice-start.4 = ((s8[4718592]{0:T(1024)(128)(4,1)}), s8[4194304]{0:T(1024)(128)(4,1)S(1)}, s32[]{:S(2)}) async-start(s8[4718592]{0:T(1024)(128)(4,1)} %bitcast.232), calls=%async_computation.19 | async-start | bytes 8388608
  179.3 9.9 %slice-start.5 = ((s8[4718592]{0:T(1024)(128)(4,1)}), s8[524288]{0:T(1024)(128)(4,1)S(1)}, s32[]{:S(2)}) async-start(s8[4718592]{0:T(1024)(128)(4,1)} %bitcast.232), calls=%async_computation.20 | async-start | bytes 1048576
  188.0 31.1 %slice-start.2 = ((s8[4718592]{0:T(1024)(128)(4,1)}), s8[4194304]{0:T(1024)(128)(4,1)S(1)}, s32[]{:S(2)}) async-start(s8[4718592]{0:T(1024)(128)(4,1)} %bitcast.184), calls=%async_computation.17 | async-start | bytes 8388608
  188.9 50.5 %copy-start.12 = (f32[512,768]{1,0:T(8,128)}, f32[512,768]{1,0:T(8,128)S(1)}, u32[]{:S(2)}) copy-start(f32[512,768]{1,0:T(8,128)S(1)} %get-tuple-element.61) | copy-start | bytes 4718596
  189.3 29.9 %slice-start.3 = ((s8[4718592]{0:T(1024)(128)(4,1)}), s8[524288]{0:T(1024)(128)(4,1)S(1)}, s32[]{:S(2)}) async-start(s8[4718592]{0:T(1024)(128)(4,1)} %bitcast.184), calls=%async_computation.18 | async-start | bytes 1048576
  243.5 14.1 %slice-start = ((s8[6291456]{0:T(1024)(128)(4,1)}), s8[2097152]{0:T(1024)(128)(4,1)S(1)}, s32[]{:S(2)}) async-start(s8[6291456]{0:T(1024)(128)(4,1)} %bitcast.177), calls=%async_computation.15 | async-start | bytes 4194304
  247.1 10.2 %copy-start.8 = (f32[2,256,12,64]{1,0,3,2:T(2,128)S(1)}, f32[2,256,12,64]{1,0,3,2:T(2,128)}, u32[]{:S(2)}) copy-start(f32[2,256,12,64]{1,0,3,2:T(2,128)} %reshape.236) | copy-start | bytes 4718596
  247.1 10.2 %copy-start.11 = (f32[2,256,12,64]{1,3,2,0:T(8,128)S(1)}, f32[2,256,12,64]{1,3,2,0:T(8,128)}, u32[]{:S(2)}) copy-start(f32[2,256,12,64]{1,3,2,0:T(8,128)} %get-tuple-element.59) | copy-start | bytes 4718596
  247.1 10.5 %slice-start.1 = ((s8[6291456]{0:T(1024)(128)(4,1)}), s8[4194304]{0:T(1024)(128)(4,1)S(1)}, s32[]{:S(2)}) async-start(s8[6291456]{0:T(1024)(128)(4,1)} %bitcast.177), calls=%async_computation.16 | async-start | bytes 8388608
  265.1 121.4 %reduce-scatter.19.cloned.1.call-start = ((), (), s32[]{:S(2)}) async-start(), calls=%async_computation.13 | async-start | bytes 5308416
  279.8 140.9 %reduce-scatter.9.cloned.1.call-start = ((), (), s32[]{:S(2)}) async-start(), calls=%async_computation.8 | async-start | bytes 1327104 | tf_op jit(solution)/shard_map/reduce_scatter | solution.py:339
  281.2 9.6 %copy-start.7 = (f32[2,256,12,64]{1,0,3,2:T(2,128)S(1)}, f32[2,256,12,64]{1,0,3,2:T(2,128)}, u32[]{:S(2)}) copy-start(f32[2,256,12,64]{1,0,3,2:T(2,128)} %copy-done.6) | copy-start | bytes 4718596
  299.0 155.2 %reduce-scatter.15.cloned.1.call-start = ((), (), s32[]{:S(2)}) async-start(), calls=%async_computation.11 | async-start | bytes 1327104 | tf_op jit(solution)/shard_map/reduce_scatter | solution.py:342
  302.0 186.2 %reduce-scatter.11.cloned.1.call-start = ((), (), s32[]{:S(2)}) async-start(), calls=%async_computation.9 | async-start | bytes 1327104 | tf_op jit(solution)/shard_map/reduce_scatter | solution.py:340
  347.4 174.3 %reduce-scatter.13.cloned.1.call-start = ((), (), s32[]{:S(2)}) async-start(), calls=%async_computation.10 | async-start | bytes 1327104 | tf_op jit(solution)/shard_map/reduce_scatter | solution.py:341
  359.4 217.6 %reduce-scatter.17.cloned.1.call-start = ((), (), s32[]{:S(2)}) async-start(), calls=%async_computation.12 | async-start | bytes 5308416 | tf_op jit(solution)/shard_map/reduce_scatter | solution.py:344
  366.7 210.3 %copy-start.46 = (u32[32]{0:T(128)S(1)}, u32[32]{0:T(128)}, u32[]{:S(2)}) copy-start(u32[32]{0:T(128)} %constant.90) | copy-start | bytes 388
  366.8 249.8 %copy-start.24 = (bf16[96,8,2,256]{3,1,2,0:T(8,128)(2,1)S(1)}, bf16[96,8,2,256]{3,1,2,0:T(8,128)(2,1)}, u32[]{:S(2)}) copy-start(bf16[96,8,2,256]{3,1,2,0:T(8,128)(2,1)} %copy-done.23) | copy-start | bytes 2359300
  366.8 277.2 %all-reduce.15.cloned.1.call-start = ((), (), s32[]{:S(2)}) async-start(), calls=%async_computation.14 | async-start | bytes 3538944 | tf_op jit(solution)/shard_map/psum | solution.py:362
  (39 other events, 117.5 us)
Sparse Core Ops, SparseCore 0:
  106.5 66.1 all-reduce.10
  265.2 64.0 all-reduce.12
  331.6 54.8 reduce-scatter.18
  389.2 31.4 reduce-scatter.8
  422.8 31.3 reduce-scatter.14
  456.9 31.3 reduce-scatter.10
  490.5 31.0 reduce-scatter.12
  523.9 53.0 reduce-scatter.16
  580.8 63.0 all-reduce.14

commit v2 on v1

v2 whole, which is shorter than its diff:
```python
import functools
from functools import partial

import jax
import jax.numpy as jnp
from jax import lax
from jax.experimental import pallas as pl
from jax.experimental.pallas import tpu as pltpu
from jax.sharding import PartitionSpec as P

MESH = pl.DeviceIdType.MESH
bf, f32 = jnp.bfloat16, jnp.float32
HEAD = 64
EPS = 1e-12
FWD_STATE = f32


def coords():
    s, d = lax.axis_index("seq"), lax.axis_index("dp")
    return s // 2, s % 2, d // 2, d % 2

def dev(y, x, z, c):
    return (y * 2 + x, z * 2 + c)

def entry_barrier(peers):
    sem = pltpu.get_barrier_semaphore()
    for p in peers:
        pl.semaphore_signal(sem, inc=1, device_id=p, device_id_type=MESH)
    pl.semaphore_wait(sem, len(peers))

def piece(g, ref, d, y, x):
    if g < 2:  return ref.at[y, d, x]
    if g == 2: return ref.at[d, y, x]
    return ref.at[y, x, d]
def lpiece(g, ref, y, x):
    return ref.at[y, x]
def shard(g, ref, d):
    if g < 2:  return ref.at[:, d]
    if g == 2: return ref.at[d]
    return ref.at[:, :, d]

def ag_kernel(nz, *refs):
    loc, out, sems = refs[:4], refs[4:8], refs[8:]
    zs, zr, xs, xr, ys, yr, ds_, dr, ss, sr, ls = sems
    y, x, z, c = coords()
    ynb, xnb, sib = dev(1 - y, x, z, c), dev(y, 1 - x, z, c), dev(y, x, z, 1 - c)
    zpeer = [dev(y, x, (z + k) % nz, c) for k in range(1, nz)]
    entry_barrier([ynb, xnb, sib] + zpeer)
    half = loc[0].shape[-1] // 2
    H = (pl.ds(0, half), pl.ds(half, half))
    me = z * 2 + c
    started = []
    def rc(src, dst, ssem, rsem, to):
        cp = pltpu.make_async_remote_copy(src_ref=src, dst_ref=dst, send_sem=ssem, recv_sem=rsem, device_id=to, device_id_type=MESH)
        return cp
    def go(cp):
        cp.start(); started.append(cp)
    def recv(dst, ssem, rsem, to):
        rc(dst, dst, ssem, rsem, to).wait_recv()
    G = range(4)
    for g in G:
        for k in range(1, nz):
            go(rc(lpiece(g, loc[g], y, x), piece(g, out[g], me, y, x), zs.at[g, k-1], zr.at[g, k-1], zpeer[k-1]))
        go(rc(loc[g], shard(g, out[g], me), ss.at[g, 0], sr.at[g, 0], sib))
    lc = []
    for g in G:
        cp = pltpu.make_async_copy(loc[g], shard(g, out[g], me), ls.at[g]); cp.start(); lc.append(cp)
    def st1(g):
        for k in range(1, nz):
            d = ((z + nz - k) % nz) * 2 + c
            p = piece(g, out[g], d, y, x)
            recv(p, zs.at[g, k-1], zr.at[g, k-1], zpeer[k-1])
            go(rc(p, p, xs.at[g, k-1], xr.at[g, k-1], xnb))
            go(rc(p, p, ys.at[g, k-1], yr.at[g, k-1], ynb))
    def st2(g):
        for k in range(1, nz):
            d = ((z + nz - k) % nz) * 2 + c
            p = piece(g, out[g], d, y, 1 - x)
            recv(p, xs.at[g, k-1], xr.at[g, k-1], xnb)
            pa = p.at[:, H[0]]
            go(rc(pa, pa, ds_.at[g, k-1, 0], dr.at[g, k-1, 0], ynb))
            p = piece(g, out[g], d, 1 - y, x)
            recv(p, ys.at[g, k-1], yr.at[g, k-1], ynb)
            pb = p.at[:, H[1]]
            go(rc(pb, pb, ds_.at[g, k-1, 1], dr.at[g, k-1, 1], xnb))
    def st3(g):
        for k in range(1, nz):
            d = ((z + nz - k) % nz) * 2 + c
            p = piece(g, out[g], d, 1 - y, 1 - x)
            pa, pb = p.at[:, H[0]], p.at[:, H[1]]
            recv(pa, ds_.at[g, k-1, 0], dr.at[g, k-1, 0], ynb)
            recv(pb, ds_.at[g, k-1, 1], dr.at[g, k-1, 1], xnb)
            sh = shard(g, out[g], d)
            go(rc(sh, sh, ss.at[g, k], sr.at[g, k], sib))
    for t in range(6):
        if t < 4: st1(t)
        if 0 <= t - 1 < 4: st2(t - 1)
        if 0 <= t - 2 < 4: st3(t - 2)
    for g in G:
        for k in range(nz):
            d = ((z + nz - k) % nz) * 2 + (1 - c)
            sh = shard(g, out[g], d)
            recv(sh, ss.at[g, k], sr.at[g, k], sib)
    for cp in lc: cp.wait()
    for cp in started: cp.wait_send()

def gather_weights(kv, qo, win, wout, dp):
    nz = dp // 2
    D = kv.shape[-1]
    a, b, c_ = kv.shape[2], win.shape[2], wout.shape[2]
    shp = [(2, dp, 2, a, D), (2, dp, 2, a, D), (dp, 2, 2, b, D), (2, 2, dp, c_, D)]
    S = pltpu.SemaphoreType.DMA
    n = nz - 1
    hb = pl.BlockSpec(memory_space=pl.ANY)
    return pl.pallas_call(
        functools.partial(ag_kernel, nz),
        out_shape=[jax.ShapeDtypeStruct(s, bf) for s in shp],
        in_specs=[hb] * 4, out_specs=[hb] * 4,
        scratch_shapes=[S((4, n)), S((4, n)), S((4, n)), S((4, n)), S((4, n)), S((4, n)), S((4, n, 2)), S((4, n, 2)), S((4, nz)), S((4, nz)), S((4,))],
        compiler_params=pltpu.CompilerParams(collective_id=1, has_side_effects=True),
    )(kv, qo, win, wout)

def pack(wq, wk, wv, wo, win, wout):
    D = wq.shape[0]
    sh = wq.shape[1]
    t = jnp.transpose
    kv = jnp.stack([t(wk), t(wv)]).reshape(2, 2, sh // 2, D)
    qo = jnp.stack([t(wq), t(wo)]).reshape(2, 2, sh // 2, D)
    wi = t(win).reshape(2, 2, win.shape[1] // 4, D)
    ff = wout.shape[0]
    wu = t(wout.reshape(ff // D, D, sh), (0, 2, 1)).reshape(2, 2, sh, D)
    return kv, qo, wi, wu


def nn(a, b): return lax.dot_general(a, b, (((1,), (0,)), ((), ())), preferred_element_type=f32)
def nt(a, b): return lax.dot_general(a, b, (((1,), (1,)), ((), ())), preferred_element_type=f32)
def tn(a, b): return lax.dot_general(a, b, (((0,), (0,)), ((), ())), preferred_element_type=f32)

def ds(i, n): return pl.ds(pl.multiple_of(i * n, n), n)

def project(tok, w, dst):
    D = tok.shape[1]
    for n in range(D // 256):
        o = nt(tok[...], w[n * 256:(n + 1) * 256, :]).astype(bf)
        dst[2 * n] = o[:, :128]
        dst[2 * n + 1] = o[:, 128:]

def features(x, wf):
    xf = x.astype(f32)
    sq = xf * xf
    hi = sq.astype(bf)
    lo = (sq - hi.astype(f32)).astype(bf)
    return jnp.exp(nn(jnp.concatenate([x, x, hi, lo], 1), wf[...]))

def pair_mask(m):
    r = lax.broadcasted_iota(jnp.int32, (128, 2 * m), 0) < HEAD
    c = lax.broadcasted_iota(jnp.int32, (128, 2 * m), 1) < m
    return (r == c)

def compact(st, m):
    return jnp.concatenate([st[:HEAD, :m], st[HEAD:, m:]], 0)

def key_side(kp, vp, wf, vm, kf, st, kt, nseq, loc):
    P_ = kp.shape[0]
    M = wf.shape[1] // 2
    def body(p, _):
        f = features(kp[p], wf) * jnp.concatenate([vm[...]] * (2 * M // 128), 1)
        fb = f.astype(bf)
        kf[p] = fb
        for b in range(nseq):
            rows = slice(b * loc, (b + 1) * loc)
            st[b, p] = compact(tn(vp[p, rows, :], fb[rows]), M)
            kt[b, p] = jnp.broadcast_to(jnp.sum(f[rows], 0, keepdims=True), (8, 2 * M))
        return 0
    lax.fori_loop(0, P_, body, 0)

def query_side(qp, wf, qf):
    def body(p, _):
        qf[p] = features(qp[p], wf).astype(bf)
        return 0
    lax.fori_loop(0, qp.shape[0], body, 0)

def build_right(st, kt, right, m):
    mask = pair_mask(m)
    nseq, P_ = st.shape[:2]
    for b in range(nseq):
        def body(p, _):
            c = st[b, p].astype(f32)
            s = jnp.where(mask, jnp.concatenate([c, c], 1), 0.0)
            t = jnp.where(mask, jnp.broadcast_to(kt[b, p][:1], (128, 2 * m)), 0.0)
            right[b, p] = jnp.concatenate([s, t], 0).astype(bf)
            return 0
        lax.fori_loop(0, P_, body, 0)

def mix_forward(qf, right, ctx, den, ctxb, nseq, loc):
    def body(p, _):
        for b in range(nseq):
            rows = slice(b * loc, (b + 1) * loc)
            o = nt(qf[p, rows, :], right[b, p])
            d = o[:, 128:]
            c = o[:, :128] / d
            ctx[p, rows, :] = c
            den[p, rows, :] = d
            ctxb[rows, ds(p, 128)] = c.astype(bf)
        return 0
    lax.fori_loop(0, qf.shape[0], body, 0)

def mean(a): return jnp.mean(a, -1, keepdims=True)

def attend_out(ctxb, wo, tok, vec, n1, inv1, hlow, resid):
    T, D = tok.shape
    for n in range(D // 256):
        resid[:, n * 256:(n + 1) * 256] = nt(ctxb[...], wo[n * 256:(n + 1) * 256, :])
    R = 64
    def body(i, _):
        r = ds(i, R)
        x = tok[r, :].astype(f32) + resid[r, :]
        cen = x - mean(x)
        inv = lax.rsqrt(mean(cen * cen) + EPS)
        n = cen * inv
        n1[r, :] = n
        inv1[r, :] = jnp.broadcast_to(inv, (R, 128))
        hlow[r, :] = (n * vec[0:1, :] + vec[1:2, :]).astype(bf)
        return 0
    lax.fori_loop(0, T // R, body, 0)

def ffn_chunk(j, hlow, win, wout, act, gp, acc, first):
    D = hlow.shape[1]
    C = act.shape[2]
    per = D // C
    pre = nt(hlow[...], win[ds(j, C), :])
    cdf = 0.5 * (1.0 + lax.erf(pre * 0.7071067811865476))
    a = (pre * cdf).astype(bf)
    act[j] = a
    gp[j] = (cdf + pre * (jnp.exp(-0.5 * pre * pre) * 0.3989422804014327)).astype(bf)
    o = nt(a, wout[j // per, :, ds(lax.rem(j, per), C)])
    if first: acc[...] = o
    else: acc[...] += o

def ffn_forward(hlow, win, wout, act, gp, acc):
    ffn_chunk(0, hlow, win, wout, act, gp, acc, True)
    def body(j, _):
        ffn_chunk(j, hlow, win, wout, act, gp, acc, False)
        return 0
    lax.fori_loop(1, act.shape[0], body, 0)

def fold8(a):
    return jnp.sum(a.reshape(a.shape[0] // 8, 8, a.shape[1]), 0)

def norm_pull(g, n, inv, gain):
    e = g * gain
    return inv * (e - mean(e) - n * mean(e * n))

def second_norm(acc, n1, vec, vm, cot, out, gr2, gffn, sums):
    T, D = acc.shape
    R = 64
    sums[0] = jnp.zeros((8, D), f32)
    sums[1] = jnp.zeros((8, D), f32)
    def body(i, _):
        r = ds(i, R)
        x = n1[r, :] * vec[0:1, :] + vec[1:2, :] + acc[r, :]
        cen = x - mean(x)
        inv = lax.rsqrt(mean(cen * cen) + EPS)
        n = cen * inv
        v = vm[r, :]
        vv = jnp.concatenate([v] * (D // 128), 1)
        out[r, :] = ((n * vec[2:3, :] + vec[3:4, :]) * vv).astype(bf)
        gy = cot[r, :].astype(f32) * vv
        sums[0] += fold8(gy * n)
        sums[1] += fold8(gy)
        g = norm_pull(gy, n, inv, vec[2:3, :])
        gr2[r, :] = g
        gffn[r, :] = g.astype(bf)
        return 0
    lax.fori_loop(0, T // R, body, 0)

def ffn_backward(j, gffn, gffn_t, hlow, win, wout, act, gp, gwin, gwout, gh, first):
    D = gffn.shape[1]
    C = act.shape[2]
    per = D // C
    jj, cc = j // per, lax.rem(j, per)
    ga = nn(gffn[...], wout[jj, :, ds(cc, C)])
    gpre = (ga * gp[j].astype(f32)).astype(bf)
    gwout[jj, :, ds(cc, C)] = nn(gffn_t[...], act[j]).astype(bf)
    gwin[ds(j, C), :] = tn(gpre, hlow[...]).astype(bf)
    o = nn(gpre, win[ds(j, C), :])
    if first: gh[...] = o
    else: gh[...] += o

def first_norm_back(gh, gr2, n1, inv1, vec, gr1, gattn, sums):
    T, D = gh.shape
    R = 64
    sums[2] = jnp.zeros((8, D), f32)
    sums[3] = jnp.zeros((8, D), f32)
    def body(i, _):
        r = ds(i, R)
        g = gr2[r, :] + gh[r, :]
        n = n1[r, :]
        sums[2] += fold8(g * n)
        sums[3] += fold8(g)
        o = norm_pull(g, n, inv1[r, :][:, :1], vec[0:1, :])
        gr1[r, :] = o
        gattn[r, :] = o.astype(bf)
        return 0
    lax.fori_loop(0, T // R, body, 0)

def weight_grad(gt, x, dst):
    D = x.shape[1]
    for n in range(D // 256):
        dst[n * 256:(n + 1) * 256, :] = nn(gt[n * 256:(n + 1) * 256, :], x[...]).astype(bf)

def weight_grad_pairs(gp_, x, dst):
    P_ = gp_.shape[0]
    for n in range(P_ // 2):
        g = jnp.concatenate([gp_[2 * n], gp_[2 * n + 1]], 1)
        dst[n * 256:(n + 1) * 256, :] = tn(g, x[...]).astype(bf)

def mix_back_query(gattn, wo, qp, qf, right, ctx, den, fbm, gst, gkt, gq, nseq, loc):
    M = qf.shape[2] // 2
    mask = pair_mask(M)
    def body(p, _):
        gc = nn(gattn[...], wo[:, ds(p, 128)]).astype(bf).astype(f32)
        gn = gc / den[p]
        t = -gn * ctx[p]
        g = jnp.concatenate([gn, t], 1).astype(bf)
        for b in range(nseq):
            rows = slice(b * loc, (b + 1) * loc)
            q = qf[p, rows, :]
            s = tn(g[rows], q)
            gst[b, p] = compact(s[:128], M)
            gkt[b, p] = jnp.broadcast_to(jnp.sum(jnp.where(mask, s[128:], 0.0), 0, keepdims=True), (8, 2 * M))
            pr = (nn(g[rows], right[b, p]) * q.astype(f32)).astype(bf)
            o = nn(pr, fbm[...])
            gq[p, rows, :] = (o[:, :128] - 0.125 * qp[p, rows, :].astype(f32) * o[:, 128:]).astype(bf)
        return 0
    lax.fori_loop(0, qf.shape[0], body, 0)

def mix_back_key(kp, vp, kf, gst, gkt, fbm, gk, gv, nseq, loc):
    M = kf.shape[2] // 2
    mask = pair_mask(M)
    def body(p, _):
        for b in range(nseq):
            rows = slice(b * loc, (b + 1) * loc)
            c = gst[b, p].astype(f32)
            s = jnp.where(mask, jnp.concatenate([c, c], 1), 0.0).astype(bf)
            k = kf[p, rows, :]
            pr = ((nn(vp[p, rows, :], s) + gkt[b, p][:1]) * k.astype(f32)).astype(bf)
            o = nn(pr, fbm[...])
            gk[p, rows, :] = (o[:, :128] - 0.125 * kp[p, rows, :].astype(f32) * o[:, 128:]).astype(bf)
            gv[p, rows, :] = nt(k, s).astype(bf)
        return 0
    lax.fori_loop(0, kf.shape[0], body, 0)

def join(g):
    return jnp.concatenate([g[i] for i in range(g.shape[0])], 1)

def token_grad(gr1, gq, gk, gv, wq, wk, wv, dst):
    D = gr1.shape[1]
    for n in range(D // 256):
        c = slice(n * 256, (n + 1) * 256)
        dst[:, c] = gr1[:, c] + (nn(join(gq), wq[:, c]) + nn(join(gk), wk[:, c]) + nn(join(gv), wv[:, c]))

def mixer_constants(rf):
    M = rf.shape[1]
    c = HEAD ** (-0.25)
    w = rf * c
    hi = w.astype(bf)
    lo = (w - hi.astype(f32)).astype(bf)
    z = jnp.zeros((HEAD, M), bf)
    def bd(a): return jnp.concatenate([jnp.concatenate([a, z], 1), jnp.concatenate([z, a], 1)], 0)
    s = jnp.full((HEAD, M), -0.0625, bf)
    wf = jnp.concatenate([bd(hi), bd(lo), bd(s), bd(s)], 0)
    fbm = jnp.concatenate([bd(hi), bd(jnp.ones((HEAD, M), bf))], 0).T
    return wf, fbm


class Reduce:
    def __init__(self, nz, grads, scratch, sems, fins):
        self.nz, self.grads, self.fins = nz, grads, fins
        G = len(grads)
        self.sib, self.a1, self.b1, self.a2, self.b2, self.tot, self.zrec = (scratch[i * G:(i + 1) * G] for i in range(7))
        self.sem = sems
        self.started = []
        y, x, z, c = self.pos = coords()
        self.ynb, self.xnb, self.sibdev = dev(1 - y, x, z, c), dev(y, 1 - x, z, c), dev(y, x, z, 1 - c)
        self.diag = dev(1 - y, 1 - x, z, c)
        self.zpeer = [dev(y, x, (z + k) % nz, c) for k in range(1, nz)]

    def peers(self):
        return [self.ynb, self.xnb, self.sibdev, self.diag] + self.zpeer

    def _cp(self, src, dst, g, i, to):
        s, r = self.sem
        return pltpu.make_async_remote_copy(src_ref=src, dst_ref=dst, send_sem=s.at[g, i], recv_sem=r.at[g, i], device_id=to, device_id_type=MESH)

    def _go(self, src, dst, g, i, to):
        cp = self._cp(src, dst, g, i, to)
        cp.start()
        self.started.append(cp)

    def _recv(self, dst, g, i, to):
        self._cp(dst, dst, g, i, to).wait_recv()

    def s0(self, g):
        y, x, z, c = self.pos
        for k in range(self.nz):
            self._go(shard(g, self.grads[g], k * 2 + 1 - c), self.sib[g].at[k], g, k, self.sibdev)

    def s1(self, g):
        y, x, z, c = self.pos
        nz, gr, sib = self.nz, self.grads[g], self.sib[g]
        half = gr.shape[-1] // 2
        A, B = pl.ds(0, half), pl.ds(half, half)
        for k in range(nz):
            self._recv(sib.at[k], g, k, self.sibdev)
        def body(i, _):
            k, q = i // 4, lax.rem(i, 4)
            qy, qx = q // 2, lax.rem(q, 2)
            sib[k, qy, qx] = (sib[k, qy, qx].astype(f32) + piece(g, gr, k * 2 + c, qy, qx)[...].astype(f32)).astype(bf)
            return 0
        lax.fori_loop(0, nz * 4, body, 0)
        self._go(sib.at[:, :, 1 - x, :, A], self.a1[g], g, nz, self.xnb)
        self._go(sib.at[:, 1 - y, :, :, B], self.b1[g], g, nz + 1, self.ynb)

    def s2(self, g):
        y, x, z, c = self.pos
        nz, sib = self.nz, self.sib[g]
        a1, b1 = self.a1[g], self.b1[g]
        half = a1.shape[-1]
        self._recv(a1, g, nz, self.xnb)
        self._recv(b1, g, nz + 1, self.ynb)
        def body(i, _):
            k, j = i // 2, lax.rem(i, 2)
            a1[k, j] = (a1[k, j].astype(f32) + sib[k, j, x, :, :half].astype(f32)).astype(bf)
            b1[k, j] = (b1[k, j].astype(f32) + sib[k, y, j, :, half:].astype(f32)).astype(bf)
            return 0
        lax.fori_loop(0, nz * 2, body, 0)
        self._go(a1.at[:, 1 - y], self.a2[g], g, nz + 2, self.ynb)
        self._go(b1.at[:, 1 - x], self.b2[g], g, nz + 3, self.xnb)

    def s3(self, g):
        y, x, z, c = self.pos
        nz = self.nz
        a1, b1, a2, b2, tot = self.a1[g], self.b1[g], self.a2[g], self.b2[g], self.tot[g]
        half = a1.shape[-1]
        self._recv(a2, g, nz + 2, self.ynb)
        self._recv(b2, g, nz + 3, self.xnb)
        def body(k, _):
            tot[k, :, :half] = (a1[k, y].astype(f32) + a2[k].astype(f32)).astype(bf)
            tot[k, :, half:] = (b1[k, x].astype(f32) + b2[k].astype(f32)).astype(bf)
            return 0
        lax.fori_loop(0, nz, body, 0)
        for k in range(1, nz):
            self._go(tot.at[(z + k) % nz], self.zrec[g].at[k - 1], g, nz + 3 + k, self.zpeer[k - 1])

    def s4(self, g):
        y, x, z, c = self.pos
        nz, zrec, fin = self.nz, self.zrec[g], self.fins[g]
        for k in range(1, nz):
            self._recv(zrec.at[k - 1], g, nz + 3 + k, self.zpeer[k - 1])
        t = self.tot[g][z].astype(f32)
        for k in range(1, nz):
            t = t + zrec[k - 1].astype(f32)
        mine = fin.at[y, x]
        fin[y, x] = t.astype(bf)
        for i, to in enumerate((self.xnb, self.ynb, self.diag)):
            self._go(mine, mine, g, 2 * nz + 3 + i, to)

    def s5(self, g):
        y, x, z, c = self.pos
        nz, fin = self.nz, self.fins[g]
        for i, (py, px, to) in enumerate(((y, 1 - x, self.xnb), (1 - y, x, self.ynb), (1 - y, 1 - x, self.diag))):
            self._recv(fin.at[py, px], g, 2 * nz + 3 + i, to)

    def finish(self):
        for cp in self.started:
            cp.wait_send()

def grad_shapes(dp, D, a, b, c_):
    return [(2, dp, 2, a, D), (2, dp, 2, a, D), (dp, 2, 2, b, D), (2, 2, dp, c_, D)]

def reduce_scratch(dp, D, a, b, c_):
    nz, h = dp // 2, D // 2
    rows = (a, a, b, c_)
    out = []
    for shp in (lambda r: (nz, 2, 2, r, D), lambda r: (nz, 2, r, h), lambda r: (nz, 2, r, h), lambda r: (nz, r, h),
                lambda r: (nz, r, h), lambda r: (nz, r, D), lambda r: (nz - 1, r, D)):
        out += [pltpu.VMEM(shp(r), bf) for r in rows]
    return out

def rs_kernel(nz, *refs):
    grads, fins = refs[:4], refs[4:8]
    scratch, sems = refs[8:8 + 28], refs[36:38]
    R = Reduce(nz, grads, scratch, sems, fins)
    entry_barrier(R.peers())
    for g in range(4): R.s0(g)
    stages = (R.s1, R.s2, R.s3, R.s4, R.s5)
    for t in range(4 + len(stages) - 1):
        for i, st in enumerate(stages):
            if 0 <= t - i < 4: st(t - i)
    R.finish()

def reduce_grads(grads, dp):
    D = grads[0].shape[-1]
    a, b, c_ = grads[0].shape[3], grads[2].shape[3], grads[3].shape[3]
    VM = pl.BlockSpec(memory_space=pltpu.VMEM)
    S = pltpu.SemaphoreType.DMA
    nz = dp // 2
    return pl.pallas_call(
        functools.partial(rs_kernel, nz),
        out_shape=[jax.ShapeDtypeStruct((2, 2, r, D), bf) for r in (a, a, b, c_)],
        in_specs=[VM] * 4, out_specs=[VM] * 4,
        scratch_shapes=reduce_scratch(dp, D, a, b, c_) + [S((4, 2 * nz + 6)), S((4, 2 * nz + 6))],
        compiler_params=pltpu.CompilerParams(collective_id=2, has_side_effects=True, vmem_limit_bytes=67043328),
    )(*grads)

def state_kernel(cid_dtype, st, kt, sto, kto, sb, srec, krec, ks, sems, semr):
    y, x, z, c = coords()
    peers = [dev(y, 1 - x, z, c), dev(1 - y, x, z, c), dev(1 - y, 1 - x, z, c)]
    sid = [y * 2 + 1 - x, (1 - y) * 2 + x, (1 - y) * 2 + 1 - x]
    me = y * 2 + x
    entry_barrier(peers)
    sb[...] = st[...].astype(cid_dtype)
    def cp(src, dst, i, k):
        return pltpu.make_async_remote_copy(src_ref=src, dst_ref=dst, send_sem=sems.at[i, k], recv_sem=semr.at[i, k], device_id=peers[k], device_id_type=MESH)
    out = []
    for k in range(3):
        a = cp(sb.at[sid[k]], srec.at[k], 0, k); a.start()
        b = cp(kt.at[sid[k]], krec.at[k], 1, k); b.start()
        out += [a, b]
    for k in range(3):
        cp(srec.at[k], srec.at[k], 0, k).wait_recv()
        cp(krec.at[k], krec.at[k], 1, k).wait_recv()
    t, u = st[me], kt[me]
    for k in range(3):
        t = t + srec[k].astype(f32)
        u = u + krec[k]
    sto[me] = t.astype(cid_dtype)
    kto[me] = u
    for k in range(3):
        a = cp(sto.at[me], sto.at[me], 2, k); a.start()
        b = cp(kto.at[me], kto.at[me], 3, k); b.start()
        out += [a, b]
    for k in range(3):
        cp(sto.at[sid[k]], sto.at[sid[k]], 2, k).wait_recv()
        cp(kto.at[sid[k]], kto.at[sid[k]], 3, k).wait_recv()
    for a in out: a.wait_send()

def sum_state(st, kt, cid, dtype):
    ns, P_, _, M = st.shape
    n = ns * P_ // 4
    st4, kt4 = st.reshape(4, n, 128, M), kt.reshape(4, n, 8, 2 * M)
    VM = pl.BlockSpec(memory_space=pltpu.VMEM)
    S = pltpu.SemaphoreType.DMA
    sto, kto = pl.pallas_call(
        functools.partial(state_kernel, dtype),
        out_shape=[jax.ShapeDtypeStruct(st4.shape, dtype), jax.ShapeDtypeStruct(kt4.shape, f32)],
        in_specs=[VM] * 2, out_specs=[VM] * 2,
        scratch_shapes=[pltpu.VMEM(st4.shape, dtype), pltpu.VMEM((3, n, 128, M), dtype), pltpu.VMEM((3, n, 8, 2 * M), f32), pltpu.VMEM((8, 128), f32), S((4, 3)), S((4, 3))],
        compiler_params=pltpu.CompilerParams(collective_id=cid, has_side_effects=True, vmem_limit_bytes=33554432),
    )(st4, kt4)
    return sto.reshape(st.shape), kto.reshape(kt.shape)


VM = pl.BlockSpec(memory_space=pltpu.VMEM)
ALLV = 67043328
COLS = 256


def call(body, ins, outs, scratch=(), name=None):
    return pl.pallas_call(
        body,
        out_shape=[jax.ShapeDtypeStruct(s, d) for s, d in outs],
        in_specs=[VM] * len(ins),
        out_specs=[VM] * len(outs),
        scratch_shapes=list(scratch),
        name=name,
        compiler_params=pltpu.CompilerParams(vmem_limit_bytes=ALLV),
    )(*ins)


def key_query_kernel(ns, loc, tok, kvw, qow, wf, vm, kp, vp, qp, kf, qf, st, kt):
    project(tok, kvw.at[0], kp)
    project(tok, kvw.at[1], vp)
    project(tok, qow.at[0], qp)
    key_side(kp, vp, wf, vm, kf, st, kt, ns, loc)
    query_side(qp, wf, qf)


def forward_kernel(ns, loc, tok, cot, qow, win, wout, vec, vm, qf, st, kt, ctx, den, ctxb, right, n1, inv1, hlow, act, gp, out, gr2, gffn, sums, acc):
    build_right(st, kt, right, qf.shape[2] // 2)
    mix_forward(qf, right, ctx, den, ctxb, ns, loc)
    attend_out(ctxb, qow.at[1], tok, vec, n1, inv1, hlow, acc)
    ffn_forward(hlow, win, wout, act, gp, acc)
    second_norm(acc, n1, vec, vm, cot, out, gr2, gffn, sums)


def backward_kernel(ns, loc, gffn, gr2, hlow, win, wout, act, gp, n1, inv1, vec, qow, ctxb, ctx, den, qp, qf, right, fbm, tok, gwin, gwout, gqo, gr1, gq, gst, gkt, sums, gh, gattn, tr):
    tr[...] = gffn[...].T
    ffn_backward(0, gffn, tr, hlow, win, wout, act, gp, gwin, gwout, gh, True)

    def body(j, _):
        ffn_backward(j, gffn, tr, hlow, win, wout, act, gp, gwin, gwout, gh, False)
        return 0

    lax.fori_loop(1, act.shape[0], body, 0)
    first_norm_back(gh, gr2, n1, inv1, vec, gr1, gattn, sums)
    tr[...] = gattn[...].T
    weight_grad(tr, ctxb, gqo.at[1])
    mix_back_query(gattn, qow.at[1], qp, qf, right, ctx, den, fbm, gst, gkt, gq, ns, loc)
    weight_grad_pairs(gq, tok, gqo.at[0])


def last_kernel(ns, loc, kp, vp, kf, gst, gkt, fbm, gr1, gq, kvw, qow, tok, gkv, tg, gk, gv):
    mix_back_key(kp, vp, kf, gst, gkt, fbm, gk, gv, ns, loc)
    weight_grad_pairs(gk, tok, gkv.at[0])
    weight_grad_pairs(gv, tok, gkv.at[1])
    token_grad(gr1, gq, gk, gv, qow.at[0], kvw.at[0], kvw.at[1], tg)


def shards(tokens, lengths, random_features, w_query, w_key, w_value, w_output, w_in, w_out, ln1_gain, ln1_bias, ln2_gain, ln2_bias, cotangent):
    ns, loc, D = tokens.shape
    T = ns * loc
    dp, parts = lax.axis_size("dp"), lax.axis_size("seq")
    part = w_query.shape[1]
    FF = w_out.shape[0]
    M = random_features.shape[1]
    P_ = D // 128
    fast = parts == 4 and dp == 8 and part % 32 == 0 and D == part * dp
    wf, fbm = mixer_constants(random_features)
    pos = lax.axis_index("seq") * loc + jnp.arange(loc, dtype=jnp.int32)
    valid = (pos[None, :] < lengths[:, None]).astype(f32).reshape(T, 1)
    vm = jnp.broadcast_to(valid, (T, 128))
    tok, cot = tokens.reshape(T, D), cotangent.reshape(T, D)
    vec = lax.all_gather(jnp.stack([ln1_gain, ln1_bias, ln2_gain, ln2_bias]), "dp", axis=1, tiled=True)
    vec = jnp.pad(vec.astype(f32), ((0, 4), (0, 0)))
    if fast:
        kvw, qow, win, wout = gather_weights(*pack(w_query, w_key, w_value, w_output, w_in, w_out), dp)
    else:
        def full(w):
            return lax.all_gather(w, "dp", axis=1, tiled=True).T
        kvw, qow = jnp.stack([full(w_key), full(w_value)]), jnp.stack([full(w_query), full(w_output)])
        win = full(w_in)
        wout = jnp.transpose(full(w_out).reshape(D, FF // D, D), (1, 0, 2))
    kvw, qow, win, wout = kvw.reshape(2, D, D), qow.reshape(2, D, D), win.reshape(FF, D), wout.reshape(FF // D, D, D)
    pm, pf, stt, ktt = (P_, T, 128), (P_, T, 2 * M), (ns, P_, 128, M), (ns, P_, 8, 2 * M)
    kp, vp, qp, kf, qf, st, kt = call(
        partial(key_query_kernel, ns, loc), (tok, kvw, qow, wf, vm),
        [(pm, bf)] * 3 + [(pf, bf)] * 2 + [(stt, f32), (ktt, f32)], name="key_query")
    if fast:
        st, kt = sum_state(st, kt, 3, FWD_STATE)
    else:
        st, kt = lax.psum((st, kt), "seq")
    ch = (FF // COLS, T, COLS)
    ctx, den, ctxb, right, n1, inv1, hlow, act, gp, out, gr2, gffn, sums = call(
        partial(forward_kernel, ns, loc), (tok, cot, qow, win, wout, vec, vm, qf, st, kt),
        [(pm, f32), (pm, f32), ((T, D), bf), ((ns, P_, 256, 2 * M), bf), ((T, D), f32), ((T, 128), f32), ((T, D), bf), (ch, bf), (ch, bf), ((T, D), bf), ((T, D), f32), ((T, D), bf), ((4, 8, D), f32)],
        [pltpu.VMEM((T, D), f32)], name="forward")
    gwin, gwout, gqo, gr1, gq, gst, gkt, sums2 = call(
        partial(backward_kernel, ns, loc), (gffn, gr2, hlow, win, wout, act, gp, n1, inv1, vec, qow, ctxb, ctx, den, qp, qf, right, fbm, tok),
        [((FF, D), bf), ((FF // D, D, D), bf), ((2, D, D), bf), ((T, D), f32), (pm, bf), (stt, f32), (ktt, f32), ((4, 8, D), f32)],
        [pltpu.VMEM((T, D), f32), pltpu.VMEM((T, D), bf), pltpu.VMEM((D, T), bf)], name="backward")
    if fast:
        gst, gkt = sum_state(gst, gkt, 4, bf)
    else:
        gst, gkt = lax.psum((gst, gkt), "seq")
    gkv, tg = call(
        partial(last_kernel, ns, loc), (kp, vp, kf, gst, gkt, fbm, gr1, gq, kvw, qow, tok),
        [((2, D, D), bf), ((T, D), f32)], [pltpu.VMEM(pm, bf), pltpu.VMEM(pm, bf)], name="last")
    small = jnp.sum(jnp.concatenate([sums2[2:], sums[:2]]), 1)
    small = lax.psum(small, ("seq", "dp"))
    small = lax.dynamic_slice_in_dim(small, lax.axis_index("dp") * part, part, 1)
    if fast:
        shp = grad_shapes(dp, D, part // 2, FF // dp // 4, part)
        kvg, qog, wig, wug = reduce_grads([g.reshape(s) for g, s in zip((gkv, gqo, gwin, gwout), shp)], dp)
        wk_g, wv_g, wq_g, wo_g = kvg[0].reshape(part, D).T, kvg[1].reshape(part, D).T, qog[0].reshape(part, D).T, qog[1].reshape(part, D).T
        wi_g = wig.reshape(FF // dp, D).T
        wu_g = jnp.transpose(wug.reshape(FF // D, part, D), (0, 2, 1)).reshape(FF, part)
        grads = (wq_g, wk_g, wv_g, wo_g, wi_g, wu_g)
    else:
        whole = (gqo[0].T, gkv[0].T, gkv[1].T, gqo[1].T, gwin.T, jnp.transpose(gwout, (0, 2, 1)).reshape(FF, D))
        grads = tuple(lax.psum(lax.psum_scatter(g, "dp", scatter_dimension=1, tiled=True), "seq") for g in whole)
    return (out.reshape(tokens.shape), tg.reshape(tokens.shape), *(g.astype(f32) for g in grads), small[0], small[1], small[2], small[3])


def solution(mesh):
    rows, cols, vecs = P("dp", "seq", None), P(None, "dp"), P("dp")
    return jax.shard_map(
        shards,
        mesh=mesh,
        in_specs=(rows, vecs, P(), *([cols] * 6), *([vecs] * 4), rows),
        out_specs=(rows, rows, *([cols] * 6), *([vecs] * 4)),
        check_vma=False,
    )
```

time: 669 us -> 415 us (0.62); the launches traced: 660 us -> 414 us
  waiting for transfers between devices: 288 us -> 0 us
  Pallas kernels: 67.9 us -> 326 us
  matrix products: 168 us -> 0 us
  local copies, waits for them, and re-layouts: 49.1 us -> 19.9 us
  between operations: 15.8 us -> 0.9 us
  other arithmetic: 21 us -> 7.97 us
  blocking collectives: 49.9 us -> 59.4 us
    pallas_call x0 -> x7, Pallas kernels: none -> 260 us  [the longest x4 99.6 us: call(): pl.pallas_call(body, out_shape=[jax.ShapeDtypeStruct(s, d) for s, d in ou...]
    reduce_scatter x5 -> x0, waiting for transfers between devices: 188 us -> none  [the longest x1 55.4 us: shards(): lax.psum_scatter(grad_wout.astype(jnp.bfloat16), 'dp', scatter_dimension=...]
    dot_general x30 -> x0, matrix products: 168 us -> none  [the longest x1 29.8 us: shards(): lax.dot_general(hidden_low, win_full, (((1,), (1,)), ((), ())), preferred...]
    psum x3 -> x0, waiting for transfers between devices: 80 us -> none  [the longest x2 58.2 us: seq_sum(): lax.psum(jnp.concatenate([key_state, key_total[..., None]], -1), 'seq')]
    psum x1, blocking collectives: 9.92 us -> 46 us  [shards(): small = lax.psum(small, ('seq', 'dp'))]
    unnamed x1 -> x0, blocking collectives: 25.9 us -> none
    unnamed x10 -> x0, waiting for transfers between devices: 19.8 us -> none
    unnamed x122 -> x45, local copies, waits for them, and re-layouts: 19.9 us -> 9.15 us
  transfers between devices with their start and end apart: 9 -> 0, of which waited for: 9 -> 0; matrix products, arithmetic and copies ran while one was open for 15% -> 0% of each run, Pallas kernels for 0% -> 0%
where the time goes in v2:
time: 415 us; the launch traced here: 414 us
  Pallas kernels  326 us (79%)
  blocking collectives  59.4 us (14%)
  local copies, waits for them, and re-layouts  19.9 us (5%)
  other arithmetic  7.97 us (2%)
    pallas_call x4, Pallas kernels, call(): pl.pallas_call(body, out_shape=[jax.ShapeDtypeStruct(s, d) for s, d in ou...  99.6 us
    pallas_call x1, Pallas kernels, reduce_grads(): pl.pallas_call(functools.partial(rs_kernel, nz), out_shape=[jax.ShapeDtyp...  91.5 us
    pallas_call x2, Pallas kernels, sum_state(): pl.pallas_call(functools.partial(state_kernel, dtype), out_shape=[jax.Sha...  68.9 us
    pallas_call x1, Pallas kernels, gather_weights(): pl.pallas_call(functools.partial(ag_kernel, nz), out_shape=[jax.ShapeDtyp...  66 us
    psum x1, blocking collectives, shards(): small = lax.psum(small, ('seq', 'dp'))  46 us
    all_gather x1, blocking collectives, shards(): lax.all_gather(jnp.stack([ln1_gain, ln1_bias, ln2_gain, ln2_bias]), 'dp',...  13.5 us
    unnamed x45, local copies, waits for them, and re-layouts  9.15 us

profile of v2, /device:TPU:0, one launch (start us, length us, event | category | flops | bytes accessed | tf_op | source)
XLA Modules:
  0.0 414.2 jit_solution(16591943311562372842)
XLA Ops:
  2.3 13.5 %all-gather = bf16[8,96,4]{1,2,0:T(4,128)(2,1)S(1)} all-gather(bf16[1,96,4]{1,2,0:T(4,128)(2,1)S(1)} %maximum_bitcast_fusion.1), channel_id=1, replica_groups=mesh['seq'=4,'dp'=8] {'dp'}, dimensions={0}, use_global_device_ids=true | all-gather | bytes 6912 | tf_op jit(solution)/shard_map/all_gather | solution.py:635
  16.4 0.9 copy.36
  18.3 0.9 maximum_bitcast_fusion.fbm
  19.8 1.0 copy.37.wf
  20.8 1.1 copy.33
  23.6 66.0 %shard_map.229 = (bf16[2,8,2,48,768]{4,3,2,1,0:T(8,128)(2,1)}, bf16[2,8,2,48,768]{4,3,2,1,0:T(8,128)(2,1)}, bf16[8,2,2,96,768]{4,3,2,1,0:T(8,128)(2,1)}, bf16[2,2,8,96,768]{4,3,2,1,0:T(8,128)(2,1)}) custom-call(bf16[2,2,48,768]{3,2,1,0:T(8,128)(2,1)} %get-tuple-element.110.refs_0_, bf16[2,2,48,768]{3,2,1,0:T(8,128)(2,1)} %get-tuple-element.111.refs_1_, ...), custom_call_target="tpu_custom_call" | custom-call | tf_op jit(solution)/shard_map/pallas_call | solution.py:115
  89.6 15.1 %key_query.1 = (bf16[6,512,128]{2,1,0:T(8,128)(2,1)}, bf16[6,512,128]{2,1,0:T(8,128)(2,1)}, bf16[6,512,128]{2,1,0:T(8,128)(2,1)}, bf16[6,512,512]{2,1,0:T(8,128)...) custom-call(bf16[512,768]{1,0:T(8,128)(2,1)} %bitcast.112, ...), custom_call_target="tpu_custom_call" | custom-call | tf_op jit(solution)/shard_map/key_query/pallas_call | solution.py:571
  104.7 1.4 copy-done.2
  106.1 0.9 copy-done.6
  107.0 44.3 %shard_map.230 = (f32[4,3,128,256]{3,2,1,0:T(8,128)S(1)}, f32[4,3,8,512]{3,2,1,0:T(8,128)S(1)}) custom-call(f32[4,3,128,256]{3,2,1,0:T(8,128)S(1)} %bitcast.98, f32[4,3,8,512]{3,2,1,0:T(8,128)S(1)} %bitcast.102), custom_call_target="tpu_custom_call" | custom-call | tf_op jit(solution)/shard_map/pallas_call | solution.py:555
  151.3 1.1 copy-done
  153.2 32.9 %forward.1 = (f32[6,512,128]{2,1,0:T(8,128)}, f32[6,512,128]{2,1,0:T(8,128)}, bf16[512,768]{1,0:T(8,128)(2,1)}, bf16[2,6,256,512]{3,2,1,0:T(8,128)(2,1)}, f32[51...) custom-call(bf16[512,768]{1,0:T(8,128)(2,1)} %bitcast.113, ...), custom_call_target="tpu_custom_call" | custom-call | tf_op jit(solution)/shard_map/forward/pallas_call | solution.py:571
  186.1 1.4 slice.35
  187.5 38.3 %backward.1 = (bf16[3072,768]{1,0:T(8,128)(2,1)}, bf16[4,768,768]{2,1,0:T(8,128)(2,1)}, bf16[2,768,768]{2,1,0:T(8,128)(2,1)}, f32[512,768]{1,0:T(8,128)}, bf16[6...) custom-call(bf16[512,768]{1,0:T(8,128)(2,1)} %get-tuple-element.67.gffn, ...), custom_call_target="tpu_custom_call" | custom-call | tf_op jit(solution)/shard_map/backward/pallas_call | solution.py:571
  225.8 1.4 copy-done.1
  227.2 0.9 copy-done.5
  228.1 24.6 %shard_map.231 = (bf16[4,3,128,256]{3,2,1,0:T(8,128)(2,1)S(1)}, f32[4,3,8,512]{3,2,1,0:T(8,128)S(1)}) custom-call(f32[4,3,128,256]{3,2,1,0:T(8,128)S(1)} %bitcast.97, f32[4,3,8,512]{3,2,1,0:T(8,128)S(1)} %bitcast.101), custom_call_target="tpu_custom_call" | custom-call | tf_op jit(solution)/shard_map/pallas_call | solution.py:555
  252.7 0.9 copy-done.3
  254.3 13.3 %last.1 = (bf16[2,768,768]{2,1,0:T(8,128)(2,1)}, f32[512,768]{1,0:T(8,128)}) custom-call(bf16[6,512,128]{2,1,0:T(8,128)(2,1)} %get-tuple-element.64.kp, bf16[6,512,128]{2,1,0:T(8,128)(2,1)} %get-tuple-element.65.vp, bf16[6,512,512]{2,1,0:T(8,128)(2,1)} %get-tuple-element.66.kf, bf16[2,6,128,256]{3,2,1,0:T(8,128)(2,1)} %bitcast.99, ...), custom_call_target="tpu_custom_call" | custom-call | tf_op jit(solution)/shard_map/last/pallas_call | solution.py:571
  267.5 91.5 %shard_map.232 = (bf16[2,2,48,768]{3,2,1,0:T(8,128)(2,1)}, bf16[2,2,48,768]{3,2,1,0:T(8,128)(2,1)}, bf16[2,2,96,768]{3,2,1,0:T(8,128)(2,1)}, bf16[2,2,96,768]{3,2,1,0:T(8,128)(2,1)}) custom-call(bf16[2,8,2,48,768]{4,3,2,1,0:T(8,128)(2,1)} %bitcast.121, bf16[2,8,2,48,768]{4,3,2,1,0:T(8,128)(2,1)} %bitcast.120, bf16[8,2,2,96,768]{4,3,2,1,0:T(8,128)(2,1)} %bitcast.118, ...), custom_call_target="tpu_custom_call" | custom-call | tf_op jit(solution)/shard_map/pallas_call | solution.py:509
  359.1 1.1 fusion.1
  361.8 46.0 %psum.7 = f32[4,768]{1,0:T(4,128)S(1)} all-reduce(f32[4,768]{1,0:T(4,128)S(1)} %maximum_reduce_fusion), channel_id=1, replica_groups=mesh['seq'=4,'dp'=8] {'seq','dp'}, use_global_device_ids=true, to_apply=%region_1.2 | all-reduce | flops 3072 | bytes 24576 | tf_op jit(solution)/shard_map/psum | solution.py:671
  411.5 1.4 copy.38
  413.0 1.1 copy.41
  (60 shorter events, 12.3 us)
Async XLA Ops:
  0.6 17.7 %copy-start.19 = (bf16[64,512]{0,1:T(8,128)(2,1)S(1)}, bf16[64,512]{0,1:T(8,128)(2,1)}, u32[]{:S(2)}) copy-start(bf16[64,512]{0,1:T(8,128)(2,1)} %constant.11.clone.1) | copy-start | bytes 196612
  0.7 17.7 %copy-start.20 = (bf16[64,512]{0,1:T(8,128)(2,1)S(1)}, bf16[64,512]{0,1:T(8,128)(2,1)}, u32[]{:S(2)}) copy-start(bf16[64,512]{0,1:T(8,128)(2,1)} %constant.10.clone.1) | copy-start | bytes 196612
  0.7 18.6 %copy-start.12 = (bf16[64,512]{0,1:T(8,128)(2,1)S(1)}, bf16[64,512]{0,1:T(8,128)(2,1)}, u32[]{:S(2)}) copy-start(bf16[64,512]{0,1:T(8,128)(2,1)} %constant.9.clone.1) | copy-start | bytes 196612
  0.7 18.6 %copy-start.13 = (bf16[64,512]{0,1:T(8,128)(2,1)S(1)}, bf16[64,512]{0,1:T(8,128)(2,1)}, u32[]{:S(2)}) copy-start(bf16[64,512]{0,1:T(8,128)(2,1)} %constant.8.clone.1) | copy-start | bytes 196612
  18.3 2.5 copy-start.10
  19.2 2.6 copy-start.11
  19.7 3.0 copy-start.15
  19.7 3.0 copy-start.16
  19.7 3.0 copy-start.17
  19.8 3.0 copy-start.18
  104.7 1.4 copy-start.2
  106.1 0.9 copy-start.6
  151.3 1.1 copy-start
  152.5 0.7 copy-start.4
  225.8 1.4 copy-start.1
  227.2 0.9 copy-start.5
  252.7 0.9 copy-start.3
  253.6 0.7 copy-start.7
  359.1 50.8 %copy-start.14 = (bf16[2,2,48,768]{3,2,1,0:T(8,128)(2,1)S(1)}, bf16[2,2,48,768]{3,2,1,0:T(8,128)(2,1)}, u32[]{:S(2)}) copy-start(bf16[2,2,48,768]{3,2,1,0:T(8,128)(2,1)} %get-tuple-element.91) | copy-start | bytes 884740
  359.1 52.3 %copy-start.9 = (bf16[2,2,96,768]{3,2,1,0:T(8,128)(2,1)S(1)}, bf16[2,2,96,768]{3,2,1,0:T(8,128)(2,1)}, u32[]{:S(2)}) copy-start(bf16[2,2,96,768]{3,2,1,0:T(8,128)(2,1)} %get-tuple-element.92) | copy-start | bytes 1769476
  411.5 1.4 copy-start.8

commit v3 on v2

v3 whole, which is shorter than its diff:
```python
import functools
from functools import partial

import jax
import jax.numpy as jnp
from jax import lax
from jax.experimental import pallas as pl
from jax.experimental.pallas import tpu as pltpu
from jax.sharding import PartitionSpec as P

MESH = pl.DeviceIdType.MESH
bf, f32 = jnp.bfloat16, jnp.float32
HEAD = 64
EPS = 1e-12


def coords():
    s, d = lax.axis_index("seq"), lax.axis_index("dp")
    return s // 2, s % 2, d // 2, d % 2

def dev(y, x, z, c):
    return (y * 2 + x, z * 2 + c)

def entry_barrier(peers):
    sem = pltpu.get_barrier_semaphore()
    for p in peers:
        pl.semaphore_signal(sem, inc=1, device_id=p, device_id_type=MESH)
    pl.semaphore_wait(sem, len(peers))

GROUPS = ((0, 0), (1, 0), (2, 0), (2, 1), (3, 0), (3, 1))
NAMES = ("kv", "qo", "wi0", "wi1", "wu0", "wu1")
ZFIRST = (2,)
EARLY = 4
NG = len(GROUPS)

def some(g, r):
    return pl.ds(GROUPS[g][1] * r, r)
def piece(g, ref, d, y, x, r):
    i = GROUPS[g][0]
    if i < 2:  return ref.at[y, d, x]
    if i == 2: return ref.at[d, y, x, some(g, r)]
    return ref.at[y, x, d, some(g, r)]
def lpiece(g, ref, y, x, r):
    return ref.at[y, x, some(g, r)]
def local_rows(g, ref, r):
    return ref.at[:, :, some(g, r)]
def shard(g, ref, d, r):
    i = GROUPS[g][0]
    if i < 2:  return ref.at[:, d]
    if i == 2: return ref.at[d, :, :, some(g, r)]
    return ref.at[:, :, d, some(g, r)]

class Gather:
    def __init__(self, nz, loc, out, sems, r):
        self.nz, self.sems, self.r = nz, sems, r
        self.loc, self.out = [loc[i] for i, _ in GROUPS], [out[i] for i, _ in GROUPS]
        y, x, z, c = self.pos = coords()
        dp = nz * 2
        self.ynb, self.xnb, self.sib = dev(1 - y, x, z, c), dev(y, 1 - x, z, c), dev(y, x, z, 1 - c)
        self.zpeer = [dev(y, x, (z + k) % nz, c) for k in range(1, nz)]
        self.me = z * 2 + c
        self.dpeer = [dev(y, x, (self.me + k) % dp // 2, (self.me + k) % 2) for k in range(1, dp)]
        self.started = []
        half = loc[3].shape[-1] // 2
        self.H = (pl.ds(0, half), pl.ds(half, half))

    def _rc(self, src, dst, ssem, rsem, to):
        return pltpu.make_async_remote_copy(src_ref=src, dst_ref=dst, send_sem=ssem, recv_sem=rsem, device_id=to, device_id_type=MESH)

    def _go(self, *a):
        cp = self._rc(*a)
        cp.start()
        self.started.append(cp)

    def _recv(self, dst, ssem, rsem, to):
        self._rc(dst, dst, ssem, rsem, to).wait_recv()

    def _local(self, g):
        return pltpu.make_async_copy(local_rows(g, self.loc[g], self.r), shard(g, self.out[g], self.me, self.r), self.sems[10].at[g])

    def _own(self, g):
        ss, sr = self.sems[8:10]
        self._go(local_rows(g, self.loc[g], self.r), shard(g, self.out[g], self.me, self.r), ss.at[g, 0], sr.at[g, 0], self.sib)
        self._local(g).start()

    def _vlocal(self, vloc, vout):
        return pltpu.make_async_copy(vloc, vout.at[self.me], self.sems[10].at[NG])

    def start(self, wz, vloc, vout):
        zs, zr, vs, vr = *self.sems[:2], *self.sems[11:13]
        y, x, z, c = self.pos
        for g in range(EARLY):
            for k in range(1, self.nz):
                self._go(lpiece(g, self.loc[g], y, x, self.r), piece(g, self.out[g], self.me, y, x, self.r), zs.at[g, k-1], zr.at[g, k-1], self.zpeer[k-1])
            self._own(g)
        for k in range(1, self.nz):
            self._go(self.loc[EARLY].at[y, x], wz.at[k - 1], zs.at[EARLY, k-1], zr.at[EARLY, k-1], self.zpeer[k-1])
        for k in range(1, self.nz * 2):
            self._go(vloc, vout.at[self.me], vs.at[k - 1], vr.at[k - 1], self.dpeer[k - 1])
        self._vlocal(vloc, vout).start()

    def _wz_local(self, wz, g, k):
        y, x, z, c = self.pos
        return pltpu.make_async_copy(wz.at[k - 1, some(g, self.r)], piece(g, self.out[g], self._from(k, c), y, x, self.r), self.sems[0].at[g, k - 1])

    def relay(self, wz):
        xs, xr, ys, yr = self.sems[2:6]
        y, x, z, c = self.pos
        for g in range(EARLY, NG):
            for k in range(1, self.nz):
                p, src = piece(g, self.out[g], self._from(k, c), y, x, self.r), wz.at[k - 1, some(g, self.r)]
                self._go(src, p, xs.at[g, k-1], xr.at[g, k-1], self.xnb)
                self._go(src, p, ys.at[g, k-1], yr.at[g, k-1], self.ynb)
        for g in range(EARLY, NG):
            for k in range(1, self.nz): self._wz_local(wz, g, k).start()
            self._own(g)

    def stage(self, g, i):
        (None, self.st1, self.st2, self.st3, self.done)[i](g)

    def _from(self, k, c):
        return ((self.pos[2] + self.nz - k) % self.nz) * 2 + c

    def st1(self, g):
        zs, zr, xs, xr, ys, yr = self.sems[:6]
        y, x, z, c = self.pos
        for k in range(1, self.nz):
            p = piece(g, self.out[g], self._from(k, c), y, x, self.r)
            self._recv(p, zs.at[g, k-1], zr.at[g, k-1], self.zpeer[k-1])
            self._go(p, p, xs.at[g, k-1], xr.at[g, k-1], self.xnb)
            self._go(p, p, ys.at[g, k-1], yr.at[g, k-1], self.ynb)

    def st2(self, g):
        xs, xr, ys, yr, ds_, dr = self.sems[2:8]
        y, x, z, c = self.pos
        for k in range(1, self.nz):
            d = self._from(k, c)
            p = piece(g, self.out[g], d, y, 1 - x, self.r)
            self._recv(p, xs.at[g, k-1], xr.at[g, k-1], self.xnb)
            pa = p.at[:, self.H[0]]
            self._go(pa, pa, ds_.at[g, k-1, 0], dr.at[g, k-1, 0], self.ynb)
            p = piece(g, self.out[g], d, 1 - y, x, self.r)
            self._recv(p, ys.at[g, k-1], yr.at[g, k-1], self.ynb)
            pb = p.at[:, self.H[1]]
            self._go(pb, pb, ds_.at[g, k-1, 1], dr.at[g, k-1, 1], self.xnb)

    def st3(self, g):
        ds_, dr, ss, sr = self.sems[6:10]
        y, x, z, c = self.pos
        for k in range(1, self.nz):
            d = self._from(k, c)
            p = piece(g, self.out[g], d, 1 - y, 1 - x, self.r)
            pa, pb = p.at[:, self.H[0]], p.at[:, self.H[1]]
            self._recv(pa, ds_.at[g, k-1, 0], dr.at[g, k-1, 0], self.ynb)
            self._recv(pb, ds_.at[g, k-1, 1], dr.at[g, k-1, 1], self.xnb)
            sh = shard(g, self.out[g], d, self.r)
            self._go(sh, sh, ss.at[g, k], sr.at[g, k], self.sib)

    def done(self, g):
        ss, sr = self.sems[8:10]
        for k in range(self.nz):
            self._recv(shard(g, self.out[g], self._from(k, 1 - self.pos[3]), self.r), ss.at[g, k], sr.at[g, k], self.sib)
        self._local(g).wait()

    def end(self, wz, vloc, vout):
        zs, zr, vs, vr = *self.sems[:2], *self.sems[11:13]
        dp = self.nz * 2
        for k in range(1, self.nz):
            self._recv(wz.at[k - 1], zs.at[EARLY, k-1], zr.at[EARLY, k-1], self.zpeer[k-1])
        for k in range(1, dp):
            self._recv(vout.at[(self.me + dp - k) % dp], vs.at[k - 1], vr.at[k - 1], self.dpeer[k - 1])
        self._vlocal(vloc, vout).wait()
        self.finish()

    def finish(self):
        for cp in self.started:
            cp.wait_send()

def gather_sems(dp):
    nz = dp // 2
    n = nz - 1
    S = pltpu.SemaphoreType.DMA
    return [S((NG, n)) for _ in range(6)] + [S((NG, n, 2)), S((NG, n, 2)), S((NG, nz)), S((NG, nz)), S((NG + 1,)), S((dp - 1,)), S((dp - 1,))]

def pack(wq, wk, wv, wo, win, wout):
    D = wq.shape[0]
    sh = wq.shape[1]
    t = jnp.transpose
    kv = jnp.stack([t(wk), t(wv)]).reshape(2, 2, sh // 2, D)
    qo = jnp.stack([t(wq), t(wo)]).reshape(2, 2, sh // 2, D)
    wi = t(win).reshape(2, 2, win.shape[1] // 4, D)
    ff = wout.shape[0]
    wu = t(wout.reshape(ff // D, D, sh), (0, 2, 1)).reshape(2, 2, sh, D)
    return kv, qo, wi, wu


def nn(a, b): return lax.dot_general(a, b, (((1,), (0,)), ((), ())), preferred_element_type=f32)
def nt(a, b): return lax.dot_general(a, b, (((1,), (1,)), ((), ())), preferred_element_type=f32)
def tn(a, b): return lax.dot_general(a, b, (((0,), (0,)), ((), ())), preferred_element_type=f32)

def ds(i, n): return pl.ds(pl.multiple_of(i * n, n), n)

def mat(w):
    return w[...].reshape(-1, w.shape[-1])

def project(tok, w, dst):
    D = tok.shape[1]
    v = mat(w)
    for n in range(D // 256):
        o = nt(tok[...], v[n * 256:(n + 1) * 256, :]).astype(bf)
        dst[2 * n] = o[:, :128]
        dst[2 * n + 1] = o[:, 128:]

def features(x, wf):
    xf = x.astype(f32)
    sq = xf * xf
    hi = sq.astype(bf)
    lo = (sq - hi.astype(f32)).astype(bf)
    return jnp.exp(nn(jnp.concatenate([x, x, hi, lo], 1), wf[...]))

def pair_mask(m):
    r = lax.broadcasted_iota(jnp.int32, (128, 2 * m), 0) < HEAD
    c = lax.broadcasted_iota(jnp.int32, (128, 2 * m), 1) < m
    return (r == c)

def compact(st, m):
    return jnp.concatenate([st[:HEAD, :m], st[HEAD:, m:]], 0)

def key_side(kp, vp, wf, vm, kf, st, kt, nseq, loc):
    P_ = kp.shape[0]
    M = wf.shape[1] // 2
    def body(p, _):
        f = features(kp[p], wf) * jnp.concatenate([vm[...]] * (2 * M // 128), 1)
        fb = f.astype(bf)
        kf[p] = fb
        for b in range(nseq):
            rows = slice(b * loc, (b + 1) * loc)
            st[b, p] = compact(tn(vp[p, rows, :], fb[rows]), M)
            kt[b, p] = jnp.broadcast_to(jnp.sum(f[rows], 0, keepdims=True), (8, 2 * M))
        return 0
    lax.fori_loop(0, P_, body, 0)

def query_side(qp, wf, qf):
    def body(p, _):
        qf[p] = features(qp[p], wf).astype(bf)
        return 0
    lax.fori_loop(0, qp.shape[0], body, 0)

def build_right(st, kt, right, m):
    mask = pair_mask(m)
    nseq, P_ = right.shape[:2]
    for b in range(nseq):
        def body(p, _):
            c = st[b, p].astype(f32)
            s = jnp.where(mask, jnp.concatenate([c, c], 1), 0.0)
            t = jnp.where(mask, jnp.broadcast_to(kt[b, p][:1], (128, 2 * m)), 0.0)
            right[b, p] = jnp.concatenate([s, t], 0).astype(bf)
            return 0
        lax.fori_loop(0, P_, body, 0)

def mix_forward(qf, right, ctx, den, ctxb, nseq, loc):
    def body(p, _):
        for b in range(nseq):
            rows = slice(b * loc, (b + 1) * loc)
            o = nt(qf[p, rows, :], right[b, p])
            d = o[:, 128:]
            c = o[:, :128] / d
            ctx[p, rows, :] = c
            den[p, rows, :] = d
            ctxb[rows, ds(p, 128)] = c.astype(bf)
        return 0
    lax.fori_loop(0, qf.shape[0], body, 0)

def mean(a): return jnp.mean(a, -1, keepdims=True)

def attend_out(ctxb, wo, tok, n1, inv1, resid):
    T, D = tok.shape
    v = mat(wo)
    for n in range(D // 256):
        resid[:, n * 256:(n + 1) * 256] = nt(ctxb[...], v[n * 256:(n + 1) * 256, :])
    R = 64
    def body(i, _):
        r = ds(i, R)
        x = tok[r, :].astype(f32) + resid[r, :]
        cen = x - mean(x)
        inv = lax.rsqrt(mean(cen * cen) + EPS)
        n1[r, :] = cen * inv
        inv1[r, :] = jnp.broadcast_to(inv, (R, 128))
        return 0
    lax.fori_loop(0, T // R, body, 0)

def ffn_chunk(j, hlow, win, act, gp):
    C = act.shape[2]
    pre = nt(hlow[...], win[ds(j, C), :])
    cdf = 0.5 * (1.0 + lax.erf(pre * 0.7071067811865476))
    act[j] = (pre * cdf).astype(bf)
    gp[j] = (cdf + pre * (jnp.exp(-0.5 * pre * pre) * 0.3989422804014327)).astype(bf)

def out_columns(wout, j, C):
    per = wout.shape[-1] // C
    jj, cc = j // per, ds(lax.rem(j, per), C)
    if len(wout.shape) == 3:
        return wout[jj, :, cc]
    return wout[jj // 2, lax.rem(jj, 2), :, :, cc].reshape(-1, C)

def ffn_output(j, act, wout, acc, first):
    o = nt(act[j], out_columns(wout, j, act.shape[2]))
    if first: acc[...] = o
    else: acc[...] += o

def hidden_rows(n1, vec, hlow):
    R = 64
    def body(i, _):
        r = ds(i, R)
        hlow[r, :] = (n1[r, :] * vec[0:1, :] + vec[1:2, :]).astype(bf)
        return 0
    lax.fori_loop(0, n1.shape[0] // R, body, 0)

def fold8(a):
    return jnp.sum(a.reshape(a.shape[0] // 8, 8, a.shape[1]), 0)

def norm_pull(g, n, inv, gain):
    e = g * gain
    return inv * (e - mean(e) - n * mean(e * n))

def second_norm(acc, n1, vec, vm, cot, out, gr2, gffn, sums):
    T, D = acc.shape
    R = 64
    sums[0] = jnp.zeros((8, D), f32)
    sums[1] = jnp.zeros((8, D), f32)
    def body(i, _):
        r = ds(i, R)
        x = n1[r, :] * vec[0:1, :] + vec[1:2, :] + acc[r, :]
        cen = x - mean(x)
        inv = lax.rsqrt(mean(cen * cen) + EPS)
        n = cen * inv
        v = vm[r, :]
        vv = jnp.concatenate([v] * (D // 128), 1)
        out[r, :] = ((n * vec[2:3, :] + vec[3:4, :]) * vv).astype(bf)
        gy = cot[r, :].astype(f32) * vv
        sums[0] += fold8(gy * n)
        sums[1] += fold8(gy)
        g = norm_pull(gy, n, inv, vec[2:3, :])
        gr2[r, :] = g
        gffn[r, :] = g.astype(bf)
        return 0
    lax.fori_loop(0, T // R, body, 0)

def ffn_out_grad(j, gffn_t, act, gwout):
    C = act.shape[2]
    per = gwout.shape[-1] // C
    o = nn(gffn_t[...], act[j]).astype(bf)
    jj, cc = j // per, ds(lax.rem(j, per), C)
    if len(gwout.shape) == 3:
        gwout[jj, :, cc] = o
    else:
        gwout[jj // 2, lax.rem(jj, 2), :, :, cc] = o.reshape(gwout.shape[2], gwout.shape[3], C)

def ffn_backward(j, gffn, hlow, win, wout, gp, gwin, gh, first):
    C = gp.shape[2]
    ga = nn(gffn[...], out_columns(wout, j, C))
    gpre = (ga * gp[j].astype(f32)).astype(bf)
    gwin[ds(j, C), :] = tn(gpre, hlow[...]).astype(bf)
    o = nn(gpre, win[ds(j, C), :])
    if first: gh[...] = o
    else: gh[...] += o

def first_norm_back(gh, gr2, n1, inv1, vec, gr1, gattn, sums):
    T, D = gh.shape
    R = 64
    sums[2] = jnp.zeros((8, D), f32)
    sums[3] = jnp.zeros((8, D), f32)
    def body(i, _):
        r = ds(i, R)
        g = gr2[r, :] + gh[r, :]
        n = n1[r, :]
        sums[2] += fold8(g * n)
        sums[3] += fold8(g)
        o = norm_pull(g, n, inv1[r, :][:, :1], vec[0:1, :])
        gr1[r, :] = o
        gattn[r, :] = o.astype(bf)
        return 0
    lax.fori_loop(0, T // R, body, 0)

def put_units(dst, n, o):
    dp, _, a, _ = dst.shape
    for u in range(dp):
        i = n * dp + u
        dst[i // 2, i % 2] = o[u * a:(u + 1) * a].astype(bf)

def weight_grad_units(gt, x, dst):
    h = gt.shape[0] // 2
    for n in range(2):
        put_units(dst, n, nn(gt[n * h:(n + 1) * h, :], x[...]))

def weight_grad_pairs_units(gp_, x, dst):
    h = gp_.shape[0] // 2
    for n in range(2):
        g = jnp.concatenate([gp_[n * h + i] for i in range(h)], 1)
        put_units(dst, n, tn(g, x[...]))

def weight_grad(gt, x, dst):
    D = x.shape[1]
    for n in range(D // 256):
        dst[n * 256:(n + 1) * 256, :] = nn(gt[n * 256:(n + 1) * 256, :], x[...]).astype(bf)

def weight_grad_pairs(gp_, x, dst):
    P_ = gp_.shape[0]
    for n in range(P_ // 2):
        g = jnp.concatenate([gp_[2 * n], gp_[2 * n + 1]], 1)
        dst[n * 256:(n + 1) * 256, :] = tn(g, x[...]).astype(bf)

def mix_back_query(gattn, wo, qp, qf, right, ctx, den, fbm, gst, gkt, gq, nseq, loc):
    M = qf.shape[2] // 2
    mask = pair_mask(M)
    def body(p, _):
        gc = nn(gattn[...], wo[:, ds(p, 128)]).astype(bf).astype(f32)
        gn = gc / den[p]
        t = -gn * ctx[p]
        g = jnp.concatenate([gn, t], 1).astype(bf)
        for b in range(nseq):
            rows = slice(b * loc, (b + 1) * loc)
            q = qf[p, rows, :]
            s = tn(g[rows], q)
            gst[b, p] = compact(s[:128], M)
            gkt[b, p] = jnp.broadcast_to(jnp.sum(jnp.where(mask, s[128:], 0.0), 0, keepdims=True), (8, 2 * M))
            pr = (nn(g[rows], right[b, p]) * q.astype(f32)).astype(bf)
            o = nn(pr, fbm[...])
            gq[p, rows, :] = (o[:, :128] - 0.125 * qp[p, rows, :].astype(f32) * o[:, 128:]).astype(bf)
        return 0
    lax.fori_loop(0, qf.shape[0], body, 0)

def mix_back_key(kp, vp, kf, gst, gkt, fbm, gk, gv, nseq, loc):
    M = kf.shape[2] // 2
    mask = pair_mask(M)
    def body(p, _):
        for b in range(nseq):
            rows = slice(b * loc, (b + 1) * loc)
            c = gst[b, p].astype(f32)
            s = jnp.where(mask, jnp.concatenate([c, c], 1), 0.0).astype(bf)
            k = kf[p, rows, :]
            pr = ((nn(vp[p, rows, :], s) + gkt[b, p][:1]) * k.astype(f32)).astype(bf)
            o = nn(pr, fbm[...])
            gk[p, rows, :] = (o[:, :128] - 0.125 * kp[p, rows, :].astype(f32) * o[:, 128:]).astype(bf)
            gv[p, rows, :] = nt(k, s).astype(bf)
        return 0
    lax.fori_loop(0, kf.shape[0], body, 0)

def join(g):
    return jnp.concatenate([g[i] for i in range(g.shape[0])], 1)

def token_grad(gr1, gq, gk, gv, wq, wk, wv, dst):
    D = gr1.shape[1]
    for n in range(D // 256):
        c = slice(n * 256, (n + 1) * 256)
        dst[:, c] = gr1[:, c] + (nn(join(gq), wq[:, c]) + nn(join(gk), wk[:, c]) + nn(join(gv), wv[:, c]))

def token_grad_query(gq, wq, dst):
    D = dst.shape[1]
    for n in range(D // 256):
        c = slice(n * 256, (n + 1) * 256)
        dst[:, c] += nn(join(gq), wq[:, c])

def token_grad_keys(gk, gv, wk, wv, dst):
    D = dst.shape[1]
    for n in range(D // 256):
        c = slice(n * 256, (n + 1) * 256)
        dst[:, c] += nn(join(gk), wk[:, c]) + nn(join(gv), wv[:, c])

def split_features(rf):
    w = rf * HEAD ** (-0.25)
    hi = w.astype(bf)
    lo = (w - hi.astype(f32)).astype(bf)
    z = jnp.zeros(rf.shape, bf)
    def bd(a): return jnp.concatenate([jnp.concatenate([a, z], 1), jnp.concatenate([z, a], 1)], 0)
    return hi, lo, bd

def feature_matrix(rf):
    hi, lo, bd = split_features(rf)
    s = bd(jnp.full(rf.shape, -0.0625, bf))
    return jnp.concatenate([bd(hi), bd(lo), s, s], 0)

def feature_pull(rf):
    hi, lo, bd = split_features(rf)
    return jnp.concatenate([bd(hi), bd(jnp.ones(rf.shape, bf))], 0).T


class Reduce:
    def __init__(self, nz, grads, own, scratch, sems, own_sem, fins, r):
        self.nz, self.own, self.own_sem, self.sem, self.r, self.sc = nz, own, own_sem, sems, r, scratch
        self.grads = [grads[i] for i, _ in GROUPS]
        if fins is not None:
            self.fins = [local_rows(g, fins[GROUPS[g][0]], r) for g in range(NG)]
            self.h = fins[0].shape[-1] // 2
        else:
            self.h = grads[3].shape[-1] // 2
        self.started = []
        y, x, z, c = self.pos = coords()
        self.ynb, self.xnb, self.sibdev = dev(1 - y, x, z, c), dev(y, 1 - x, z, c), dev(y, x, z, 1 - c)
        self.zpeer = [dev(y, x, (z + k) % nz, c) for k in range(1, nz)]
        self.A, self.B = pl.ds(0, self.h), pl.ds(self.h, self.h)

    def _cp(self, src, dst, g, i, to):
        s, r = self.sem
        return pltpu.make_async_remote_copy(src_ref=src, dst_ref=dst, send_sem=s.at[g, i], recv_sem=r.at[g, i], device_id=to, device_id_type=MESH)

    def _go(self, src, dst, g, i, to):
        cp = self._cp(src, dst, g, i, to)
        cp.start()
        self.started.append(cp)

    def _recv(self, dst, g, i, to):
        self._cp(dst, dst, g, i, to).wait_recv()

    def stage(self, g, i):
        late = g in ZFIRST
        (self.s0, self.z1 if late else self.s1, self.z2 if late else self.s2, self.z3 if late else self.s3, self.z4 if late else self.s4, self.s5, self.s6)[i](g)

    def s0(self, g):
        c = self.pos[3]
        sib = self.sc[g][0]
        for k in range(self.nz):
            self._go(shard(g, self.grads[g], k * 2 + 1 - c, self.r), sib.at[k], g, k, self.sibdev)
        if self.own[g] is not None:
            for k in range(self.nz):
                self._own(g, k).start()

    def _own(self, g, k):
        c = self.pos[3]
        return pltpu.make_async_copy(shard(g, self.grads[g], k * 2 + c, self.r), self.own[g].at[k], self.own_sem.at[g, k])

    def _pair(self, g):
        c = self.pos[3]
        sib, own, gr = self.sc[g][0], self.own[g], self.grads[g]
        for k in range(self.nz):
            self._recv(sib.at[k], g, k, self.sibdev)
            if own is not None:
                self._own(g, k).wait()
        def body(i, _):
            k, q = i // 4, lax.rem(i, 4)
            qy, qx = q // 2, lax.rem(q, 2)
            mine = piece(g, gr, k * 2 + c, qy, qx, self.r) if own is None else own.at[k, qy, qx]
            sib[k, qy, qx] = (sib[k, qy, qx].astype(f32) + mine[...].astype(f32)).astype(bf)
            return 0
        lax.fori_loop(0, self.nz * 4, body, 0)

    def s1(self, g):
        y, x, z, c = self.pos
        sib, a1, b1 = self.sc[g][:3]
        self._pair(g)
        self._go(sib.at[:, :, 1 - x, :, self.A], a1, g, self.nz, self.xnb)
        self._go(sib.at[:, 1 - y, :, :, self.B], b1, g, self.nz + 1, self.ynb)

    def recv1(self, g):
        a1, b1 = self.sc[g][1:3]
        self._recv(a1, g, self.nz, self.xnb)
        self._recv(b1, g, self.nz + 1, self.ynb)

    def s2(self, g):
        y, x, z, c = self.pos
        nz, h = self.nz, self.h
        sib, a1, b1, a2, b2 = self.sc[g][:5]
        if g < EARLY:
            self.recv1(g)
        def body(i, _):
            k, j = i // 2, lax.rem(i, 2)
            a1[k, j] = (a1[k, j].astype(f32) + sib[k, j, x, :, :h].astype(f32)).astype(bf)
            b1[k, j] = (b1[k, j].astype(f32) + sib[k, y, j, :, h:].astype(f32)).astype(bf)
            return 0
        lax.fori_loop(0, nz * 2, body, 0)
        self._go(a1.at[:, 1 - y], a2, g, nz + 2, self.ynb)
        self._go(b1.at[:, 1 - x], b2, g, nz + 3, self.xnb)

    def s3(self, g):
        y, x, z, c = self.pos
        nz, h = self.nz, self.h
        a1, b1, a2, b2, tot, zrec = self.sc[g][1:]
        self._recv(a2, g, nz + 2, self.ynb)
        self._recv(b2, g, nz + 3, self.xnb)
        def body(k, _):
            tot[k, :, :h] = (a1[k, y].astype(f32) + a2[k].astype(f32)).astype(bf)
            tot[k, :, h:] = (b1[k, x].astype(f32) + b2[k].astype(f32)).astype(bf)
            return 0
        lax.fori_loop(0, nz, body, 0)
        for k in range(1, nz):
            self._go(tot.at[(z + k) % nz], zrec.at[k - 1], g, nz + 3 + k, self.zpeer[k - 1])

    def s4(self, g):
        y, x, z, c = self.pos
        nz, fin = self.nz, self.fins[g]
        tot, zrec = self.sc[g][5:]
        for k in range(1, nz):
            self._recv(zrec.at[k - 1], g, nz + 3 + k, self.zpeer[k - 1])
        t = tot[z].astype(f32)
        for k in range(1, nz):
            t = t + zrec[k - 1].astype(f32)
        fin[y, x] = t.astype(bf)
        self._spread(g)

    def z1(self, g):
        z = self.pos[2]
        sib, zrec = self.sc[g][0], self.sc[g][6]
        self._pair(g)
        for k in range(1, self.nz):
            self._go(sib.at[(z + k) % self.nz], zrec.at[k - 1], g, self.nz + 3 + k, self.zpeer[k - 1])

    def z2(self, g):
        y, x, z, c = self.pos
        nz = self.nz
        sib, a1, b1, a2, b2, tot, zrec = self.sc[g]
        for k in range(1, nz):
            self._recv(zrec.at[k - 1], g, nz + 3 + k, self.zpeer[k - 1])
        def body(i, _):
            j, l = i // 2, lax.rem(i, 2)
            t = sib[z, j, l].astype(f32)
            for k in range(1, nz):
                t = t + zrec[k - 1, j, l].astype(f32)
            tot[j, l] = t.astype(bf)
            return 0
        lax.fori_loop(0, 4, body, 0)
        self._go(tot.at[:, 1 - x, :, self.A], a1, g, nz, self.xnb)
        self._go(tot.at[1 - y, :, :, self.B], b1, g, nz + 1, self.ynb)

    def z3(self, g):
        y, x, z, c = self.pos
        nz, h = self.nz, self.h
        sib, a1, b1, a2, b2, tot, zrec = self.sc[g]
        self._recv(a1, g, nz, self.xnb)
        self._recv(b1, g, nz + 1, self.ynb)
        for j in range(2):
            a1[j] = (a1[j].astype(f32) + tot[j, x, :, :h].astype(f32)).astype(bf)
            b1[j] = (b1[j].astype(f32) + tot[y, j, :, h:].astype(f32)).astype(bf)
        self._go(a1.at[1 - y], a2, g, nz + 2, self.ynb)
        self._go(b1.at[1 - x], b2, g, nz + 3, self.xnb)

    def z4(self, g):
        y, x, z, c = self.pos
        nz, h, fin = self.nz, self.h, self.fins[g]
        a1, b1, a2, b2 = self.sc[g][1:5]
        self._recv(a2, g, nz + 2, self.ynb)
        self._recv(b2, g, nz + 3, self.xnb)
        fin[y, x, :, :h] = (a1[y].astype(f32) + a2[...].astype(f32)).astype(bf)
        fin[y, x, :, h:] = (b1[x].astype(f32) + b2[...].astype(f32)).astype(bf)
        self._spread(g)

    def _spread(self, g):
        y, x, z, c = self.pos
        a, b = self.fins[g].at[y, x, :, self.A], self.fins[g].at[y, x, :, self.B]
        self._go(a, a, g, 2 * self.nz + 3, self.xnb)
        self._go(b, b, g, 2 * self.nz + 4, self.ynb)

    def s5(self, g):
        y, x, z, c = self.pos
        nz, fin = self.nz, self.fins[g]
        self._recv(fin.at[y, 1 - x, :, self.A], g, 2 * nz + 3, self.xnb)
        self._recv(fin.at[1 - y, x, :, self.B], g, 2 * nz + 4, self.ynb)
        a, b = fin.at[y, :, :, self.A], fin.at[:, x, :, self.B]
        self._go(a, a, g, 2 * nz + 5, self.ynb)
        self._go(b, b, g, 2 * nz + 6, self.xnb)

    def s6(self, g):
        y, x, z, c = self.pos
        nz, fin = self.nz, self.fins[g]
        self._recv(fin.at[1 - y, :, :, self.A], g, 2 * nz + 5, self.ynb)
        self._recv(fin.at[:, 1 - x, :, self.B], g, 2 * nz + 6, self.xnb)

    def finish(self):
        for cp in self.started:
            cp.wait_send()

def grad_shapes(dp, D, a, b, c_):
    return [(2, dp, 2, a, D), (2, dp, 2, a, D), (dp, 2, 2, b, D), (2, 2, dp, c_, D)]

def reduce_shapes(nz, D, r, g):
    h = D // 2
    if g in ZFIRST:
        return (nz, 2, 2, r, D), (2, r, h), (2, r, h), (r, h), (r, h), (2, 2, r, D), (nz - 1, 2, 2, r, D)
    return (nz, 2, 2, r, D), (nz, 2, r, h), (nz, 2, r, h), (nz, r, h), (nz, r, h), (nz, r, D), (nz - 1, r, D)

class SmallSum:
    def __init__(self, nz, src, dst, first, second, sems):
        self.dp, self.src, self.dst, self.first, self.second, self.sem = nz * 2, src, dst, first, second, sems
        y, x, z, c = coords()
        self.me, self.seq, dp = z * 2 + c, y * 2 + x, nz * 2
        self.dpeer = [dev(y, x, (self.me + k) % dp // 2, (self.me + k) % 2) for k in range(1, dp)]
        self.speer = [dev(y, 1 - x, z, c), dev(1 - y, x, z, c), dev(1 - y, 1 - x, z, c)]
        self.sid = [y * 2 + 1 - x, (1 - y) * 2 + x, (1 - y) * 2 + 1 - x]
        self.started = []

    def peers(self):
        return self.dpeer + self.speer

    def _cp(self, src, dst, i, to):
        s, r = self.sem
        return pltpu.make_async_remote_copy(src_ref=src, dst_ref=dst, send_sem=s.at[i], recv_sem=r.at[i], device_id=to, device_id_type=MESH)

    def _go(self, *a):
        cp = self._cp(*a)
        cp.start()
        self.started.append(cp)

    def t0(self):
        for k in range(1, self.dp):
            self._go(self.src.at[(self.me + k) % self.dp], self.first.at[k - 1], k - 1, self.dpeer[k - 1])

    def t1(self):
        t = self.src[self.me]
        for k in range(1, self.dp):
            self._cp(self.first.at[k - 1], self.first.at[k - 1], k - 1, self.dpeer[k - 1]).wait_recv()
            t = t + self.first[k - 1]
        self.second[self.seq] = t
        for i in range(3):
            self._go(self.second.at[self.seq], self.second.at[self.seq], self.dp - 1 + i, self.speer[i])

    def t2(self):
        for i in range(3):
            self._cp(self.second.at[self.sid[i]], self.second.at[self.sid[i]], self.dp - 1 + i, self.speer[i]).wait_recv()
        self.dst[...] = (self.second[0] + self.second[1]) + (self.second[2] + self.second[3])

    def finish(self):
        for cp in self.started:
            cp.wait_send()

def small_scratch(dp):
    S = pltpu.SemaphoreType.DMA
    return [pltpu.VMEM((dp - 1, 8, 128), f32), pltpu.VMEM((4, 8, 128), f32), S((dp + 2,)), S((dp + 2,))]

class StateSum:
    def __init__(self, st, kt, sto, kto, sb, srec, krec, sems):
        self.st, self.kt, self.sto, self.kto, self.srec, self.krec, self.sem = st, kt, sto, kto, srec, krec, sems
        self.sb = st if sb is None else sb
        y, x, z, c = coords()
        self.peers = [dev(y, 1 - x, z, c), dev(1 - y, x, z, c), dev(1 - y, 1 - x, z, c)]
        self.sid = [y * 2 + 1 - x, (1 - y) * 2 + x, (1 - y) * 2 + 1 - x]
        self.me = y * 2 + x
        self.started = []

    def _cp(self, src, dst, i, k):
        s, r = self.sem
        return pltpu.make_async_remote_copy(src_ref=src, dst_ref=dst, send_sem=s.at[i, k], recv_sem=r.at[i, k], device_id=self.peers[k], device_id_type=MESH)

    def _go(self, *a):
        cp = self._cp(*a)
        cp.start()
        self.started.append(cp)

    def _recv(self, dst, i, k):
        self._cp(dst, dst, i, k).wait_recv()

    def start(self):
        if self.sb is not self.st:
            self.sb[...] = self.st[...].astype(self.sb.dtype)
        for k in range(3):
            self._go(self.sb.at[self.sid[k]], self.srec.at[k], 0, k)
            self._go(self.kt.at[self.sid[k]], self.krec.at[k], 1, k)

    def stage(self, i):
        (self.start, self.mid, self.end)[i]()

    def mid(self):
        me = self.me
        t, u = self.st[me], self.kt[me]
        for k in range(3):
            self._recv(self.srec.at[k], 0, k)
            self._recv(self.krec.at[k], 1, k)
            t = t + self.srec[k].astype(f32)
            u = u + self.krec[k]
        self.sto[me] = t.astype(self.sto.dtype)
        self.kto[me] = u
        for k in range(3):
            self._go(self.sto.at[me], self.sto.at[me], 2, k)
            self._go(self.kto.at[me], self.kto.at[me], 3, k)

    def end(self):
        for k in range(3):
            self._recv(self.sto.at[self.sid[k]], 2, k)
            self._recv(self.kto.at[self.sid[k]], 3, k)

    def finish(self):
        for cp in self.started:
            cp.wait_send()

class Flat:
    def __init__(self, ref, pairs):
        self.ref, self.pairs = ref, pairs

    def _at(self, i):
        f = i[0] * self.pairs + i[1]
        return (f // self.ref.shape[1], f % self.ref.shape[1])

    def __getitem__(self, i):
        return self.ref[self._at(i)]

    def __setitem__(self, i, v):
        self.ref[self._at(i)] = v

class FlatRow:
    def __init__(self, ref, pairs, n):
        self.ref, self.pairs, self.n = ref, pairs, n

    def _at(self, i):
        f = i[0] * self.pairs + i[1]
        return (f // self.n, pl.ds(f % self.n, 1), slice(None))

    def __getitem__(self, i):
        return self.ref[self._at(i)]

    def __setitem__(self, i, v):
        self.ref[self._at(i)] = v[:1]

def state_scratch(n, M, dtype):
    S = pltpu.SemaphoreType.DMA
    sb = [] if dtype == f32 else [pltpu.VMEM((4, n, 128, M), dtype)]
    return sb + [pltpu.VMEM((3, n, 128, M), dtype), pltpu.VMEM((3, 8, 2 * M), f32), S((4, 3)), S((4, 3))]

VM = pl.BlockSpec(memory_space=pltpu.VMEM)
ALLV = 67043328
COLS = 256


def call(body, ins, outs, scratch=(), name=None):
    return pl.pallas_call(
        body,
        out_shape=[jax.ShapeDtypeStruct(s, d) for s, d in outs],
        in_specs=[VM] * len(ins),
        out_specs=[VM] * len(outs),
        scratch_shapes=list(scratch),
        name=name,
        compiler_params=pltpu.CompilerParams(vmem_limit_bytes=ALLV),
    )(*ins)


def key_query_kernel(ns, loc, tok, kvw, qow, wf, vm, kp, vp, qp, kf, qf, st, kt):
    project(tok, kvw.at[0], kp)
    project(tok, kvw.at[1], vp)
    project(tok, qow.at[0], qp)
    key_side(kp, vp, wf, vm, kf, st, kt, ns, loc)
    query_side(qp, wf, qf)


def mix_kernel(ns, loc, tok, qow, qf, st, kt, ctx, den, ctxb, right, n1, inv1, resid):
    build_right(st, kt, right, qf.shape[2] // 2)
    mix_forward(qf, right, ctx, den, ctxb, ns, loc)
    attend_out(ctxb, qow.at[1], tok, n1, inv1, resid)


KEPT = 11
HEAD_ORDER = (
    "kv.1", "kv.2", "qo.1", "kv.3", "wi0.1", "kv.4", "qo.2", "pk", "wi1.1", "ks", "qo.3", "s.0",
    "wi0.2", "s.1", "wi0.3", "qo.4", "pq", "qs", "s.2", "wi1.2", "mx", "wi1.3", "wi0.4", "at",
    "wi1.4",
)


def run_order(order, compute, stage, state):
    for op in order:
        if op in compute:
            compute[op]()
        else:
            name, i = op.split(".")
            if name == "s":
                state(int(i))
            else:
                stage(NAMES.index(name), int(i))


def head_kernel(ns, loc, nz, *refs):
    local, (vloc, tok, rf, vm), refs = refs[:4], refs[4:8], refs[8:]
    whole, wz, vout, kept, refs = (*refs[:3], None), refs[3], refs[4], refs[5:5 + KEPT], refs[5 + KEPT:]
    sems, (kvs, qos, lsem), here, ksem, refs = refs[:13], refs[13:16], refs[16:16 + KEPT], refs[16 + KEPT], refs[17 + KEPT:]
    st, kt, sto, kto, sb, srec, krec, ss, sr, resid, wf = refs
    kp, vp, qp, kf, qf, ctx, den, ctxb, right, n1, inv1 = here
    P_, M = qf.shape[0], qf.shape[2] // 2
    n = ns * P_ // 4

    def keep(i):
        return pltpu.make_async_copy(here[i], kept[i], ksem.at[i])

    def load(i, dst):
        return pltpu.make_async_copy(whole[i], dst, lsem.at[i])
    G = Gather(nz, local, whole, sems, local[0].shape[2])
    S = StateSum(st, kt, sto, kto, sb, srec, krec, (ss, sr))
    entry_barrier([G.ynb, S.peers[0], S.peers[2]] + G.dpeer)
    G.start(wz, vloc, vout)
    wf[...] = feature_matrix(rf[...])

    def key_values():
        load(0, kvs).start()
        load(0, kvs).wait()
        project(tok, kvs.at[0], kp)
        project(tok, kvs.at[1], vp)
        for i in (0, 1): keep(i).start()

    def keys():
        kt[...] = jnp.zeros_like(kt)
        key_side(kp, vp, wf, vm, kf, Flat(st, P_), FlatRow(kt, P_, n), ns, loc)
        keep(3).start()

    def queries():
        load(1, qos).start()
        load(1, qos).wait()
        project(tok, qos.at[0], qp)
        keep(2).start()

    def query_features():
        query_side(qp, wf, qf)
        keep(4).start()

    def mix():
        build_right(Flat(sto, P_), FlatRow(kto, P_, n), right, M)
        mix_forward(qf, right, ctx, den, ctxb, ns, loc)
        for i in (5, 6, 7, 8): keep(i).start()

    def attend():
        attend_out(ctxb, qos.at[1], tok, n1, inv1, resid)
        for i in (9, 10): keep(i).start()
    run_order(HEAD_ORDER, {"pk": key_values, "ks": keys, "pq": queries, "qs": query_features, "mx": mix, "at": attend}, G.stage, S.stage)
    S.finish()
    G.end(wz, vloc, vout)
    for i in range(KEPT): keep(i).wait()


def head(ns, loc, dp, packed, vloc, tok, rf, vm):
    T, D = tok.shape
    nz = dp // 2
    M = rf.shape[1]
    P_ = D // 128
    shp = grad_shapes(dp, D, packed[0].shape[2], packed[2].shape[2], packed[3].shape[2])
    n = ns * P_ // 4
    pm, pf = (P_, T, 128), (P_, T, 2 * M)
    kept = [(pm, bf)] * 3 + [(pf, bf)] * 2 + [(pm, f32)] * 2 + [((T, D), bf), ((ns, P_, 256, 2 * M), bf), ((T, D), f32), ((T, 128), f32)]
    S = pltpu.SemaphoreType.DMA
    hb = pl.BlockSpec(memory_space=pl.ANY)
    scratch = gather_sems(dp) + [pltpu.VMEM(shp[0], bf), pltpu.VMEM(shp[1], bf), S((2,))] + [pltpu.VMEM(a, t) for a, t in kept] + [S((KEPT,))]
    scratch += [pltpu.VMEM((4, n, 128, M), f32), pltpu.VMEM((4, 8, 2 * M), f32), pltpu.VMEM((4, n, 128, M), bf), pltpu.VMEM((4, 8, 2 * M), f32)]
    scratch += state_scratch(n, M, bf) + [pltpu.VMEM((T, D), f32), pltpu.VMEM((8 * HEAD, 2 * M), bf)]
    return pl.pallas_call(
        partial(head_kernel, ns, loc, nz),
        out_shape=[jax.ShapeDtypeStruct(a, bf) for a in shp[:3]] + [jax.ShapeDtypeStruct((nz - 1, packed[3].shape[2], D), bf), jax.ShapeDtypeStruct((dp,) + vloc.shape, f32)] + [jax.ShapeDtypeStruct(a, t) for a, t in kept],
        in_specs=[hb] * 5 + [VM] * 3, out_specs=[hb] * (5 + KEPT),
        scratch_shapes=scratch,
        name="head",
        compiler_params=pltpu.CompilerParams(collective_id=1, has_side_effects=True, vmem_limit_bytes=ALLV),
    )(*packed, vloc, tok, rf, vm)


def ffn_kernel(nz, *refs):
    (vec, *given, win), wout, refs = refs[:6], refs[6:8 if nz else 7], refs[8 if nz else 7:]
    (gr1, gattn, sums, outh, gwin), refs = refs[:5], refs[5:]
    gwout, refs = refs[:6 if nz else 1], refs[6 if nz else 1:]
    (wi, wu, gwi, gwu, act, gp, hlow, acc, gr2, gffn, tr, n1, inv1, vm, cot, out, lsem, ssem, gsem), sems = refs[:19], refs[19:]
    sibs, sems = (sems[:2], sems[2:]) if nz else ((), sems)
    J, _, C = act.shape

    def rows(j): return ds(j, C)
    def load(j):
        return pltpu.make_async_copy(win.at[rows(j)], wi.at[rows(j)], lsem.at[j])
    def store(j):
        return pltpu.make_async_copy(gwi.at[rows(j)], gwin.at[rows(j)], ssem.at[j])
    def start_load(j, _):
        load(j).start()
        return 0
    def forward(j, _):
        load(j).wait()
        ffn_chunk(j, hlow, wi, act, gp)
        return 0
    def output(j, _):
        ffn_output(j, act, wu, acc, False)
        return 0
    def out_grad(j, _):
        ffn_out_grad(j, tr, act, gwu)
        return 0
    def backward(j, first):
        ffn_backward(j, gffn, hlow, wi, wu, gp, gwi, acc, first)
        store(j).start()
        return 0
    def some_backward(lo, hi):
        lax.fori_loop(lo, hi, lambda j, _: backward(j, False), 0)
    def end_store(j, _):
        store(j).wait()
        return 0
    here = [pltpu.make_async_copy(a, b, gsem.at[i]) for i, (a, b) in enumerate(zip(given, (n1, inv1, vm, cot)))]
    done_out = pltpu.make_async_copy(out, outh, gsem.at[4])

    def begin():
        for cp in here: cp.start()
        lax.fori_loop(0, J, start_load, 0)
        for cp in here: cp.wait()
        hidden_rows(n1, vec, hlow)
    if nz:
        wz, loc = wout
        r = loc.shape[2] // 2
        G = Gather(nz, (None, None, None, loc), (None, None, None, wu), sems[2:], r)
        entry_barrier([G.ynb, G.xnb, G.sib])
        G.relay(wz)
        begin()
        lax.fori_loop(0, J // 2, forward, 0)
        G.st2(EARLY)
        lax.fori_loop(J // 2, J - J // 6, forward, 0)
        G.st2(EARLY + 1)
        for g in (EARLY, EARLY + 1):
            for k in range(1, nz): G._wz_local(wz, g, k).wait()
        G.st3(EARLY)
        lax.fori_loop(J - J // 6, J, forward, 0)
        G.st3(EARLY + 1)
        G.done(EARLY)
        G.done(EARLY + 1)
    else:
        whole = pltpu.make_async_copy(wout[0], wu, ssem.at[0])
        whole.start()
        begin()
        lax.fori_loop(0, J, forward, 0)
        whole.wait()
    ffn_output(0, act, wu, acc, True)
    lax.fori_loop(1, J, output, 0)
    second_norm(acc, n1, vec, vm, cot, out, gr2, gffn, sums)
    done_out.start()
    tr[...] = gffn[...].T
    lax.fori_loop(0, J, out_grad, 0)
    if nz:
        sc = [()] * EARLY + [(sibs[0], *gwout[1:3]), (sibs[1], *gwout[4:])]
        kept = [pltpu.make_async_copy(sibs[i], gwout[3 * i], gsem.at[5 + i]) for i in range(2)]
        R = Reduce(nz, (None, None, None, gwu), (None,) * NG, sc, sems[:2], None, None, r)
        R.s0(EARLY)
        R.s0(EARLY + 1)
        backward(0, True)
        some_backward(1, J // 4)
        R.s1(EARLY)
        kept[0].start()
        some_backward(J // 4, J // 2)
        R.s1(EARLY + 1)
        kept[1].start()
        some_backward(J // 2, J)
    else:
        backward(0, True)
        some_backward(1, J)
    first_norm_back(acc, gr2, n1, inv1, vec, gr1, gattn, sums)
    if nz:
        for g in (EARLY, EARLY + 1): R.recv1(g)
        G.finish()
        R.finish()
        for cp in kept: cp.wait()
    done_out.wait()
    lax.fori_loop(0, J, end_store, 0)
    if not nz:
        cp = pltpu.make_async_copy(gwu, gwout[0], lsem.at[0])
        cp.start()
        cp.wait()


def ffn(n1, inv1, vec, vm, cot, win, wout, dp=0):
    T, D = n1.shape
    FF = win.shape[0]
    J = FF // COLS
    nz = dp // 2
    hb = pl.BlockSpec(memory_space=pl.ANY)
    S = pltpu.SemaphoreType.DMA
    ws, us, ch = (FF, D), (FF // D, D, D), (J, T, COLS)
    gs = (2, 2, dp, D // dp, D) if dp else us
    part_sums = [a for g in (EARLY, EARLY + 1) for a in reduce_shapes(nz, D, D // dp // 2, g)[:3]] if dp else [us]
    outs = [((T, D), f32), ((T, D), bf), ((4, 8, D), f32), ((T, D), bf), (ws, bf)] + [(a, bf) for a in part_sums]
    scratch = [(ws, bf), (gs, bf), (ws, bf), (gs, bf), (ch, bf), (ch, bf), ((T, D), bf), ((T, D), f32), ((T, D), f32), ((T, D), bf), ((D, T), bf)]
    scratch += [(n1.shape, f32), (inv1.shape, f32), (vm.shape, f32), ((T, D), bf), ((T, D), bf)]
    sems = [pltpu.VMEM(part_sums[0], bf)] * 2 + [S((NG, 2 * nz + 7)), S((NG, 2 * nz + 7))] + gather_sems(dp) if dp else []
    remote = dict(collective_id=3, has_side_effects=True) if dp else {}
    return pl.pallas_call(
        partial(ffn_kernel, nz),
        out_shape=[jax.ShapeDtypeStruct(a, t) for a, t in outs],
        in_specs=[VM] + [hb] * (5 + len(wout)), out_specs=[VM] * 3 + [hb] * 2 + ([hb, VM, VM] * 2 if dp else [hb]),
        scratch_shapes=[pltpu.VMEM(a, t) for a, t in scratch] + [S((J,)), S((J,)), S((7,))] + sems,
        name="ffn",
        compiler_params=pltpu.CompilerParams(vmem_limit_bytes=ALLV, **remote),
    )(vec, n1, inv1, vm, cot, win, *wout)


def mix_back_kernel(ns, loc, gattn, qow, ctxb, ctx, den, qp, qf, right, fbm, tok, gqo, gq, gst, gkt, tr):
    tr[...] = gattn[...].T
    weight_grad(tr, ctxb, gqo.at[1])
    mix_back_query(gattn, qow.at[1], qp, qf, right, ctx, den, fbm, gst, gkt, gq, ns, loc)
    weight_grad_pairs(gq, tok, gqo.at[0])


LATE = 11
TAIL_ORDER = (
    "wu1.2", "mq", "s.0", "gq", "wi0.0", "wo", "wu1.3", "wu0.2", "wi1.0", "wi0.1", "qo.0", "tq",
    "s.1", "wi1.1", "qo.1", "s.2", "mk", "wu0.3", "gkv", "kv.0", "wi1.2", "qo.2", "kv.1", "wi0.2",
    "wi1.3", "wu0.4", "qo.3", "kv.2", "wi1.4", "wu1.4", "wi0.3", "kv.3", "wu0.5", "qo.4", "wu1.5", "wi0.4",
    "wi1.5", "wi0.5", "wu0.6", "wu1.6", "kv.4", "qo.5", "wi1.6", "tk", "kv.5", "wi0.6", "kv.6", "qo.6",
)


def tail_kernel(ns, loc, nz, *refs):
    (gattn, ctxb, small, rf), refs = refs[:4], refs[4:]
    (gwin, gr1, *part_sums), refs = refs[:8], refs[8:]
    late, refs = refs[:LATE], refs[LATE:]
    tg, fins, sout, refs = refs[0], refs[1:5], refs[5], refs[6:]
    there, lsem, refs = refs[:LATE], refs[LATE], refs[LATE + 1:]
    (gkv, gqo, *own, gq, gk, gv, tr, gst, gkt, sto, kto), refs = refs[:12], refs[12:]
    (sb, srec, krec, ss, sr), refs = refs[:5], refs[5:]
    scratch, refs = [refs[g * 7:(g + 1) * 7] for g in range(NG)], refs[7 * NG:]
    rsend, rrecv, osem, sfirst, ssecond, qsend, qrecv, fbm = refs
    qow, qp, qf, right, ctx, den, tok, kp, vp, kf, kvw = there
    P_ = gq.shape[0]
    n = ns * P_ // 4

    def load(i):
        return pltpu.make_async_copy(late[i], there[i], lsem.at[i])
    grl = pltpu.make_async_copy(gr1, tg, lsem.at[LATE])
    early = [pltpu.make_async_copy(part_sums[i], scratch[EARLY + i // 3][i % 3], lsem.at[LATE + 1 + i]) for i in range(6)]
    for cp in early: cp.start()
    for i in range(LATE): load(i).start()
    grl.start()
    R = Reduce(nz, (gkv, gqo, gwin, None), (None, None, *own, None, None), scratch, (rsend, rrecv), osem, fins, gkv.shape[3])
    Q = SmallSum(nz, small, sout, sfirst, ssecond, (qsend, qrecv))
    S = StateSum(gst, gkt, sto, kto, sb, srec, krec, (ss, sr))
    entry_barrier(S.peers + Q.dpeer)
    Q.t0()
    fbm[...] = feature_pull(rf[...])
    wait_for = iter(range(LATE))

    def need(n):
        for _ in range(n): load(next(wait_for)).wait()

    def output_grad():
        tr[...] = gattn[...].T
        weight_grad_units(tr, ctxb, gqo.at[1])

    def mix_query():
        need(7)
        gkt[...] = jnp.zeros_like(gkt)
        mix_back_query(gattn, qow.at[1], qp, qf, right, ctx, den, fbm, Flat(gst, P_), FlatRow(gkt, P_, n), gq, ns, loc)

    def query_token():
        grl.wait()
        token_grad_query(gq, qow.at[0], tg)

    def mix_key():
        need(4)
        mix_back_key(kp, vp, kf, Flat(sto, P_), FlatRow(kto, P_, n), fbm, gk, gv, ns, loc)

    def key_grads():
        weight_grad_pairs_units(gk, tok, gkv.at[0])
        weight_grad_pairs_units(gv, tok, gkv.at[1])
        Q.t1()
    compute = {
        "wo": output_grad, "mq": mix_query, "gq": lambda: weight_grad_pairs_units(gq, tok, gqo.at[0]), "tq": query_token, "mk": mix_key,
        "gkv": key_grads, "tk": lambda: token_grad_keys(gk, gv, kvw.at[0], kvw.at[1], tg),
    }

    def stage(g, i):
        if g >= EARLY and i == 2:
            for cp in early[(g - EARLY) * 3:(g - EARLY) * 3 + 3]: cp.wait()
        R.stage(g, i)
    run_order(TAIL_ORDER, compute, stage, S.stage)
    Q.t2()
    S.finish()
    Q.finish()
    R.finish()


def tail(ns, loc, dp, gattn, ctxb, small, rf, gwin, gr1, part_sums, late):
    T, D = gattn.shape
    nz = dp // 2
    qf = late[2]
    P_, M = qf.shape[0], qf.shape[2] // 2
    part, ff = D // dp, gwin.shape[0]
    rows = (part // 2, part // 2, ff // dp // 4, part)
    shp = grad_shapes(dp, D, rows[0], rows[2], rows[3])
    n = ns * P_ // 4
    S = pltpu.SemaphoreType.DMA
    pm = pltpu.VMEM((P_, T, 128), bf)
    scratch = [pltpu.VMEM(a.shape, a.dtype) for a in late] + [S((LATE + 7,))]
    scratch += [pltpu.VMEM(shp[0], bf), pltpu.VMEM(shp[1], bf)] + [pltpu.VMEM((nz, 2, 2, rows[0], D), bf)] * 2
    scratch += [pm, pm, pm, pltpu.VMEM((D, T), bf), pltpu.VMEM((4, n, 128, M), f32), pltpu.VMEM((4, 8, 2 * M), f32)]
    scratch += [pltpu.VMEM((4, n, 128, M), bf), pltpu.VMEM((4, 8, 2 * M), f32)] + state_scratch(n, M, bf)
    scratch += [pltpu.VMEM(a, bf) for g in range(NG) for a in reduce_shapes(nz, D, rows[0], g)] + [S((NG, 2 * nz + 7)), S((NG, 2 * nz + 7)), S((NG, nz))] + small_scratch(dp) + [pltpu.VMEM((2 * M, 4 * HEAD), bf)]
    hb = pl.BlockSpec(memory_space=pl.ANY)
    return pl.pallas_call(
        partial(tail_kernel, ns, loc, nz),
        out_shape=[jax.ShapeDtypeStruct((T, D), f32)] + [jax.ShapeDtypeStruct((2, 2, r, D), bf) for r in rows] + [jax.ShapeDtypeStruct(small.shape[1:], f32)],
        in_specs=[VM] * 4 + [hb] * (8 + LATE), out_specs=[VM] * 6,
        scratch_shapes=scratch,
        name="tail",
        compiler_params=pltpu.CompilerParams(collective_id=2, has_side_effects=True, vmem_limit_bytes=ALLV),
    )(gattn, ctxb, small, rf, gwin.reshape(shp[2]), gr1, *part_sums, *late)


def last_kernel(ns, loc, kp, vp, kf, gst, gkt, fbm, gr1, gq, kvw, qow, tok, gkv, tg, gk, gv):
    mix_back_key(kp, vp, kf, gst, gkt, fbm, gk, gv, ns, loc)
    weight_grad_pairs(gk, tok, gkv.at[0])
    weight_grad_pairs(gv, tok, gkv.at[1])
    token_grad(gr1, gq, gk, gv, qow.at[0], kvw.at[0], kvw.at[1], tg)


def shards(tokens, lengths, random_features, w_query, w_key, w_value, w_output, w_in, w_out, ln1_gain, ln1_bias, ln2_gain, ln2_bias, cotangent):
    ns, loc, D = tokens.shape
    T = ns * loc
    dp, parts = lax.axis_size("dp"), lax.axis_size("seq")
    part = w_query.shape[1]
    FF = w_out.shape[0]
    M = random_features.shape[1]
    P_ = D // 128
    fast = parts == 4 and dp == 8 and part % 32 == 0 and D == part * dp and part <= 128 and ns * P_ % 4 == 0 and ns * P_ <= 32 and FF == 4 * D
    pos = lax.axis_index("seq") * loc + jnp.arange(loc, dtype=jnp.int32)
    valid = (pos[None, :] < lengths[:, None]).astype(f32).reshape(T, 1)
    vm = jnp.broadcast_to(valid, (T, 128))
    tok, cot = tokens.reshape(T, D), cotangent.reshape(T, D)
    vloc = jnp.stack([ln1_gain, ln1_bias, ln2_gain, ln2_bias]).astype(f32)
    pm, pf, stt, ktt = (P_, T, 128), (P_, T, 2 * M), (ns, P_, 128, M), (ns, P_, 8, 2 * M)
    if fast:
        vloc = jnp.pad(vloc, ((0, 4), (0, 128 - part)))
        packed = pack(w_query, w_key, w_value, w_output, w_in, w_out)
        kvw, qow, win, wz, vec, *kept = head(ns, loc, dp, packed, vloc, tok, random_features, vm)
        wout = wz, packed[3]
        kp, vp, qp, kf, qf, ctx, den, ctxb, right, n1, inv1 = kept
        vec = jnp.transpose(vec[:, :, :part], (1, 0, 2)).reshape(8, D)
    else:
        vec = jnp.pad(lax.all_gather(vloc, "dp", axis=1, tiled=True), ((0, 4), (0, 0)))
        def full(w):
            return lax.all_gather(w, "dp", axis=1, tiled=True).T
        kvw, qow = jnp.stack([full(w_key), full(w_value)]), jnp.stack([full(w_query), full(w_output)])
        win = full(w_in)
        wout = (jnp.transpose(full(w_out).reshape(D, FF // D, D), (1, 0, 2)),)
    kvw, qow, win = kvw.reshape(2, D, D), qow.reshape(2, D, D), win.reshape(FF, D)
    if not fast:
        wf, fbm = feature_matrix(random_features), feature_pull(random_features)
        kp, vp, qp, kf, qf, st, kt = call(
            partial(key_query_kernel, ns, loc), (tok, kvw, qow, wf, vm),
            [(pm, bf)] * 3 + [(pf, bf)] * 2 + [(stt, f32), (ktt, f32)], name="key_query")
        st, kt = lax.psum((st, kt), "seq")
        ctx, den, ctxb, right, n1, inv1 = call(
            partial(mix_kernel, ns, loc), (tok, qow, qf, st, kt),
            [(pm, f32), (pm, f32), ((T, D), bf), ((ns, P_, 256, 2 * M), bf), ((T, D), f32), ((T, 128), f32)],
            [pltpu.VMEM((T, D), f32)], name="mix")
    gr1, gattn, sums, out, gwin, *gwout = ffn(n1, inv1, vec, vm, cot, win, wout, dp if fast else 0)
    small = jnp.sum(jnp.concatenate([sums[2:], sums[:2]]), 1)
    if fast:
        small = jnp.transpose(jnp.pad(small.reshape(4, dp, part), ((0, 4), (0, 0), (0, 128 - part))), (1, 0, 2))
        tg, kvg, qog, wig, wug, small = tail(ns, loc, dp, gattn, ctxb, small, random_features, gwin, gr1, gwout, (qow, qp, qf, right, ctx, den, tok, kp, vp, kf, kvw))
        small = small[:, :part]
        wk_g, wv_g, wq_g, wo_g = kvg[0].reshape(part, D).T, kvg[1].reshape(part, D).T, qog[0].reshape(part, D).T, qog[1].reshape(part, D).T
        wi_g = wig.reshape(FF // dp, D).T
        wu_g = jnp.transpose(wug.reshape(FF // D, part, D), (0, 2, 1)).reshape(FF, part)
        grads = (wq_g, wk_g, wv_g, wo_g, wi_g, wu_g)
    else:
        gqo, gq, gst, gkt = call(
            partial(mix_back_kernel, ns, loc), (gattn, qow, ctxb, ctx, den, qp, qf, right, fbm, tok),
            [((2, D, D), bf), (pm, bf), (stt, f32), (ktt, f32)], [pltpu.VMEM((D, T), bf)], name="mix_back")
        gst, gkt = lax.psum((gst, gkt), "seq")
        gkv, tg = call(
            partial(last_kernel, ns, loc), (kp, vp, kf, gst, gkt, fbm, gr1, gq, kvw, qow, tok),
            [((2, D, D), bf), ((T, D), f32)], [pltpu.VMEM(pm, bf), pltpu.VMEM(pm, bf)], name="last")
        small = lax.psum(small, ("seq", "dp"))
        small = lax.dynamic_slice_in_dim(small, lax.axis_index("dp") * part, part, 1)
        whole = (gqo[0].T, gkv[0].T, gkv[1].T, gqo[1].T, gwin.T, jnp.transpose(gwout[0], (0, 2, 1)).reshape(FF, D))
        grads = tuple(lax.psum(lax.psum_scatter(g, "dp", scatter_dimension=1, tiled=True), "seq") for g in whole)
    return (out.reshape(tokens.shape), tg.reshape(tokens.shape), *(g.astype(f32) for g in grads), small[0], small[1], small[2], small[3])


def solution(mesh):
    rows, cols, vecs = P("dp", "seq", None), P(None, "dp"), P("dp")
    return jax.shard_map(
        shards,
        mesh=mesh,
        in_specs=(rows, vecs, P(), *([cols] * 6), *([vecs] * 4), rows),
        out_specs=(rows, rows, *([cols] * 6), *([vecs] * 4)),
        check_vma=False,
    )
```

time: 415 us -> 246 us (0.59)
  Pallas kernels: 326 us -> 224 us
  blocking collectives: 59.4 us -> 0 us
  local copies, waits for them, and re-layouts: 19.9 us -> 14 us
    pallas_call x8 -> x3, Pallas kernels: 326 us -> 224 us  [the longest x1 89.2 us: tail(): pl.pallas_call(partial(tail_kernel, ns, loc, nz), out_shape=[jax.ShapeDty...]
    psum x1 -> x0, blocking collectives: 46 us -> none  [shards(): small = lax.psum(small, ('seq', 'dp'))]
    all_gather x1 -> x0, blocking collectives: 13.5 us -> none  [shards(): lax.all_gather(jnp.stack([ln1_gain, ln1_bias, ln2_gain, ln2_bias]), 'dp',...]
    unnamed x45 -> x23, local copies, waits for them, and re-layouts: 9.15 us -> 2.26 us
where the time goes in v3:
time: 246 us; the launch traced here: 245 us
  Pallas kernels  224 us (91%)
  local copies, waits for them, and re-layouts  14 us (6%)
  other arithmetic  6.24 us (3%)
    pallas_call x1, Pallas kernels, tail(): pl.pallas_call(partial(tail_kernel, ns, loc, nz), out_shape=[jax.ShapeDty...  89.2 us
    pallas_call x1, Pallas kernels, head(): pl.pallas_call(partial(head_kernel, ns, loc, nz), out_shape=[jax.ShapeDty...  79.2 us
    pallas_call x1, Pallas kernels, ffn(): pl.pallas_call(partial(ffn_kernel, nz), out_shape=[jax.ShapeDtypeStruct(a...  55.9 us

profile of v3, /device:TPU:0, one launch (start us, length us, event | category | flops | bytes accessed | tf_op | source)
XLA Modules:
  0.0 245.3 jit_solution(16822051595996969233)
XLA Ops:
  0.7 0.8 fusion.5
  1.5 1.3 fusion.10.refs_4_
  2.8 0.8 broadcast_in_dim.2.refs_7_.refs_3_
  3.7 2.1 copy.31
  5.8 0.9 copy.41
  6.7 0.9 pad_maximum_fusion
  7.5 79.2 %head.1 = (bf16[2,8,2,48,768]{4,3,2,1,0:T(8,128)(2,1)}, bf16[2,8,2,48,768]{4,3,2,1,0:T(8,128)(2,1)}, bf16[8,2,2,96,768]{4,3,2,1,0:T(8,128)(2,1)}, bf16[3,96,768]...) custom-call(bf16[2,2,48,768]{3,2,1,0:T(8,128)(2,1)} %get-tuple-eleme, ...), custom_call_target="tpu_custom_call" | custom-call | tf_op jit(solution)/shard_map/head/pallas_call | solution.py:937
  86.8 0.8 slice_bitcast_fusion
  87.5 0.7 reshape.117.refs_0_
  88.2 55.9 %ffn.1 = (f32[512,768]{1,0:T(8,128)}, bf16[512,768]{1,0:T(8,128)(2,1)}, f32[4,8,768]{2,1,0:T(8,128)}, bf16[512,768]{1,0:T(8,128)(2,1)}, bf16[3072,768]{1,0:T(8,1...) custom-call(f32[8,768]{1,0:T(8,128)} %reshape.117.refs_0_, ...), custom_call_target="tpu_custom_call" | custom-call | tf_op jit(solution)/shard_map/ffn/pallas_call | solution.py:1066
  144.1 0.8 fusion.16
  145.1 0.6 pad_bitcast_fusion.refs_2_
  145.7 89.2 %tail.1 = (f32[512,768]{1,0:T(8,128)}, bf16[2,2,48,768]{3,2,1,0:T(8,128)(2,1)}, bf16[2,2,48,768]{3,2,1,0:T(8,128)(2,1)}, bf16[2,2,96,768]{3,2,1,0:T(8,128)(2,1)}...) custom-call(bf16[512,768]{1,0:T(8,128)(2,1)} %get-tuple-element.51.refs_0_, ...), custom_call_target="tpu_custom_call" | custom-call | tf_op jit(solution)/shard_map/tail/pallas_call | solution.py:1178
  234.9 1.3 slice_bitcast_fusion.1
  236.2 1.0 fusion.14
  237.2 0.7 convert_bitcast_fusion.1
  238.0 0.7 convert_bitcast_fusion.4
  238.8 0.7 convert_bitcast_fusion.2
  239.5 0.7 convert_bitcast_fusion.3
  240.4 1.4 copy.35
  241.9 1.1 copy.38
  243.0 0.2 copy-done.1
  243.2 0.9 copy.44
  244.1 1.1 copy.45
  (28 shorter events, 0.4 us)
Async XLA Ops:
  0.6 5.1 %copy-start.4 = (bf16[3072,96]{0,1:T(8,128)(2,1)S(1)}, bf16[3072,96]{0,1:T(8,128)(2,1)}, u32[]{:S(2)}) copy-start(bf16[3072,96]{0,1:T(8,128)(2,1)} %param.22) | copy-start | bytes 1769476
  0.7 6.0 %copy-start.8 = (bf16[768,96]{0,1:T(8,128)(2,1)S(1)}, bf16[768,96]{0,1:T(8,128)(2,1)}, u32[]{:S(2)}) copy-start(bf16[768,96]{0,1:T(8,128)(2,1)} %param.20) | copy-start | bytes 442372
  0.7 6.0 %copy-start.6 = (bf16[768,96]{0,1:T(8,128)(2,1)S(1)}, bf16[768,96]{0,1:T(8,128)(2,1)}, u32[]{:S(2)}) copy-start(bf16[768,96]{0,1:T(8,128)(2,1)} %param.19) | copy-start | bytes 442372
  0.7 6.0 %copy-start.7 = (bf16[768,96]{0,1:T(8,128)(2,1)S(1)}, bf16[768,96]{0,1:T(8,128)(2,1)}, u32[]{:S(2)}) copy-start(bf16[768,96]{0,1:T(8,128)(2,1)} %param.18) | copy-start | bytes 442372
  0.7 6.0 %copy-start.9 = (bf16[768,96]{0,1:T(8,128)(2,1)S(1)}, bf16[768,96]{0,1:T(8,128)(2,1)}, u32[]{:S(2)}) copy-start(bf16[768,96]{0,1:T(8,128)(2,1)} %param.17) | copy-start | bytes 442372
  234.9 3.9 %copy-start.5 = (bf16[2,2,48,768]{3,2,1,0:T(8,128)(2,1)S(1)}, bf16[2,2,48,768]{3,2,1,0:T(8,128)(2,1)}, u32[]{:S(2)}) copy-start(bf16[2,2,48,768]{3,2,1,0:T(8,128)(2,1)} %get-tuple-element.74) | copy-start | bytes 884740
  234.9 5.4 %copy-start.3 = (bf16[2,2,96,768]{3,2,1,0:T(8,128)(2,1)S(1)}, bf16[2,2,96,768]{3,2,1,0:T(8,128)(2,1)}, u32[]{:S(2)}) copy-start(bf16[2,2,96,768]{3,2,1,0:T(8,128)(2,1)} %get-tuple-element.75) | copy-start | bytes 1769476
  240.4 1.4 copy-start.2
  241.9 1.3 copy-start.1
  241.9 2.2 copy-start

commit v4 on v3

--- a/solution.py
+++ b/solution.py
@@ -701,10 +701,10 @@
 
     def t0(self):
         for k in range(1, self.dp):
-            self._go(self.src.at[(self.me + k) % self.dp], self.first.at[k - 1], k - 1, self.dpeer[k - 1])
+            self._go(self.src, self.first.at[k - 1], k - 1, self.dpeer[k - 1])
 
     def t1(self):
-        t = self.src[self.me]
+        t = self.src[...]
         for k in range(1, self.dp):
             self._cp(self.first.at[k - 1], self.first.at[k - 1], k - 1, self.dpeer[k - 1]).wait_recv()
             t = t + self.first[k - 1]
@@ -721,9 +721,9 @@
         for cp in self.started:
             cp.wait_send()
 
-def small_scratch(dp):
+def small_scratch(dp, D):
     S = pltpu.SemaphoreType.DMA
-    return [pltpu.VMEM((dp - 1, 8, 128), f32), pltpu.VMEM((4, 8, 128), f32), S((dp + 2,)), S((dp + 2,))]
+    return [pltpu.VMEM((dp - 1, 8, D), f32), pltpu.VMEM((4, 8, D), f32), S((dp + 2,)), S((dp + 2,)), pltpu.VMEM((8, D), f32)]
 
 class StateSum:
     def __init__(self, st, kt, sto, kto, sb, srec, krec, sems):
@@ -944,11 +944,12 @@
     )(*packed, vloc, tok, rf, vm)
 
 
-def ffn_kernel(nz, *refs):
-    (vec, *given, win), wout, refs = refs[:6], refs[6:8 if nz else 7], refs[8 if nz else 7:]
+def ffn_kernel(nz, part, *refs):
+    (shards_, *given, win), wout, refs = refs[:6], refs[6:8 if nz else 7], refs[8 if nz else 7:]
     (gr1, gattn, sums, outh, gwin), refs = refs[:5], refs[5:]
     gwout, refs = refs[:6 if nz else 1], refs[6 if nz else 1:]
     (wi, wu, gwi, gwu, act, gp, hlow, acc, gr2, gffn, tr, n1, inv1, vm, cot, out, lsem, ssem, gsem), sems = refs[:19], refs[19:]
+    vec, sems = sems[0], sems[1:]
     sibs, sems = (sems[:2], sems[2:]) if nz else ((), sems)
     J, _, C = act.shape
 
@@ -985,6 +986,7 @@
     def begin():
         for cp in here: cp.start()
         lax.fori_loop(0, J, start_load, 0)
+        vec[...] = jnp.concatenate([shards_[d][:, :part] for d in range(shards_.shape[0])], 1)
         for cp in here: cp.wait()
         hidden_rows(n1, vec, hlow)
     if nz:
@@ -1064,10 +1066,10 @@
     sems = [pltpu.VMEM(part_sums[0], bf)] * 2 + [S((NG, 2 * nz + 7)), S((NG, 2 * nz + 7))] + gather_sems(dp) if dp else []
     remote = dict(collective_id=3, has_side_effects=True) if dp else {}
     return pl.pallas_call(
-        partial(ffn_kernel, nz),
+        partial(ffn_kernel, nz, D // vec.shape[0]),
         out_shape=[jax.ShapeDtypeStruct(a, t) for a, t in outs],
         in_specs=[VM] + [hb] * (5 + len(wout)), out_specs=[VM] * 3 + [hb] * 2 + ([hb, VM, VM] * 2 if dp else [hb]),
-        scratch_shapes=[pltpu.VMEM(a, t) for a, t in scratch] + [S((J,)), S((J,)), S((7,))] + sems,
+        scratch_shapes=[pltpu.VMEM(a, t) for a, t in scratch] + [S((J,)), S((J,)), S((7,)), pltpu.VMEM((8, D), f32)] + sems,
         name="ffn",
         compiler_params=pltpu.CompilerParams(vmem_limit_bytes=ALLV, **remote),
     )(vec, n1, inv1, vm, cot, win, *wout)
@@ -1090,7 +1092,7 @@
 
 
 def tail_kernel(ns, loc, nz, *refs):
-    (gattn, ctxb, small, rf), refs = refs[:4], refs[4:]
+    (gattn, ctxb, sums, rf), refs = refs[:4], refs[4:]
     (gwin, gr1, *part_sums), refs = refs[:8], refs[8:]
     late, refs = refs[:LATE], refs[LATE:]
     tg, fins, sout, refs = refs[0], refs[1:5], refs[5], refs[6:]
@@ -1098,7 +1100,7 @@
     (gkv, gqo, *own, gq, gk, gv, tr, gst, gkt, sto, kto), refs = refs[:12], refs[12:]
     (sb, srec, krec, ss, sr), refs = refs[:5], refs[5:]
     scratch, refs = [refs[g * 7:(g + 1) * 7] for g in range(NG)], refs[7 * NG:]
-    rsend, rrecv, osem, sfirst, ssecond, qsend, qrecv, fbm = refs
+    rsend, rrecv, osem, sfirst, ssecond, qsend, qrecv, ssrc, fbm = refs
     qow, qp, qf, right, ctx, den, tok, kp, vp, kf, kvw = there
     P_ = gq.shape[0]
     n = ns * P_ // 4
@@ -1111,9 +1113,12 @@
     for i in range(LATE): load(i).start()
     grl.start()
     R = Reduce(nz, (gkv, gqo, gwin, None), (None, None, *own, None, None), scratch, (rsend, rrecv), osem, fins, gkv.shape[3])
-    Q = SmallSum(nz, small, sout, sfirst, ssecond, (qsend, qrecv))
+    Q = SmallSum(nz, ssrc, sout, sfirst, ssecond, (qsend, qrecv))
     S = StateSum(gst, gkt, sto, kto, sb, srec, krec, (ss, sr))
     entry_barrier(S.peers + Q.dpeer)
+    ssrc[...] = jnp.zeros_like(ssrc)
+    for i in range(4):
+        ssrc[i:i + 1, :] = jnp.sum(sums[i], 0, keepdims=True)
     Q.t0()
     fbm[...] = feature_pull(rf[...])
     wait_for = iter(range(LATE))
@@ -1158,7 +1163,7 @@
     R.finish()
 
 
-def tail(ns, loc, dp, gattn, ctxb, small, rf, gwin, gr1, part_sums, late):
+def tail(ns, loc, dp, gattn, ctxb, sums, rf, gwin, gr1, part_sums, late):
     T, D = gattn.shape
     nz = dp // 2
     qf = late[2]
@@ -1173,16 +1178,16 @@
     scratch += [pltpu.VMEM(shp[0], bf), pltpu.VMEM(shp[1], bf)] + [pltpu.VMEM((nz, 2, 2, rows[0], D), bf)] * 2
     scratch += [pm, pm, pm, pltpu.VMEM((D, T), bf), pltpu.VMEM((4, n, 128, M), f32), pltpu.VMEM((4, 8, 2 * M), f32)]
     scratch += [pltpu.VMEM((4, n, 128, M), bf), pltpu.VMEM((4, 8, 2 * M), f32)] + state_scratch(n, M, bf)
-    scratch += [pltpu.VMEM(a, bf) for g in range(NG) for a in reduce_shapes(nz, D, rows[0], g)] + [S((NG, 2 * nz + 7)), S((NG, 2 * nz + 7)), S((NG, nz))] + small_scratch(dp) + [pltpu.VMEM((2 * M, 4 * HEAD), bf)]
+    scratch += [pltpu.VMEM(a, bf) for g in range(NG) for a in reduce_shapes(nz, D, rows[0], g)] + [S((NG, 2 * nz + 7)), S((NG, 2 * nz + 7)), S((NG, nz))] + small_scratch(dp, D) + [pltpu.VMEM((2 * M, 4 * HEAD), bf)]
     hb = pl.BlockSpec(memory_space=pl.ANY)
     return pl.pallas_call(
         partial(tail_kernel, ns, loc, nz),
-        out_shape=[jax.ShapeDtypeStruct((T, D), f32)] + [jax.ShapeDtypeStruct((2, 2, r, D), bf) for r in rows] + [jax.ShapeDtypeStruct(small.shape[1:], f32)],
+        out_shape=[jax.ShapeDtypeStruct((T, D), f32)] + [jax.ShapeDtypeStruct((2, 2, r, D), bf) for r in rows] + [jax.ShapeDtypeStruct((8, D), f32)],
         in_specs=[VM] * 4 + [hb] * (8 + LATE), out_specs=[VM] * 6,
         scratch_shapes=scratch,
         name="tail",
         compiler_params=pltpu.CompilerParams(collective_id=2, has_side_effects=True, vmem_limit_bytes=ALLV),
-    )(gattn, ctxb, small, rf, gwin.reshape(shp[2]), gr1, *part_sums, *late)
+    )(gattn, ctxb, sums, rf, gwin.reshape(shp[2]), gr1, *part_sums, *late)
 
 
 def last_kernel(ns, loc, kp, vp, kf, gst, gkt, fbm, gr1, gq, kvw, qow, tok, gkv, tg, gk, gv):
@@ -1213,9 +1218,8 @@
         kvw, qow, win, wz, vec, *kept = head(ns, loc, dp, packed, vloc, tok, random_features, vm)
         wout = wz, packed[3]
         kp, vp, qp, kf, qf, ctx, den, ctxb, right, n1, inv1 = kept
-        vec = jnp.transpose(vec[:, :, :part], (1, 0, 2)).reshape(8, D)
     else:
-        vec = jnp.pad(lax.all_gather(vloc, "dp", axis=1, tiled=True), ((0, 4), (0, 0)))
+        vec = jnp.pad(lax.all_gather(vloc, "dp", axis=1, tiled=True), ((0, 4), (0, 0)))[None]
         def full(w):
             return lax.all_gather(w, "dp", axis=1, tiled=True).T
         kvw, qow = jnp.stack([full(w_key), full(w_value)]), jnp.stack([full(w_query), full(w_output)])
@@ -1233,11 +1237,8 @@
             [(pm, f32), (pm, f32), ((T, D), bf), ((ns, P_, 256, 2 * M), bf), ((T, D), f32), ((T, 128), f32)],
             [pltpu.VMEM((T, D), f32)], name="mix")
     gr1, gattn, sums, out, gwin, *gwout = ffn(n1, inv1, vec, vm, cot, win, wout, dp if fast else 0)
-    small = jnp.sum(jnp.concatenate([sums[2:], sums[:2]]), 1)
     if fast:
-        small = jnp.transpose(jnp.pad(small.reshape(4, dp, part), ((0, 4), (0, 0), (0, 128 - part))), (1, 0, 2))
-        tg, kvg, qog, wig, wug, small = tail(ns, loc, dp, gattn, ctxb, small, random_features, gwin, gr1, gwout, (qow, qp, qf, right, ctx, den, tok, kp, vp, kf, kvw))
-        small = small[:, :part]
+        tg, kvg, qog, wig, wug, small = tail(ns, loc, dp, gattn, ctxb, sums, random_features, gwin, gr1, gwout, (qow, qp, qf, right, ctx, den, tok, kp, vp, kf, kvw))
         wk_g, wv_g, wq_g, wo_g = kvg[0].reshape(part, D).T, kvg[1].reshape(part, D).T, qog[0].reshape(part, D).T, qog[1].reshape(part, D).T
         wi_g = wig.reshape(FF // dp, D).T
         wu_g = jnp.transpose(wug.reshape(FF // D, part, D), (0, 2, 1)).reshape(FF, part)
@@ -1250,11 +1251,11 @@
         gkv, tg = call(
             partial(last_kernel, ns, loc), (kp, vp, kf, gst, gkt, fbm, gr1, gq, kvw, qow, tok),
             [((2, D, D), bf), ((T, D), f32)], [pltpu.VMEM(pm, bf), pltpu.VMEM(pm, bf)], name="last")
-        small = lax.psum(small, ("seq", "dp"))
-        small = lax.dynamic_slice_in_dim(small, lax.axis_index("dp") * part, part, 1)
+        small = lax.psum(jnp.sum(sums, 1), ("seq", "dp"))
         whole = (gqo[0].T, gkv[0].T, gkv[1].T, gqo[1].T, gwin.T, jnp.transpose(gwout[0], (0, 2, 1)).reshape(FF, D))
         grads = tuple(lax.psum(lax.psum_scatter(g, "dp", scatter_dimension=1, tiled=True), "seq") for g in whole)
-    return (out.reshape(tokens.shape), tg.reshape(tokens.shape), *(g.astype(f32) for g in grads), small[0], small[1], small[2], small[3])
+    small = lax.dynamic_slice_in_dim(small, lax.axis_index("dp") * part, part, 1)
+    return (out.reshape(tokens.shape), tg.reshape(tokens.shape), *(g.astype(f32) for g in grads), small[2], small[3], small[0], small[1])
 
 
 def solution(mesh):

time: 246 us -> 244 us (level)
  local copies, waits for them, and re-layouts: 14 us -> 11 us
where the time goes in v4:
time: 244 us; the launch traced here: 243 us
  Pallas kernels  225 us (92%)
  local copies, waits for them, and re-layouts  11 us (5%)
  other arithmetic  6.21 us (3%)
    pallas_call x1, Pallas kernels, tail(): pl.pallas_call(partial(tail_kernel, ns, loc, nz), out_shape=[jax.ShapeDty...  90.1 us
    pallas_call x1, Pallas kernels, head(): pl.pallas_call(partial(head_kernel, ns, loc, nz), out_shape=[jax.ShapeDty...  79.2 us
    pallas_call x1, Pallas kernels, ffn(): pl.pallas_call(partial(ffn_kernel, nz, D // vec.shape[0]), out_shape=[jax...  55.9 us

profile of v4, /device:TPU:0, one launch (start us, length us, event | category | flops | bytes accessed | tf_op | source)
XLA Modules:
  0.0 243.2 jit_solution(17698137915303266225)
XLA Ops:
  0.6 0.0 copy-start.4
  0.7 0.8 fusion.5
  1.5 1.3 fusion.10.refs_4_
  2.8 0.8 broadcast_in_dim.2.refs_7_.refs_3_
  3.7 2.1 copy.26
  5.8 0.9 copy.34
  6.7 0.9 pad_maximum_fusion
  7.5 79.2 %head.1 = (bf16[2,8,2,48,768]{4,3,2,1,0:T(8,128)(2,1)}, bf16[2,8,2,48,768]{4,3,2,1,0:T(8,128)(2,1)}, bf16[8,2,2,96,768]{4,3,2,1,0:T(8,128)(2,1)}, bf16[3,96,768]...) custom-call(bf16[2,2,48,768]{3,2,1,0:T(8,128)(2,1)} %get-tuple-eleme, ...), custom_call_target="tpu_custom_call" | custom-call | tf_op jit(solution)/shard_map/head/pallas_call | solution.py:937
  86.8 55.9 %ffn.1 = (f32[512,768]{1,0:T(8,128)}, bf16[512,768]{1,0:T(8,128)(2,1)}, f32[4,8,768]{2,1,0:T(8,128)}, bf16[512,768]{1,0:T(8,128)(2,1)}, bf16[3072,768]{1,0:T(8,1...) custom-call(f32[8,8,128]{2,1,0:T(8,128)} %get-tuple-element.45.refs_, ...), custom_call_target="tpu_custom_call" | custom-call | tf_op jit(solution)/shard_map/ffn/pallas_call | solution.py:1068
  142.7 90.1 %tail.1 = (f32[512,768]{1,0:T(8,128)}, bf16[2,2,48,768]{3,2,1,0:T(8,128)(2,1)}, bf16[2,2,48,768]{3,2,1,0:T(8,128)(2,1)}, bf16[2,2,96,768]{3,2,1,0:T(8,128)(2,1)}...) custom-call(bf16[512,768]{1,0:T(8,128)(2,1)} %get-tuple-element.51.refs_0_, ...), custom_call_target="tpu_custom_call" | custom-call | tf_op jit(solution)/shard_map/tail/pallas_call | solution.py:1183
  232.8 0.9 constant_dynamic-slice_fusion
  233.7 0.5 slice_bitcast_fusion
  234.2 1.0 fusion.14
  235.2 0.7 convert_bitcast_fusion.1
  236.0 0.7 convert_bitcast_fusion.4
  236.7 0.7 convert_bitcast_fusion.2
  237.5 0.7 convert_bitcast_fusion.3
  238.2 0.1 bitcast_convert_fusion
  238.4 1.4 copy.28
  239.8 0.1 convert_bitcast_fusion
  239.9 1.1 copy.31
  241.0 0.2 copy-done.1
  241.2 0.9 copy.37
  242.1 1.1 copy.38
  (21 shorter events, 0.1 us)
Async XLA Ops:
  0.6 5.1 %copy-start.4 = (bf16[3072,96]{0,1:T(8,128)(2,1)S(1)}, bf16[3072,96]{0,1:T(8,128)(2,1)}, u32[]{:S(2)}) copy-start(bf16[3072,96]{0,1:T(8,128)(2,1)} %param.22) | copy-start | bytes 1769476
  0.7 6.0 %copy-start.8 = (bf16[768,96]{0,1:T(8,128)(2,1)S(1)}, bf16[768,96]{0,1:T(8,128)(2,1)}, u32[]{:S(2)}) copy-start(bf16[768,96]{0,1:T(8,128)(2,1)} %param.20) | copy-start | bytes 442372
  0.7 6.0 %copy-start.6 = (bf16[768,96]{0,1:T(8,128)(2,1)S(1)}, bf16[768,96]{0,1:T(8,128)(2,1)}, u32[]{:S(2)}) copy-start(bf16[768,96]{0,1:T(8,128)(2,1)} %param.19) | copy-start | bytes 442372
  0.7 6.0 %copy-start.7 = (bf16[768,96]{0,1:T(8,128)(2,1)S(1)}, bf16[768,96]{0,1:T(8,128)(2,1)}, u32[]{:S(2)}) copy-start(bf16[768,96]{0,1:T(8,128)(2,1)} %param.18) | copy-start | bytes 442372
  0.7 6.0 %copy-start.9 = (bf16[768,96]{0,1:T(8,128)(2,1)S(1)}, bf16[768,96]{0,1:T(8,128)(2,1)}, u32[]{:S(2)}) copy-start(bf16[768,96]{0,1:T(8,128)(2,1)} %param.17) | copy-start | bytes 442372
  232.8 3.9 %copy-start.5 = (bf16[2,2,48,768]{3,2,1,0:T(8,128)(2,1)S(1)}, bf16[2,2,48,768]{3,2,1,0:T(8,128)(2,1)}, u32[]{:S(2)}) copy-start(bf16[2,2,48,768]{3,2,1,0:T(8,128)(2,1)} %get-tuple-element.74) | copy-start | bytes 884740
  232.8 5.4 %copy-start.3 = (bf16[2,2,96,768]{3,2,1,0:T(8,128)(2,1)S(1)}, bf16[2,2,96,768]{3,2,1,0:T(8,128)(2,1)}, u32[]{:S(2)}) copy-start(bf16[2,2,96,768]{3,2,1,0:T(8,128)(2,1)} %get-tuple-element.75) | copy-start | bytes 1769476
  238.4 1.4 copy-start.2
  239.9 1.3 copy-start.1
  239.9 2.2 copy-start

commit v5 on v4

--- a/solution.py
+++ b/solution.py
@@ -815,7 +815,7 @@
 
 VM = pl.BlockSpec(memory_space=pltpu.VMEM)
 ALLV = 67043328
-COLS = 256
+COLS = 768
 
 
 def call(body, ins, outs, scratch=(), name=None):
@@ -998,12 +998,12 @@
         begin()
         lax.fori_loop(0, J // 2, forward, 0)
         G.st2(EARLY)
-        lax.fori_loop(J // 2, J - J // 6, forward, 0)
+        lax.fori_loop(J // 2, J - max(1, J // 6), forward, 0)
         G.st2(EARLY + 1)
         for g in (EARLY, EARLY + 1):
             for k in range(1, nz): G._wz_local(wz, g, k).wait()
         G.st3(EARLY)
-        lax.fori_loop(J - J // 6, J, forward, 0)
+        lax.fori_loop(J - max(1, J // 6), J, forward, 0)
         G.st3(EARLY + 1)
         G.done(EARLY)
         G.done(EARLY + 1)

time: 244 us -> 242 us (level)
    pallas_call x1, Pallas kernels: 55.9 us -> 53.2 us  [ffn(): pl.pallas_call(partial(ffn_kernel, nz, D // vec.shape[0]), out_shape=[jax...]
where the time goes in v5:
time: 242 us; the launch traced here: 241 us
  Pallas kernels  223 us (92%)
  local copies, waits for them, and re-layouts  11 us (5%)
  other arithmetic  6.21 us (3%)
    pallas_call x1, Pallas kernels, tail(): pl.pallas_call(partial(tail_kernel, ns, loc, nz), out_shape=[jax.ShapeDty...  90.6 us
    pallas_call x1, Pallas kernels, head(): pl.pallas_call(partial(head_kernel, ns, loc, nz), out_shape=[jax.ShapeDty...  79.2 us
    pallas_call x1, Pallas kernels, ffn(): pl.pallas_call(partial(ffn_kernel, nz, D // vec.shape[0]), out_shape=[jax...  53.2 us

profile of v5, /device:TPU:0, one launch (start us, length us, event | category | flops | bytes accessed | tf_op | source)
XLA Modules:
  0.0 241.1 jit_solution(6249325970599558479)
XLA Ops:
  0.7 0.8 fusion.5
  1.5 1.3 fusion.10.refs_4_
  2.8 0.8 broadcast_in_dim.2.refs_7_.refs_3_
  3.7 2.1 copy.26
  5.8 0.9 copy.34
  6.7 0.0 copy-done.9
  6.7 0.9 pad_maximum_fusion
  7.5 79.2 %head.1 = (bf16[2,8,2,48,768]{4,3,2,1,0:T(8,128)(2,1)}, bf16[2,8,2,48,768]{4,3,2,1,0:T(8,128)(2,1)}, bf16[8,2,2,96,768]{4,3,2,1,0:T(8,128)(2,1)}, bf16[3,96,768]...) custom-call(bf16[2,2,48,768]{3,2,1,0:T(8,128)(2,1)} %get-tuple-eleme, ...), custom_call_target="tpu_custom_call" | custom-call | tf_op jit(solution)/shard_map/head/pallas_call | solution.py:937
  86.8 53.2 %ffn.1 = (f32[512,768]{1,0:T(8,128)}, bf16[512,768]{1,0:T(8,128)(2,1)}, f32[4,8,768]{2,1,0:T(8,128)}, bf16[512,768]{1,0:T(8,128)(2,1)}, bf16[3072,768]{1,0:T(8,1...) custom-call(f32[8,8,128]{2,1,0:T(8,128)} %get-tuple-element.45.refs_, ...), custom_call_target="tpu_custom_call" | custom-call | tf_op jit(solution)/shard_map/ffn/pallas_call | solution.py:1068
  140.0 90.6 %tail.1 = (f32[512,768]{1,0:T(8,128)}, bf16[2,2,48,768]{3,2,1,0:T(8,128)(2,1)}, bf16[2,2,48,768]{3,2,1,0:T(8,128)(2,1)}, bf16[2,2,96,768]{3,2,1,0:T(8,128)(2,1)}...) custom-call(bf16[512,768]{1,0:T(8,128)(2,1)} %get-tuple-element.51.refs_0_, ...), custom_call_target="tpu_custom_call" | custom-call | tf_op jit(solution)/shard_map/tail/pallas_call | solution.py:1183
  230.7 0.9 constant_dynamic-slice_fusion
  231.5 0.5 slice_bitcast_fusion
  232.1 1.0 fusion.14
  233.1 0.7 convert_bitcast_fusion.1
  233.8 0.7 convert_bitcast_fusion.4
  234.6 0.7 convert_bitcast_fusion.2
  235.3 0.7 convert_bitcast_fusion.3
  236.1 0.1 bitcast_convert_fusion
  236.2 1.4 copy.28
  237.6 0.1 convert_bitcast_fusion
  237.7 1.1 copy.31
  238.9 0.2 copy-done.1
  239.0 0.9 copy.37
  239.9 1.1 copy.38
  (21 shorter events, 0.1 us)
Async XLA Ops:
  0.6 5.1 %copy-start.4 = (bf16[3072,96]{0,1:T(8,128)(2,1)S(1)}, bf16[3072,96]{0,1:T(8,128)(2,1)}, u32[]{:S(2)}) copy-start(bf16[3072,96]{0,1:T(8,128)(2,1)} %param.22) | copy-start | bytes 1769476
  0.7 6.0 %copy-start.8 = (bf16[768,96]{0,1:T(8,128)(2,1)S(1)}, bf16[768,96]{0,1:T(8,128)(2,1)}, u32[]{:S(2)}) copy-start(bf16[768,96]{0,1:T(8,128)(2,1)} %param.20) | copy-start | bytes 442372
  0.7 6.0 %copy-start.6 = (bf16[768,96]{0,1:T(8,128)(2,1)S(1)}, bf16[768,96]{0,1:T(8,128)(2,1)}, u32[]{:S(2)}) copy-start(bf16[768,96]{0,1:T(8,128)(2,1)} %param.19) | copy-start | bytes 442372
  0.7 6.0 %copy-start.7 = (bf16[768,96]{0,1:T(8,128)(2,1)S(1)}, bf16[768,96]{0,1:T(8,128)(2,1)}, u32[]{:S(2)}) copy-start(bf16[768,96]{0,1:T(8,128)(2,1)} %param.18) | copy-start | bytes 442372
  0.7 6.0 %copy-start.9 = (bf16[768,96]{0,1:T(8,128)(2,1)S(1)}, bf16[768,96]{0,1:T(8,128)(2,1)}, u32[]{:S(2)}) copy-start(bf16[768,96]{0,1:T(8,128)(2,1)} %param.17) | copy-start | bytes 442372
  230.7 3.9 %copy-start.5 = (bf16[2,2,48,768]{3,2,1,0:T(8,128)(2,1)S(1)}, bf16[2,2,48,768]{3,2,1,0:T(8,128)(2,1)}, u32[]{:S(2)}) copy-start(bf16[2,2,48,768]{3,2,1,0:T(8,128)(2,1)} %get-tuple-element.74) | copy-start | bytes 884740
  230.7 5.4 %copy-start.3 = (bf16[2,2,96,768]{3,2,1,0:T(8,128)(2,1)S(1)}, bf16[2,2,96,768]{3,2,1,0:T(8,128)(2,1)}, u32[]{:S(2)}) copy-start(bf16[2,2,96,768]{3,2,1,0:T(8,128)(2,1)} %get-tuple-element.75) | copy-start | bytes 1769476
  236.2 1.4 copy-start.2
  237.7 1.3 copy-start.1
  237.7 2.2 copy-start
